TPU v7x, 128 devices: a whole 4x4x4 slice. The times are simulated.
128 devices in a mesh: cuts: 16 (over x_lo, z, core), slab: 8 (over y, x_hi).
Axes of the slice: x: 4 (x_hi: 2, x_lo: 2; x = x_hi * 2 + x_lo), y: 4, z: 4, core: 2. Of those that a mesh axis runs over, the one named last changes fastest.
Arguments:
- current_block: float32 [16, 64, 16, 512], P('cuts', 'slab'), may hold values from -6 to 6
- previous_block: float32 [16, 64, 16, 512], P('cuts', 'slab'), may hold values from -6 to 6
- previous_coupling: float32 [16, 16, 16], P('cuts'), may hold values from -3 to 3
- locked_vectors: bfloat16 [16, 64, 64, 512], P('cuts', None, 'slab'), may hold values from -6 to 6
- pivot_inverse: bfloat16 [2, 64, 512, 512], P(None, 'slab'), as said below
- hopping: float32 [64, 512], P('slab'), may hold values from 0.7 to 1.3
- partner: int32 [64, 512], P('slab'), may hold values from 0 to 511, each once within a row
- shift_index: int32 [16], P('cuts'), may hold values from 0 to 1
Outputs:
- next_block: float32 [16, 64, 16, 512], P('cuts', 'slab')
- coupling: float32 [16, 16, 16], P('cuts')
- ritz_values: float32 [16, 16], P('cuts')
Inputs may be any that keep to these rules, and one draw needn't show every extreme that they name: `pivot_inverse`: every pivot block is symmetric. `partner`: each row is a permutation of 0 to 511.
All inputs are finite; a program needn't handle non-finite values.
Results may differ from a plain program's by a relative error of at most 0.03.
Values may be sent and summed in bfloat16 or wider, within the bound.
No kernel may reach another device: no remote copies, remote signals or barrier semaphores. Data moves between devices by JAX's collectives and lax.ppermute only.
A program may use at most 64 MiB of HBM per device.

v0:
```python
import jax
import jax.numpy as jnp
import numpy as np
from jax import lax
from jax.sharding import PartitionSpec as P

JSWEEPS = 8


def shifted(value, axis, steps):
    count = lax.axis_size(axis)
    initial, last = (max(0, -steps), min(count, count - steps))
    return lax.ppermute(value, axis, [(source, source + steps) for source in range(initial, last)])


def padded(block, sides, width):
    for axis, dim in sides:
        count = lax.axis_size(axis)
        forward = [(i, i + 1) for i in range(count - 1)]
        backward = [(target, source) for source, target in forward]
        low = lax.ppermute(
            lax.slice_in_dim(block, block.shape[dim] - width, None, axis=dim), axis, forward
        )
        high = lax.ppermute(lax.slice_in_dim(block, 0, width, axis=dim), axis, backward)
        block = jnp.concatenate([low, block, high], axis=dim)
    return block


def round_robin(order_size):
    players = list(range(order_size))
    plan = []
    for round_index in range(order_size - 1):
        plan.append(
            [
                (
                    min(players[place_index], players[order_size - 1 - place_index]),
                    max(players[place_index], players[order_size - 1 - place_index]),
                )
                for place_index in range(order_size // 2)
            ]
        )
        players = [players[0], players[-1]] + players[1:-1]
    return np.array(plan, dtype=np.int32)


def jacobi_values(matrix):
    order_size = matrix.shape[-1]
    plan = round_robin(order_size)
    identity = jnp.eye(order_size, dtype=matrix.dtype)
    highest = lax.Precision.HIGHEST

    def one_sweep(sweep_index, current):
        for round_index in range(order_size - 1):
            first_rows = plan[round_index, :, 0]
            second_rows = plan[round_index, :, 1]
            onehot_first = identity[first_rows]
            onehot_second = identity[second_rows]
            first_first = current[:, first_rows, first_rows]
            second_second = current[:, second_rows, second_rows]
            first_second = current[:, first_rows, second_rows]
            rotation_angle = 0.5 * jnp.arctan2(2.0 * first_second, second_second - first_first)
            cosine_less = jnp.cos(rotation_angle) - 1.0
            sine_value = jnp.sin(rotation_angle)
            rotation = identity[None] + jnp.einsum(
                "hi,sh,hj->sij", onehot_first, cosine_less, onehot_first, precision=highest
            )
            rotation = rotation + jnp.einsum(
                "hi,sh,hj->sij", onehot_second, cosine_less, onehot_second, precision=highest
            )
            rotation = rotation + jnp.einsum(
                "hi,sh,hj->sij", onehot_first, sine_value, onehot_second, precision=highest
            )
            rotation = rotation - jnp.einsum(
                "hi,sh,hj->sij", onehot_second, sine_value, onehot_first, precision=highest
            )
            current = jnp.einsum("sji,sjk,skl->sil", rotation, current, rotation, precision=highest)
        return current

    settled = lax.fori_loop(0, JSWEEPS, one_sweep, matrix)
    return jnp.sort(jnp.diagonal(settled, axis1=-2, axis2=-1), axis=-1)


def cholesky_upper(gram_matrix):
    order_size = gram_matrix.shape[-1]
    positions = jnp.arange(order_size, dtype=jnp.int32)
    columns = []
    for column_index in range(order_size):
        column = gram_matrix[:, :, column_index]
        for done_index in range(column_index):
            column = (
                column
                - columns[done_index] * columns[done_index][:, column_index : column_index + 1]
            )
        pivot_root = jnp.sqrt(column[:, column_index : column_index + 1])
        columns.append(
            jnp.where(
                (positions >= column_index)[None, :], column / pivot_root, jnp.zeros_like(column)
            )
        )
    lower_factor = jnp.stack(columns, axis=2)
    return jnp.swapaxes(lower_factor, 1, 2)


def upper_inverse(upper_factor):
    order_size = upper_factor.shape[-1]
    identity = jnp.eye(order_size, dtype=upper_factor.dtype)
    rows = [None] * order_size
    for row_index in range(order_size - 1, -1, -1):
        row_value = identity[row_index][None, :]
        for later_index in range(row_index + 1, order_size):
            row_value = (
                row_value
                - upper_factor[:, row_index, later_index : later_index + 1] * rows[later_index]
            )
        rows[row_index] = row_value / upper_factor[:, row_index, row_index : row_index + 1]
    return jnp.stack(rows, axis=1)


def bond_matrix(part_row):
    orbitals = part_row.shape[0]
    places = lax.broadcasted_iota(jnp.int32, (orbitals, orbitals), 0)
    return (places == part_row[None, :]).astype(jnp.float32)


def apply_pivots(reduced, pivot_inverse, front_shift, slab_index):
    count, rows, orbitals = reduced.shape
    flat = reduced.reshape(count * rows, orbitals).astype(jnp.bfloat16)
    pivot_block = lax.dynamic_slice(
        pivot_inverse, (front_shift[0], slab_index, 0, 0), (1, 1, orbitals, orbitals)
    )[0, 0]
    return jnp.dot(flat, pivot_block, preferred_element_type=jnp.float32).reshape(1, rows, orbitals)


def relay_down(slab_major, pivot_inverse, shift_index, hopping, partner, fronts):
    devices = lax.axis_size("slab")
    position = lax.axis_index("slab")
    highest = lax.Precision.HIGHEST
    slab_count, slice_count, block_width, orbitals = slab_major.shape
    front_slices = slice_count // fronts

    def sweep(front_block, front_shift, inflow):

        def advance(carry_value, inputs):
            source, hop_row, part_row, slab_index = inputs
            bonds = bond_matrix(part_row)
            pulled = jnp.einsum("sbj,ji->sbi", carry_value, bonds, precision=highest)
            reduced = source - hop_row * pulled
            result = apply_pivots(reduced, pivot_inverse, front_shift, slab_index)
            return (result, result)

        return lax.scan(
            advance,
            inflow,
            (front_block, hopping, partner, jnp.arange(slab_count, dtype=jnp.int32)),
        )

    def section(section_index, relay_state):
        outgoing, collected = relay_state
        incoming = shifted(outgoing, "slab", 1)
        front_index = section_index - position
        active = (front_index >= 0) & (front_index < fronts)
        last_value, values = sweep(slab_major, shift_index, incoming)
        return (last_value, jnp.where(active, values, collected))

    start_state = (
        jnp.zeros((front_slices, block_width, orbitals), jnp.float32),
        jnp.zeros((slab_count, slice_count, block_width, orbitals), jnp.float32),
    )
    return lax.fori_loop(0, devices + fronts - 1, section, start_state)[1]


def relay_up(lower_values, pivot_inverse, shift_index, hopping, partner, fronts):
    devices = lax.axis_size("slab")
    position = lax.axis_index("slab")
    highest = lax.Precision.HIGHEST
    slab_count, slice_count, block_width, orbitals = lower_values.shape
    front_slices = slice_count // fronts

    def sweep(front_block, front_shift, inflow):

        def retreat(carry_value, inputs):
            lower_slab, hop_row, part_row, slab_index = inputs
            result = lower_slab - apply_pivots(carry_value, pivot_inverse, front_shift, slab_index)
            bonds = bond_matrix(part_row)
            carried = jnp.einsum("sbi,ji->sbj", hop_row * result, bonds, precision=highest)
            return (carried, result)

        return lax.scan(
            retreat,
            inflow,
            (front_block, hopping, partner, jnp.arange(slab_count, dtype=jnp.int32)),
            reverse=True,
        )

    def section(section_index, relay_state):
        outgoing, collected = relay_state
        incoming = shifted(outgoing.astype(jnp.bfloat16), "slab", -1).astype(outgoing.dtype)
        front_index = section_index - (devices - 1 - position)
        active = (front_index >= 0) & (front_index < fronts)
        first_value, values = sweep(lower_values, shift_index, incoming)
        return (first_value, jnp.where(active, values, collected))

    start_state = (
        jnp.zeros((front_slices, block_width, orbitals), jnp.float32),
        jnp.zeros(lower_values.shape, jnp.float32),
    )
    return lax.fori_loop(0, devices + fronts - 1, section, start_state)[1]


def per_device(
    current_block,
    previous_block,
    previous_coupling,
    locked_vectors,
    pivot_inverse,
    hopping,
    partner,
    shift_index,
):
    highest = lax.Precision.HIGHEST
    slice_count, slab_count, block_width, orbitals = current_block.shape
    norm_scale = 1.0 / (slab_count * lax.axis_size("slab") * orbitals)
    extended = padded(locked_vectors, (("cuts", 0),), 1)
    neighbours = jnp.concatenate([extended[:slice_count], extended[2:]], axis=1)
    fronts = 1
    slab_major = jnp.swapaxes(current_block, 0, 1)
    lower_values = relay_down(slab_major, pivot_inverse, shift_index, hopping, partner, fronts)
    solved = relay_up(lower_values, pivot_inverse, shift_index, hopping, partner, fronts)
    local_projection = jnp.einsum("skaw,ksbw->sab", current_block, solved, precision=highest)
    projection = lax.psum(local_projection, "slab") * norm_scale
    first = solved - jnp.einsum(
        "skaw,sba->ksbw", previous_block, previous_coupling, precision=highest
    )
    first = first - jnp.einsum("skaw,sab->ksbw", current_block, projection, precision=highest)
    local_coefficients = jnp.einsum("slkw,ksbw->slb", neighbours, first, precision=highest)
    coefficients = lax.psum(local_coefficients, "slab") * norm_scale
    second = first - jnp.einsum("slkw,slb->ksbw", neighbours, coefficients, precision=highest)
    local_gram = jnp.einsum("ksaw,ksbw->sab", second, second, precision=highest)
    gram_matrix = lax.psum(local_gram, "slab") * norm_scale
    upper_factor = cholesky_upper(gram_matrix)
    inverse_factor = upper_inverse(upper_factor)
    next_block = jnp.einsum("ksbw,sba->skaw", second, inverse_factor, precision=highest)
    ritz_values = jacobi_values(0.5 * (projection + jnp.swapaxes(projection, 1, 2)))
    return (next_block, upper_factor, ritz_values)


def solution(mesh):
    return jax.shard_map(
        per_device,
        mesh=mesh,
        in_specs=(
            P("cuts", "slab", None, None),
            P("cuts", "slab", None, None),
            P("cuts", None, None),
            P("cuts", None, "slab", None),
            P(None, "slab", None, None),
            P("slab", None),
            P("slab", None),
            P("cuts"),
        ),
        out_specs=(P("cuts", "slab", None, None), P("cuts", None, None), P("cuts", None)),
        check_vma=False,
    )
```

profile of v0, /device:TPU:2, one launch (start us, length us, event | category | flops | bytes accessed | tf_op | source)
XLA Modules:
  0.0 1952.4 jit_solution(1302416316221036428)
XLA Ops:
  9.9 454.3 %while.135 = (s32[]{:T(128)}, f32[1,16,512]{2,1,0:T(8,128)S(1)}, f32[8,1,16,512]{3,2,1,0:T(8,128)S(1)}, f32[8,1,16,512]{3,2,1,0:T(8,128)}, f32[8,512]{1,0:T(8,12...) while((s32[]{:T(128)}, f32[1,16,512]{2,1,0:T(8,128)S(1)}, ...), condition=%wide.region_3.4_spmd.clone, body=%wide.region_0.3_spmd.clone.sunk | while | flops 59138048 | bytes 1946676 | solution.py:169
  15.8 49.0 %while.138 = (s32[]{:T(128)}, f32[1,16,512]{2,1,0:T(8,128)S(1)}, f32[8,1,16,512]{3,2,1,0:T(8,128)S(1)}, f32[8,1,16,512]{3,2,1,0:T(8,128)}, f32[8,512]{1,0:T(8,12...) while((s32[]{:T(128)}, f32[1,16,512]{2,1,0:T(8,128)S(1)}, ...), condition=%wide.region_2.2_spmd, body=%wide.region_1.1_spmd.sunk | while | flops 59006976 | bytes 701119 | solution.py:151
  72.3 49.0 %while.138 = (s32[]{:T(128)}, f32[1,16,512]{2,1,0:T(8,128)S(1)}, f32[8,1,16,512]{3,2,1,0:T(8,128)S(1)}, f32[8,1,16,512]{3,2,1,0:T(8,128)}, f32[8,512]{1,0:T(8,12...) while((s32[]{:T(128)}, f32[1,16,512]{2,1,0:T(8,128)S(1)}, ...), condition=%wide.region_2.2_spmd, body=%wide.region_1.1_spmd.sunk | while | flops 59006976 | bytes 701119 | solution.py:151
  128.8 49.0 %while.138 = (s32[]{:T(128)}, f32[1,16,512]{2,1,0:T(8,128)S(1)}, f32[8,1,16,512]{3,2,1,0:T(8,128)S(1)}, f32[8,1,16,512]{3,2,1,0:T(8,128)}, f32[8,512]{1,0:T(8,12...) while((s32[]{:T(128)}, f32[1,16,512]{2,1,0:T(8,128)S(1)}, ...), condition=%wide.region_2.2_spmd, body=%wide.region_1.1_spmd.sunk | while | flops 59006976 | bytes 701119 | solution.py:151
  185.4 49.0 %while.138 = (s32[]{:T(128)}, f32[1,16,512]{2,1,0:T(8,128)S(1)}, f32[8,1,16,512]{3,2,1,0:T(8,128)S(1)}, f32[8,1,16,512]{3,2,1,0:T(8,128)}, f32[8,512]{1,0:T(8,12...) while((s32[]{:T(128)}, f32[1,16,512]{2,1,0:T(8,128)S(1)}, ...), condition=%wide.region_2.2_spmd, body=%wide.region_1.1_spmd.sunk | while | flops 59006976 | bytes 701119 | solution.py:151
  242.8 49.0 %while.138 = (s32[]{:T(128)}, f32[1,16,512]{2,1,0:T(8,128)S(1)}, f32[8,1,16,512]{3,2,1,0:T(8,128)S(1)}, f32[8,1,16,512]{3,2,1,0:T(8,128)}, f32[8,512]{1,0:T(8,12...) while((s32[]{:T(128)}, f32[1,16,512]{2,1,0:T(8,128)S(1)}, ...), condition=%wide.region_2.2_spmd, body=%wide.region_1.1_spmd.sunk | while | flops 59006976 | bytes 701119 | solution.py:151
  300.2 49.0 %while.138 = (s32[]{:T(128)}, f32[1,16,512]{2,1,0:T(8,128)S(1)}, f32[8,1,16,512]{3,2,1,0:T(8,128)S(1)}, f32[8,1,16,512]{3,2,1,0:T(8,128)}, f32[8,512]{1,0:T(8,12...) while((s32[]{:T(128)}, f32[1,16,512]{2,1,0:T(8,128)S(1)}, ...), condition=%wide.region_2.2_spmd, body=%wide.region_1.1_spmd.sunk | while | flops 59006976 | bytes 701119 | solution.py:151
  357.6 49.0 %while.138 = (s32[]{:T(128)}, f32[1,16,512]{2,1,0:T(8,128)S(1)}, f32[8,1,16,512]{3,2,1,0:T(8,128)S(1)}, f32[8,1,16,512]{3,2,1,0:T(8,128)}, f32[8,512]{1,0:T(8,12...) while((s32[]{:T(128)}, f32[1,16,512]{2,1,0:T(8,128)S(1)}, ...), condition=%wide.region_2.2_spmd, body=%wide.region_1.1_spmd.sunk | while | flops 59006976 | bytes 701119 | solution.py:151
  415.0 49.0 %while.138 = (s32[]{:T(128)}, f32[1,16,512]{2,1,0:T(8,128)S(1)}, f32[8,1,16,512]{3,2,1,0:T(8,128)S(1)}, f32[8,1,16,512]{3,2,1,0:T(8,128)}, f32[8,512]{1,0:T(8,12...) while((s32[]{:T(128)}, f32[1,16,512]{2,1,0:T(8,128)S(1)}, ...), condition=%wide.region_2.2_spmd, body=%wide.region_1.1_spmd.sunk | while | flops 59006976 | bytes 701119 | solution.py:151
  464.7 416.2 %while.137 = (s32[]{:T(128)}, bf16[1,16,512]{2,1,0:T(8,128)(2,1)S(1)}, f32[8,1,16,512]{3,2,1,0:T(8,128)S(1)}, f32[8,512]{1,0:T(8,128)}, f32[8,1,16,512]{3,2,1,0:...) while((s32[]{:T(128)}, ...), condition=%wide.region_7.8_spmd.clone, body=%wide.region_4.7_spmd.clone.sunk | while | flops 59129860 | bytes 1848396 | solution.py:207
  473.2 43.7 %while.139 = (s32[]{:T(128)}, bf16[1,16,512]{2,1,0:T(8,128)(2,1)S(1)}, f32[8,1,16,512]{3,2,1,0:T(8,128)S(1)}, f32[8,512]{1,0:T(8,128)}, f32[8,1,16,512]{3,2,1,0:...) while((s32[]{:T(128)}, ...), condition=%wide.region_6.6_spmd, body=%wide.region_5.5_spmd.sunk | while | flops 58998788 | bytes 701127 | solution.py:188
  525.5 43.7 %while.139 = (s32[]{:T(128)}, bf16[1,16,512]{2,1,0:T(8,128)(2,1)S(1)}, f32[8,1,16,512]{3,2,1,0:T(8,128)S(1)}, f32[8,512]{1,0:T(8,128)}, f32[8,1,16,512]{3,2,1,0:...) while((s32[]{:T(128)}, ...), condition=%wide.region_6.6_spmd, body=%wide.region_5.5_spmd.sunk | while | flops 58998788 | bytes 701127 | solution.py:188
  577.4 43.7 %while.139 = (s32[]{:T(128)}, bf16[1,16,512]{2,1,0:T(8,128)(2,1)S(1)}, f32[8,1,16,512]{3,2,1,0:T(8,128)S(1)}, f32[8,512]{1,0:T(8,128)}, f32[8,1,16,512]{3,2,1,0:...) while((s32[]{:T(128)}, ...), condition=%wide.region_6.6_spmd, body=%wide.region_5.5_spmd.sunk | while | flops 58998788 | bytes 701127 | solution.py:188
  629.3 43.7 %while.139 = (s32[]{:T(128)}, bf16[1,16,512]{2,1,0:T(8,128)(2,1)S(1)}, f32[8,1,16,512]{3,2,1,0:T(8,128)S(1)}, f32[8,512]{1,0:T(8,128)}, f32[8,1,16,512]{3,2,1,0:...) while((s32[]{:T(128)}, ...), condition=%wide.region_6.6_spmd, body=%wide.region_5.5_spmd.sunk | while | flops 58998788 | bytes 701127 | solution.py:188
  681.2 43.7 %while.139 = (s32[]{:T(128)}, bf16[1,16,512]{2,1,0:T(8,128)(2,1)S(1)}, f32[8,1,16,512]{3,2,1,0:T(8,128)S(1)}, f32[8,512]{1,0:T(8,128)}, f32[8,1,16,512]{3,2,1,0:...) while((s32[]{:T(128)}, ...), condition=%wide.region_6.6_spmd, body=%wide.region_5.5_spmd.sunk | while | flops 58998788 | bytes 701127 | solution.py:188
  733.2 43.7 %while.139 = (s32[]{:T(128)}, bf16[1,16,512]{2,1,0:T(8,128)(2,1)S(1)}, f32[8,1,16,512]{3,2,1,0:T(8,128)S(1)}, f32[8,512]{1,0:T(8,128)}, f32[8,1,16,512]{3,2,1,0:...) while((s32[]{:T(128)}, ...), condition=%wide.region_6.6_spmd, body=%wide.region_5.5_spmd.sunk | while | flops 58998788 | bytes 701127 | solution.py:188
  785.1 43.7 %while.139 = (s32[]{:T(128)}, bf16[1,16,512]{2,1,0:T(8,128)(2,1)S(1)}, f32[8,1,16,512]{3,2,1,0:T(8,128)S(1)}, f32[8,512]{1,0:T(8,128)}, f32[8,1,16,512]{3,2,1,0:...) while((s32[]{:T(128)}, ...), condition=%wide.region_6.6_spmd, body=%wide.region_5.5_spmd.sunk | while | flops 58998788 | bytes 701127 | solution.py:188
  837.0 43.7 %while.139 = (s32[]{:T(128)}, bf16[1,16,512]{2,1,0:T(8,128)(2,1)S(1)}, f32[8,1,16,512]{3,2,1,0:T(8,128)S(1)}, f32[8,512]{1,0:T(8,128)}, f32[8,1,16,512]{3,2,1,0:...) while((s32[]{:T(128)}, ...), condition=%wide.region_6.6_spmd, body=%wide.region_5.5_spmd.sunk | while | flops 58998788 | bytes 701127 | solution.py:188
  881.3 23.9 %psum.21 = f32[1,16,16]{1,2,0:T(8,128)S(1)} all-reduce(f32[1,16,16]{1,2,0:T(8,128)S(1)} %convolution_bitcast_fusion.9), channel_id=1, replica_groups=mesh['cuts'=16,'slab'=8] {'slab'}, use_global_device_ids=true, to_apply=%region_8.9 | all-reduce | flops 256 | bytes 2048 | tf_op jit(solution)/shard_map/psum | solution.py:230
  905.9 725.5 %while.133 = (s32[]{:T(128)}, f32[1,16,16]{2,1,0:T(8,128)S(1)}, s32[]{:T(128)}, s32[8]{0:T(128)}, s32[8]{0:T(128)}, /*index=5*/s32[8]{0:T(128)}, s32[8]{0:T(128)...) while((s32[]{:T(128)}, f32[1,16,16]{2,1,0:T(8,128)S(1)}, ...), condition=%wide.region_12.13_spmd.clone.clone.clone, body=%wide.region_11.12_spmd.sunk.clone.clone.clone.sunk | while | flops 3011610 | bytes 414101 | solution.py:79
  1635.8 19.7 %psum.22 = f32[1,128,16]{1,2,0:T(8,128)S(1)} all-reduce(f32[1,128,16]{1,2,0:T(8,128)S(1)} %convolution_bitcast_fusion.7), channel_id=1, replica_groups=mesh['cuts'=16,'slab'=8] {'slab'}, use_global_device_ids=true, to_apply=%region_9.10 | all-reduce | flops 2048 | bytes 16384 | tf_op jit(solution)/shard_map/psum | solution.py:236
  1656.5 22.9 %psum.23 = f32[1,16,16]{1,2,0:T(8,128)S(1)} all-reduce(f32[1,16,16]{1,2,0:T(8,128)S(1)} %convolution_bitcast_fusion.8), channel_id=1, replica_groups=mesh['cuts'=16,'slab'=8] {'slab'}, use_global_device_ids=true, to_apply=%region_10.11 | all-reduce | flops 256 | bytes 2048 | tf_op jit(solution)/shard_map/psum | solution.py:239
  1784.0 75.1 %compare_select_fusion.1 = (f32[1,16,1]{1,2,0:T(1,128)S(1)}, f32[1,16,1]{1,2,0:T(1,128)S(1)}, f32[1,16,1]{1,2,0:T(1,128)S(1)}, f32[1,16,1]{1,2,0:T(1,128)S(1)}, ...) fusion(f32[1,16,16]{1,2,0:T(8,128)S(1)} %broadcast_multiply_fus, ...), kind=kLoop, calls=%fused_computation.386 | loop fusion | flops 4576 | bytes 2592 | tf_op jit(solution)/shard_map/jit(_where)/select_n | solution.py:96
  1865.0 84.9 %divide_bitcast_fusion = (f32[1,1,16]{2,1,0:T(1,128)S(1)}, f32[1,16]{1,0:T(1,128)S(1)}, f32[1,16]{1,0:T(1,128)S(1)}, f32[1,16]{1,0:T(1,128)S(1)}, f32[1,16]{1,0:...) fusion(f32[16,16]{1,0:T(8,128)S(1)} %fusion.160, ...), kind=kLoop, calls=%fused_computation.513 | loop fusion | flops 4096 | bytes 2592 | tf_op jit(solution)/shard_map/stack | solution.py:116
  (2773 shorter events, 1495.7 us)
Async XLA Ops:
  0.6 1633.2 %copy-start = (f32[1,8,16,512]{3,2,1,0:T(8,128)S(1)}, f32[1,8,16,512]{3,2,1,0:T(8,128)}, u32[]{:S(2)}) copy-start(f32[1,8,16,512]{3,2,1,0:T(8,128)} %param.169) | copy-start | bytes 786436
  1.9 1633.0 %collective-permute-start.3 = (bf16[1,64,8,512]{3,1,2,0:T(8,128)(2,1)S(1)}, bf16[1,64,8,512]{3,1,2,0:T(8,128)(2,1)S(1)}, u32[]{:S(2)}, u32[]{:S(2)}) collective-permute-start(bf16[1,64,8,512]{3,1,2,0:T(8,128)(2,1)S(1)} %copy.184), channel_id=1, source_target_pairs={{8,0},{16,8},{24,16},{32,24},{40,32},{48,40},{56,48},{64,56},{72,6... | collective-permute-start | bytes 1572872 | tf_op jit(solution)/shard_map/ppermute | solution.py:24
  7.3 1627.7 %collective-permute-start.2 = (bf16[1,64,8,512]{3,1,2,0:T(8,128)(2,1)S(1)}, bf16[1,64,8,512]{3,1,2,0:T(8,128)(2,1)S(1)}, u32[]{:S(2)}, u32[]{:S(2)}) collective-permute-start(bf16[1,64,8,512]{3,1,2,0:T(8,128)(2,1)S(1)} %copy.184), channel_id=1, source_target_pairs={{0,8},{8,16},{16,24},{24,32},{32,40},{40,48},{48,56},{56,64},{64,7... | collective-permute-start | bytes 1572872 | tf_op jit(solution)/shard_map/ppermute | solution.py:21
  9.9 5.9 collective-permute-start.1
  65.0 7.3 collective-permute-start.1
  121.5 7.3 collective-permute-start.1
  178.0 7.4 collective-permute-start.1
  234.6 8.2 collective-permute-start.1
  292.0 8.2 collective-permute-start.1
  349.4 8.2 collective-permute-start.1
  406.8 8.2 collective-permute-start.1
  464.2 441.3 %copy-start.2 = (s32[8]{0:T(128)S(1)}, s32[8]{0:T(128)}, u32[]{:S(2)}) copy-start(s32[8]{0:T(128)} %constant.2557) | copy-start | bytes 100
  464.2 441.3 %copy-start.3 = (s32[8]{0:T(128)S(1)}, s32[8]{0:T(128)}, u32[]{:S(2)}) copy-start(s32[8]{0:T(128)} %constant.2556) | copy-start | bytes 100
  464.2 441.3 %copy-start.4 = (s32[8]{0:T(128)S(1)}, s32[8]{0:T(128)}, u32[]{:S(2)}) copy-start(s32[8]{0:T(128)} %constant.2555) | copy-start | bytes 100
  464.2 441.2 %copy-start.5 = (s32[8]{0:T(128)S(1)}, s32[8]{0:T(128)}, u32[]{:S(2)}) copy-start(s32[8]{0:T(128)} %constant.2552) | copy-start | bytes 100
  464.2 441.2 %copy-start.6 = (s32[8]{0:T(128)S(1)}, s32[8]{0:T(128)}, u32[]{:S(2)}) copy-start(s32[8]{0:T(128)} %constant.2551) | copy-start | bytes 100
  464.7 8.5 collective-permute-start
  517.1 8.3 collective-permute-start
  569.3 8.0 collective-permute-start
  621.2 8.0 collective-permute-start
  673.2 8.0 collective-permute-start
  725.1 8.0 collective-permute-start
  777.0 8.0 collective-permute-start
  829.0 8.0 collective-permute-start
  (39 other events, 16834.0 us)
where the time goes:
time: 1990 us; the launch traced here: 1950 us
  local copies, waits for them, and re-layouts  658 us (33%)
  matrix products  454 us (23%)
  other arithmetic  411 us (21%)
  loops' own time  218 us (11%)
  waiting for transfers between devices  66.9 us (3%)
  blocking collectives  66.5 us (3%)
  starting transfers between devices  65.9 us (3%)
    dynamic_slice x384, local copies, waits for them, and re-layouts, sweep(): lax.scan(advance, inflow, (front_block, hopping, partner, jnp.arange(slab...  261 us
    dot_general x128, matrix products, apply_pivots(): jnp.dot(flat, pivot_block, preferred_element_type=jnp.float32)  156 us
    another operation x8, loops' own time, sweep(): lax.scan(advance, inflow, (front_block, hopping, partner, jnp.arange(slab...  108 us
    another operation x8, loops' own time, sweep(): lax.scan(retreat, inflow, (front_block, hopping, partner, jnp.arange(slab...  106 us
    another operation x1, other arithmetic, upper_inverse(): return jnp.stack(rows, axis=1)  84.9 us
    gather x120, other arithmetic, one_sweep(): onehot_second = identity[second_rows]  79.2 us
    gather x120, local copies, waits for them, and re-layouts, one_sweep(): second_second = current[:, second_rows, second_rows]  78.5 us
    gather x120, local copies, waits for them, and re-layouts, one_sweep(): first_second = current[:, first_rows, second_rows]  78.4 us
  transfers between devices with their start and end apart: 18, of which 16 were waited for; matrix products, arithmetic and copies ran while one was open for 64% of the time, Pallas kernels for 0%

commit v1 on v0

v1 whole, which is shorter than its diff:
```python
import functools

import jax
import jax.numpy as jnp
from jax import lax
from jax.experimental import pallas as pl
from jax.experimental.pallas import tpu as pltpu
from jax.sharding import PartitionSpec as P

F32 = jnp.float32
BF16 = jnp.bfloat16
VMEM_LIMIT = 32 * 1024 * 1024
SMALL_LIMIT = 16 * 1024 * 1024
SECTIONS = 5


def mm(left, right):
    return jnp.dot(left, right, preferred_element_type=F32)


def mm_t(left, right):
    return lax.dot_general(left, right, (((1,), (1,)), ((), ())), preferred_element_type=F32)


def exact(left, right):
    return jnp.dot(left, right, precision=lax.Precision.HIGHEST, preferred_element_type=F32)


def exact_t(left, right):
    return lax.dot_general(
        left, right, (((1,), (1,)), ((), ())),
        precision=lax.Precision.HIGHEST, preferred_element_type=F32,
    )


def halves(value):
    high = value.astype(BF16)
    return high, (value - high.astype(F32)).astype(BF16)


def forward_kernel(
    shift_ref, hop_ref, part_ref, cur_ref, piv_ref,
    fg_ref, source_ref, own_ref, w_ref, pp_ref, op_ref,
    pbuf, in_sem,
):
    slabs, width = hop_ref.shape
    shift = shift_ref[0]

    def fetch(k):
        return pltpu.make_async_copy(piv_ref.at[shift, k], pbuf.at[k], in_sem.at[k])

    for k in range(slabs):
        fetch(k).start()
    down = lax.broadcasted_iota(jnp.int32, (width, width), 0)
    across = lax.broadcasted_iota(jnp.int32, (width, width), 1)
    part_columns = jnp.transpose(part_ref[...].astype(F32)).astype(jnp.int32)
    hop_columns = jnp.transpose(hop_ref[...])
    response = None
    vectors = None
    for k in range(slabs):
        gather = jnp.where(down == part_ref[k : k + 1, :], 1.0, 0.0).astype(BF16)
        weight = jnp.sum(
            jnp.where(across == part_columns[:, k : k + 1], hop_columns[:, k : k + 1], 0.0),
            axis=0, keepdims=True,
        )
        w_ref[k : k + 1, :] = weight
        fetch(k).wait()
        pivot = pbuf[k]
        permuted = mm(gather, pivot).astype(BF16)
        pp_ref[k] = permuted
        source = mm(cur_ref[k].astype(BF16), pivot)
        source_ref[k] = source
        if k == 0:
            unit = jnp.where(down == across, weight, 0.0).astype(BF16)
            response = -mm(unit, permuted)
            vectors = source
        else:
            response = -mm((response * weight).astype(BF16), permuted)
            vectors = source - mm((vectors * weight).astype(BF16), permuted)
        own_ref[k] = vectors
        op_ref[k] = response.astype(BF16)
    fg_ref[:width, :] = response.astype(BF16)
    fg_ref[width:, :] = vectors.astype(BF16)


def forward_range(shift_index, hopping, partner, current, pivot_inverse):
    slabs, rows, width = current.shape
    vm = pl.BlockSpec(memory_space=pltpu.VMEM)
    hbm = pl.BlockSpec(memory_space=pltpu.HBM)
    stack = jax.ShapeDtypeStruct((slabs, width, width), BF16)
    vectors = jax.ShapeDtypeStruct((slabs, rows, width), F32)
    return pl.pallas_call(
        forward_kernel,
        out_shape=(
            jax.ShapeDtypeStruct((width + rows, width), BF16),
            vectors,
            vectors,
            jax.ShapeDtypeStruct((slabs, width), F32),
            stack,
            stack,
        ),
        in_specs=[pl.BlockSpec(memory_space=pltpu.SMEM), vm, vm, vm, hbm],
        out_specs=(vm,) * 6,
        scratch_shapes=[
            pltpu.VMEM((slabs, width, width), BF16),
            pltpu.SemaphoreType.DMA((slabs,)),
        ],
        compiler_params=pltpu.CompilerParams(vmem_limit_bytes=VMEM_LIMIT),
        cost_estimate=pl.CostEstimate(
            flops=4 * slabs * width**3, bytes_accessed=6 * slabs * width**2, transcendentals=0
        ),
        name="forward_range",
    )(shift_index, hopping, partner, current, pivot_inverse)


def backward_kernel(
    shift_ref, hop_ref, part_ref, own_ref, op_ref, piv_ref,
    sh_ref, q_ref,
    pbuf, in_sem,
):
    slabs, width = hop_ref.shape
    shift = shift_ref[0]

    def fetch(k):
        return pltpu.make_async_copy(piv_ref.at[shift, k], pbuf.at[k], in_sem.at[k])

    last = slabs - 1
    for k in range(last, -1, -1):
        fetch(k).start()
    across = lax.broadcasted_iota(jnp.int32, (width, width), 1)
    part_columns = jnp.transpose(part_ref[...].astype(F32)).astype(jnp.int32)

    def scatter(k):
        return jnp.where(across == part_columns[:, k : k + 1], 1.0, 0.0).astype(BF16)

    fetch(last).wait()
    q_ref[last] = pbuf[last]
    response = op_ref[last].astype(F32)
    vectors = own_ref[last]
    for k in range(slabs - 2, -1, -1):
        fetch(k).wait()
        permuted = mm(scatter(k + 1), pbuf[k]).astype(BF16)
        q_ref[k] = permuted
        hop = hop_ref[k + 1 : k + 2, :]
        response = op_ref[k].astype(F32) - mm((response * hop).astype(BF16), permuted)
        vectors = own_ref[k] - mm((vectors * hop).astype(BF16), permuted)
    hop = hop_ref[0:1, :]
    spread = scatter(0)
    sh_ref[:width, :] = mm((response * hop).astype(BF16), spread).astype(BF16)
    sh_ref[width:, :] = mm((vectors * hop).astype(BF16), spread).astype(BF16)


def backward_range(shift_index, hopping, partner, own, op, pivot_inverse):
    slabs, rows, width = own.shape
    vm = pl.BlockSpec(memory_space=pltpu.VMEM)
    hbm = pl.BlockSpec(memory_space=pltpu.HBM)
    stack = jax.ShapeDtypeStruct((slabs, width, width), BF16)
    return pl.pallas_call(
        backward_kernel,
        out_shape=(jax.ShapeDtypeStruct((width + rows, width), BF16), stack),
        in_specs=[pl.BlockSpec(memory_space=pltpu.SMEM), vm, vm, vm, vm, hbm],
        out_specs=(vm, vm),
        scratch_shapes=[
            pltpu.VMEM((slabs, width, width), BF16),
            pltpu.SemaphoreType.DMA((slabs,)),
        ],
        compiler_params=pltpu.CompilerParams(vmem_limit_bytes=VMEM_LIMIT),
        cost_estimate=pl.CostEstimate(
            flops=4 * slabs * width**3, bytes_accessed=6 * slabs * width**2, transcendentals=0
        ),
        name="backward_range",
    )(shift_index, hopping, partner, own, op, pivot_inverse)


def lower_kernel(inflow_ref, source_ref, w_ref, pp_ref, low_ref):
    slabs = source_ref.shape[0]
    value = inflow_ref[...].astype(F32)
    for k in range(slabs):
        value = source_ref[k] - mm((value * w_ref[k : k + 1, :]).astype(BF16), pp_ref[k])
        low_ref[k] = value


def lower_sweep(inflow, source, weights, pp):
    slabs, rows, width = source.shape
    vm = pl.BlockSpec(memory_space=pltpu.VMEM)
    return pl.pallas_call(
        lower_kernel,
        out_shape=jax.ShapeDtypeStruct((slabs, rows, width), F32),
        in_specs=[vm] * 4,
        out_specs=vm,
        compiler_params=pltpu.CompilerParams(vmem_limit_bytes=SMALL_LIMIT),
        cost_estimate=pl.CostEstimate(
            flops=2 * slabs * rows * width**2, bytes_accessed=2 * slabs * width**2, transcendentals=0
        ),
        name="lower_sweep",
    )(inflow, source, weights, pp)


def known_kernel(cur_ref, prev_ref, below_ref, above_ref, out_ref):
    slabs, rows, width = cur_ref.shape
    near = 2 * below_ref.shape[1]
    two = 2 * rows
    total = None
    for k in range(slabs):
        cur_high, cur_low = halves(cur_ref[k])
        prev_high, prev_low = halves(prev_ref[k])
        stack = jnp.concatenate(
            [below_ref[k], above_ref[k], cur_high, prev_high, cur_low, prev_low], axis=0
        )
        part = mm_t(stack, stack)
        total = part if total is None else total + part
    first = total[near : near + two]
    second = total[near + two :]
    among = first[:, near : near + two] + first[:, near + two :]
    among = among + second[:, near : near + two] + second[:, near + two :]
    out_ref[:near, :] = total[:near, :near]
    out_ref[near : near + two, :] = first[:, :near] + second[:, :near]
    out_ref[near + two : near + two + rows, :] = jnp.zeros((rows, near), F32)
    out_ref[near + two + rows :, :] = jnp.concatenate(
        [jnp.zeros((rows, near - 2 * two), F32), among[:rows], among[rows:]], axis=1
    )


def known_products(current, previous, below, above):
    slabs, rows, width = current.shape
    near = 2 * below.shape[1]
    return pl.pallas_call(
        known_kernel,
        out_shape=jax.ShapeDtypeStruct((near + 4 * rows, near), F32),
        compiler_params=pltpu.CompilerParams(vmem_limit_bytes=SMALL_LIMIT),
        cost_estimate=pl.CostEstimate(
            flops=2 * slabs * 192 * 192 * width, bytes_accessed=3 * 2**19, transcendentals=0
        ),
        name="known_products",
    )(current, previous, below, above)


def upper_kernel(
    carried_ref, low_ref, hop_ref, cur_ref, prev_ref, below_ref, above_ref, known_ref, q_ref,
    x_ref, out_ref,
):
    slabs, rows, width = low_ref.shape
    near = 2 * below_ref.shape[1]
    push = carried_ref[...]
    total = None
    for k in range(slabs - 1, -1, -1):
        value = low_ref[k] - mm(push, q_ref[k])
        x_ref[k] = value
        push = (value * hop_ref[k : k + 1, :]).astype(BF16)
        high, low = halves(value)
        pair = jnp.concatenate([high, low], axis=0)
        cur_high, cur_low = halves(cur_ref[k])
        prev_high, prev_low = halves(prev_ref[k])
        stack = jnp.concatenate(
            [below_ref[k], above_ref[k], high, cur_high, prev_high, low, cur_low, prev_low], axis=0
        )
        part = mm_t(pair, stack)
        total = part if total is None else total + part
    joined = total[:rows] + total[rows:]
    three = 3 * rows
    own = joined[:, near : near + three] + joined[:, near + three :]
    top = near + 2 * rows
    out_ref[:top, :] = known_ref[:top, :]
    out_ref[top : top + rows, :] = joined[:, :near]
    out_ref[top + rows :, :] = known_ref[top + rows :, :] + jnp.concatenate(
        [own, jnp.zeros((rows, near - three), F32)], axis=1
    )


def upper_sweep(carried, low, hopping, current, previous, below, above, known, q):
    slabs, rows, width = low.shape
    vm = pl.BlockSpec(memory_space=pltpu.VMEM)
    return pl.pallas_call(
        upper_kernel,
        out_shape=(
            jax.ShapeDtypeStruct((slabs, rows, width), F32),
            jax.ShapeDtypeStruct(known.shape, F32),
        ),
        in_specs=[vm] * 9,
        out_specs=(vm, vm),
        compiler_params=pltpu.CompilerParams(vmem_limit_bytes=SMALL_LIMIT),
        cost_estimate=pl.CostEstimate(
            flops=2 * slabs * rows * width**2, bytes_accessed=2 * slabs * width**2, transcendentals=0
        ),
        name="upper_sweep",
    )(carried, low, hopping, current, previous, below, above, known, q)


def factor(gram):
    size = gram.shape[0]
    down = lax.broadcasted_iota(jnp.int32, (size, size), 0)
    across = lax.broadcasted_iota(jnp.int32, (size, size), 1)
    left = gram
    right = jnp.where(down == across, 1.0, 0.0)
    column = lax.broadcasted_iota(jnp.int32, (size, 1), 0)
    pivots = jnp.zeros((size, 1), F32)
    for j in range(size):
        pivot = left[j : j + 1, j : j + 1]
        pivots = jnp.where(column == j, pivot, pivots)
        if j < size - 1:
            scale = jnp.where(column > j, left[:, j : j + 1] / pivot, 0.0)
            left_row = left[j : j + 1, :]
            right_row = right[j : j + 1, :]
            left = left - scale * left_row
            right = right - scale * right_row
    inverse_root = 1.0 / jnp.sqrt(pivots)
    upper = jnp.where(across >= down, left * inverse_root, 0.0)
    return upper, right * inverse_root


def tridiagonal(matrix):
    size = matrix.shape[0]
    row = lax.broadcasted_iota(jnp.int32, (1, size), 1)
    down = lax.broadcasted_iota(jnp.int32, (size, size), 0)
    across = lax.broadcasted_iota(jnp.int32, (size, size), 1)
    diagonal = []
    squares = []

    def upright(value):
        return jnp.sum(jnp.where(down == across, value, 0.0), axis=1, keepdims=True)

    for j in range(size - 2):
        diagonal.append(matrix[j : j + 1, j : j + 1])
        beside = jnp.where(row > j, matrix[j : j + 1, :], 0.0)
        square = jnp.sum(beside * beside, axis=1, keepdims=True)
        squares.append(square)
        length = jnp.sqrt(square)
        lead = matrix[j : j + 1, j + 1 : j + 2]
        signed = jnp.where(lead >= 0.0, length, -length)
        half = square + length * jnp.abs(lead)
        scale = jnp.where(half > 0.0, 1.0 / jnp.where(half > 0.0, half, 1.0), 0.0)
        v_row = beside + jnp.where(row == j + 1, signed, 0.0)
        v_col = upright(v_row)
        p_row = scale * jnp.sum(matrix * v_col, axis=0, keepdims=True)
        along = 0.5 * scale * jnp.sum(p_row * v_row, axis=1, keepdims=True)
        w_row = p_row - along * v_row
        w_col = upright(w_row)
        matrix = matrix - (v_col * w_row + w_col * v_row)
    a = size - 2
    diagonal.append(matrix[a : a + 1, a : a + 1])
    diagonal.append(matrix[a + 1 : a + 2, a + 1 : a + 2])
    squares.append(matrix[a : a + 1, a + 1 : a + 2] * matrix[a : a + 1, a + 1 : a + 2])
    return diagonal, squares


def eigenvalues(matrix):
    size = matrix.shape[0]
    diagonal, squares = tridiagonal(matrix)
    bound = jnp.max(jnp.sum(jnp.abs(matrix), axis=1, keepdims=True), axis=0, keepdims=True)
    bound = bound * (1.0 + 2.0**-18)
    shape = (8, 128)
    wide_diagonal = [jnp.broadcast_to(value, shape) for value in diagonal]
    wide_squares = [jnp.broadcast_to(value, shape) for value in squares]
    lane = lax.broadcasted_iota(jnp.int32, shape, 1)
    level = lax.broadcasted_iota(jnp.int32, shape, 0)
    second_half = lane >= 64
    rank = 2 * level + jnp.where(second_half, 1, 0)
    point = (lane - jnp.where(second_half, 64, 0) + 1).astype(F32)
    start = jnp.broadcast_to(-bound, shape)
    step = jnp.broadcast_to(bound * (2.0 / 65.0), shape)
    tiny = 1e-30
    for _ in range(SECTIONS):
        shifted = start + point * step
        pivot = wide_diagonal[0] - shifted
        pivot = jnp.where(jnp.abs(pivot) < tiny, -tiny, pivot)
        count = jnp.where(pivot < 0.0, 1, 0)
        for i in range(1, size):
            pivot = wide_diagonal[i] - shifted - wide_squares[i - 1] / pivot
            pivot = jnp.where(jnp.abs(pivot) < tiny, -tiny, pivot)
            count = count + jnp.where(pivot < 0.0, 1, 0)
        passed = jnp.where(count <= rank, 1.0, 0.0)
        all_passed = jnp.sum(passed, axis=1, keepdims=True)
        late_passed = jnp.sum(jnp.where(second_half, passed, 0.0), axis=1, keepdims=True)
        cut = jnp.where(second_half, late_passed, all_passed - late_passed)
        start = start + cut * step
        step = step * (1.0 / 65.0)
    middle = start + 32.5 * step
    even = jnp.broadcast_to(middle[:, 0:1], shape)
    odd = jnp.broadcast_to(middle[:, 127:128], shape)
    place = jnp.where(lane == 2 * level, even, jnp.where(lane == 2 * level + 1, odd, 0.0))
    return jnp.sum(place, axis=0, keepdims=True)[:, :size]


def finish_kernel(
    scale, products_ref, coupling_ref, x_ref, cur_ref, prev_ref, below_ref, above_ref,
    next_ref, upper_ref, ritz_ref,
):
    slabs, rows, width = x_ref.shape
    near = products_ref.shape[1]
    two = 2 * rows
    products = products_ref[...] * scale
    near_near = products[:near]
    known_near = products[near : near + two]
    x_near = products[near + two : near + two + rows]
    tail = products[near + two + rows :]
    x_x = tail[:, :rows]
    x_known = tail[:, rows : 3 * rows]
    among = jnp.concatenate([tail[:, near - 2 * two : near - two], tail[:, near - two :]], axis=0)
    projection_t = tail[:, rows:two]
    fixed = jnp.concatenate([-projection_t, -coupling_ref[...]], axis=1)
    coefficients_t = x_near + exact(fixed, known_near)
    with_known = x_known + exact(fixed, among) - exact_t(coefficients_t, known_near)
    with_near = coefficients_t - exact(coefficients_t, near_near)
    gram = x_x + exact_t(fixed, x_known) - exact_t(coefficients_t, x_near)
    gram = gram + exact_t(with_known, fixed) - exact_t(with_near, coefficients_t)
    upper, inverse_t = factor(gram)
    upper_ref[...] = upper
    ritz_ref[...] = eigenvalues(0.5 * (projection_t + jnp.transpose(projection_t)))
    down = lax.broadcasted_iota(jnp.int32, (rows, rows), 0)
    across = lax.broadcasted_iota(jnp.int32, (rows, rows), 1)
    unit = jnp.where(down == across, 1.0, 0.0)
    weights = exact(inverse_t, jnp.concatenate([unit, fixed, -coefficients_t], axis=1))
    weight_high, weight_low = halves(weights)
    both = jnp.concatenate([weight_high, weight_low], axis=0)
    for k in range(slabs):
        x_high, x_low = halves(x_ref[k])
        cur_high, cur_low = halves(cur_ref[k])
        prev_high, prev_low = halves(prev_ref[k])
        stack = jnp.concatenate(
            [x_high, cur_high, prev_high, below_ref[k], above_ref[k]], axis=0
        )
        rest = jnp.concatenate([x_low, cur_low, prev_low], axis=0)
        main = mm(both, stack)
        next_ref[k] = main[:rows] + main[rows:] + mm(weight_high[:, : 3 * rows], rest)


def finish(scale, products, coupling, x, current, previous, below, above):
    slabs, rows, width = x.shape
    return pl.pallas_call(
        functools.partial(finish_kernel, scale),
        out_shape=(
            jax.ShapeDtypeStruct((slabs, rows, width), F32),
            jax.ShapeDtypeStruct((rows, rows), F32),
            jax.ShapeDtypeStruct((1, rows), F32),
        ),
        compiler_params=pltpu.CompilerParams(vmem_limit_bytes=SMALL_LIMIT),
        name="finish",
    )(products, coupling, x, current, previous, below, above)


def per_device(
    current_block,
    previous_block,
    previous_coupling,
    locked_vectors,
    pivot_inverse,
    hopping,
    partner,
    shift_index,
):
    devices = lax.axis_size("slab")
    slices = lax.axis_size("cuts")
    odd = lax.axis_index("slab") % 2 == 1
    current = current_block[0]
    previous = previous_block[0]
    slabs, rows, width = current.shape
    scale = 1.0 / (slabs * devices * width)
    swap = [(i, i ^ 1) for i in range(devices)]

    def both(value):
        other = lax.ppermute(value, "slab", swap)
        return jnp.where(odd, other, value), jnp.where(odd, value, other)

    fg, source, own, weights, pp, op = forward_range(
        shift_index, hopping, partner, current, pivot_inverse
    )
    fg_first, fg_second = both(fg)
    sh, q = backward_range(shift_index, hopping, partner, own, op, pivot_inverse)
    sh_first, sh_second = both(sh)
    f_first, g_first = fg_first[:width], fg_first[width:].astype(F32)
    f_second, g_second = fg_second[:width], fg_second[width:].astype(F32)
    s_first, h_first = sh_first[:width], sh_first[width:].astype(F32)
    s_second, h_second = sh_second[:width], sh_second[width:].astype(F32)

    locked = jnp.swapaxes(locked_vectors[0], 0, 1)
    even_pairs = [(i, i ^ 1) for i in range(slices)]
    odd_pairs = [(i, i + 1) for i in range(1, slices - 1, 2)]
    odd_pairs = odd_pairs + [(j, i) for i, j in odd_pairs]
    below = lax.ppermute(locked, "cuts", even_pairs)
    above = lax.ppermute(locked, "cuts", odd_pairs)

    into_first = jnp.zeros((rows, width), BF16)
    for r in range(0, devices - 2, 2):
        into_second = (g_first + mm(into_first, f_first)).astype(BF16)
        sent = (g_second + mm(into_second, f_second)).astype(BF16)
        into_first = into_first + lax.ppermute(sent, "slab", [(r, r + 2), (r + 1, r + 3)])
    into_second = (g_first + mm(into_first, f_first)).astype(BF16)
    back_second = h_second + mm(into_second, s_second)
    back_first = h_first + mm(into_first, s_first)
    low = lower_sweep(jnp.where(odd, into_second, into_first), source, weights, pp)
    known = known_products(current, previous, below, above)
    to_second = jnp.zeros((rows, width), BF16)
    for r in range(devices - 2, 0, -2):
        to_first = (back_second + mm_t(to_second, f_second)).astype(BF16)
        sent = (back_first + mm_t(to_first, f_first)).astype(BF16)
        to_second = to_second + lax.ppermute(sent, "slab", [(r, r - 2), (r + 1, r - 1)])
    to_first = (back_second + mm_t(to_second, f_second)).astype(BF16)
    carried = jnp.where(odd, to_second, to_first)
    x, products = upper_sweep(
        carried, low, hopping, current, previous, below, above, known, q
    )
    step = 1
    while step < devices:
        products = products + lax.ppermute(products, "slab", [(i, i ^ step) for i in range(devices)])
        step *= 2
    next_block, upper, ritz = finish(
        scale, products, previous_coupling[0], x, current, previous, below, above
    )
    return next_block[None], upper[None], ritz


def solution(mesh):
    return jax.shard_map(
        per_device,
        mesh=mesh,
        in_specs=(
            P("cuts", "slab", None, None),
            P("cuts", "slab", None, None),
            P("cuts", None, None),
            P("cuts", None, "slab", None),
            P(None, "slab", None, None),
            P("slab", None),
            P("slab", None),
            P("cuts"),
        ),
        out_specs=(P("cuts", "slab", None, None), P("cuts", None, None), P("cuts", None)),
        check_vma=False,
    )
```

time: 1990 us -> 113 us (0.06); the launches traced: 1950 us -> 112 us
  local copies, waits for them, and re-layouts: 658 us -> 18.6 us
  matrix products: 454 us -> 7.08 us
  other arithmetic: 411 us -> 3.01 us
  loops' own time: 218 us -> 0 us
  blocking collectives: 66.5 us -> 0 us
  starting transfers between devices: 65.9 us -> 22.9 us
  waiting for transfers between devices: 66.9 us -> 24.8 us
  Pallas kernels: 0 us -> 33.9 us
    dot_general x983 -> x10, matrix products: 454 us -> 7.08 us  [the longest x4 5.58 us: mm_t(): lax.dot_general(left, right, (((1,), (1,)), ((), ())), preferred_element_...]
    gather x602 -> x0, local copies, waits for them, and re-layouts: 368 us -> none  [the longest x120 78.5 us: one_sweep(): second_second = current[:, second_rows, second_rows]]
    dynamic_slice x384 -> x0, local copies, waits for them, and re-layouts: 261 us -> none  [sweep(): lax.scan(advance, inflow, (front_block, hopping, partner, jnp.arange(slab...]
    another operation x19 -> x0, loops' own time: 218 us -> none  [the longest x8 108 us: sweep(): lax.scan(advance, inflow, (front_block, hopping, partner, jnp.arange(slab...]
    gather x240 -> x0, other arithmetic: 153 us -> none  [the longest x120 79.2 us: one_sweep(): onehot_second = identity[second_rows]]
    another operation x1 -> x0, other arithmetic: 84.9 us -> none  [upper_inverse(): return jnp.stack(rows, axis=1)]
    sub x135 -> x0, other arithmetic: 80 us -> none  [the longest x15 75 us: cholesky_upper(): column - columns[done_index] * columns[done_index][:, column_index:column...]
    select_n x31 -> x2, other arithmetic: 76.7 us -> 2.24 us  [both(): return (jnp.where(odd, other, value), jnp.where(odd, value, other))]
  transfers between devices with their start and end apart: 18 -> 13, of which waited for: 16 -> 8; matrix products, arithmetic and copies ran while one was open for 64% -> 8% of each run, Pallas kernels for 0% -> 8%
where the time goes in v1:
time: 113 us; the launch traced here: 112 us
  Pallas kernels  33.9 us (30%)
  waiting for transfers between devices  24.8 us (22%)
  starting transfers between devices  22.9 us (20%)
  local copies, waits for them, and re-layouts  18.6 us (16%)
  matrix products  7.08 us (6%)
  other arithmetic  3.01 us (3%)
  between operations  1.49 us (1%)
    unnamed x35, local copies, waits for them, and re-layouts  18.6 us
    pallas_call x1, Pallas kernels, finish(): pl.pallas_call(functools.partial(finish_kernel, scale), out_shape=(jax.Sh...  14 us
    ppermute x3, waiting for transfers between devices, per_device(): lax.ppermute(products, 'slab', [(i, i ^ step) for i in range(devices)])  13.4 us
    pallas_call x1, Pallas kernels, forward_range(): pl.pallas_call(forward_kernel, out_shape=(jax.ShapeDtypeStruct((width + r...  9 us
    pallas_call x1, Pallas kernels, backward_range(): pl.pallas_call(backward_kernel, out_shape=(jax.ShapeDtypeStruct((width +...  7.18 us
    ppermute x1, starting transfers between devices, per_device(): above = lax.ppermute(locked, 'cuts', odd_pairs)  6.91 us
    dot_general x4, matrix products, mm_t(): lax.dot_general(left, right, (((1,), (1,)), ((), ())), preferred_element_...  5.58 us
    ppermute x2, waiting for transfers between devices, both(): other = lax.ppermute(value, 'slab', swap)  5.42 us
  transfers between devices with their start and end apart: 13, of which 8 were waited for; matrix products, arithmetic and copies ran while one was open for 8% of the time, Pallas kernels for 8%

profile of v1, /device:TPU:2, one launch (start us, length us, event | category | flops | bytes accessed | tf_op | source)
XLA Modules:
  0.0 111.8 jit_solution(15335271359240608240)
XLA Ops:
  3.0 3.4 %copy-done.10 = bf16[2,8,512,512]{3,2,1,0:T(8,128)(2,1)S(1)} copy-done((bf16[2,8,512,512]{3,2,1,0:T(8,128)(2,1)S(1)}, bf16[2,8,512,512]{3,2,1,0:T(8,128)(2,1)}, u32[]{:S(2)}) %copy-start.10) | copy-done | bytes 8388632
  7.1 9.0 %forward_range.1 = (bf16[528,512]{1,0:T(8,128)(2,1)S(1)}, f32[8,16,512]{2,1,0:T(8,128)S(1)}, f32[8,16,512]{2,1,0:T(8,128)S(1)}, f32[8,512]{1,0:T(8,128)S(1)}, bf...) custom-call(s32[1]{0:T(128)S(6)} %copy.14.shift_ref, f32[8,512]{1,0:T(8,128)S(1)} %copy-done.7, ...), custom_call_target="tpu_custom_call" | custom-call | flops 4294967296 | bytes 12582912 | tf_op jit(solution)/shard_map/forward_range/pallas_call | solution.py:92
  16.1 2.0 %copy-done.2 = bf16[8,512,512]{2,1,0:T(8,128)(2,1)} copy-done((bf16[8,512,512]{2,1,0:T(8,128)(2,1)}, bf16[8,512,512]{2,1,0:T(8,128)(2,1)S(1)}, u32[]{:S(2)}) %copy-start.2) | copy-done | bytes 4194328
  18.0 2.0 %copy-done.13 = bf16[8,512,512]{2,1,0:T(8,128)(2,1)} copy-done((bf16[8,512,512]{2,1,0:T(8,128)(2,1)}, bf16[8,512,512]{2,1,0:T(8,128)(2,1)S(1)}, u32[]{:S(2)}) %copy-start.13) | copy-done | bytes 4194328
  20.1 2.1 %collective-permute-start.1 = (bf16[528,512]{1,0:T(8,128)(2,1)S(1)}, bf16[528,512]{1,0:T(8,128)(2,1)}, u32[]{:S(2)}, u32[]{:S(2)}) collective-permute-start(bf16[528,512]{1,0:T(8,128)(2,1)S(1)} %get-tuple-element.19), channel_id=1, source_target_pairs={{0,1},{1,0},{2,3},{3,2},{4,5},{5,4},{6,7},{7,6},{8,9},{9,8},{10,11... | collective-permute-start | bytes 1622024 | tf_op jit(solution)/shard_map/ppermute | solution.py:461
  22.2 2.2 %copy-done.14 = bf16[8,512,512]{2,1,0:T(8,128)(2,1)S(1)} copy-done((bf16[8,512,512]{2,1,0:T(8,128)(2,1)S(1)}, bf16[8,512,512]{2,1,0:T(8,128)(2,1)}, u32[]{:S(2)}) %copy-start.14) | copy-done | bytes 4194328
  24.4 7.2 %backward_range.1 = (bf16[528,512]{1,0:T(8,128)(2,1)S(1)}, bf16[8,512,512]{2,1,0:T(8,128)(2,1)S(1)}) custom-call(s32[1]{0:T(128)S(6)} %copy.14.shift_ref, f32[8,512]{1,0:T(8,128)S(1)} %copy-done.7, s32[8,512]{1,0:T(8,128)S(1)} %copy-done.12, f32[8,16,512]{2,1,0:T(8,128)S(1)} %get-tuple-element.16.own_ref, bf16[8,512,512]{2,1,0:T(8,128)(2,1)S(1)} %copy-done.14, ...), custom_call_target="tpu_custom_call" | custom-call | flops 4294967296 | bytes 12582912 | tf_op jit(solution)/shard_map/backward_range/pallas_call | solution.py:158
  31.6 2.0 %copy-done = bf16[8,512,512]{2,1,0:T(8,128)(2,1)} copy-done((bf16[8,512,512]{2,1,0:T(8,128)(2,1)}, bf16[8,512,512]{2,1,0:T(8,128)(2,1)S(1)}, u32[]{:S(2)}) %copy-start) | copy-done | bytes 4194328
  37.1 3.5 %collective-permute-start.2 = (bf16[16,512]{1,0:T(8,128)(2,1)S(1)}, bf16[16,512]{1,0:T(8,128)(2,1)S(1)}, u32[]{:S(2)}, u32[]{:S(2)}) collective-permute-start(bf16[16,512]{1,0:T(8,128)(2,1)S(1)} %fusion.1), channel_id=1, source_target_pairs={{0,2},{1,3},{8,10},{9,11},{16,18},{17,19},{24,26},{25,27},{32,34},... | collective-permute-start | bytes 49160 | tf_op jit(solution)/shard_map/ppermute | solution.py:486
  44.2 4.7 %collective-permute-done = bf16[528,512]{1,0:T(8,128)(2,1)} collective-permute-done((bf16[528,512]{1,0:T(8,128)(2,1)S(1)}, bf16[528,512]{1,0:T(8,128)(2,1)}, u32[]{:S(2)}, u32[]{:S(2)}) %collective-permute-start) | collective-permute-done | bytes 540704 | tf_op jit(solution)/shard_map/ppermute | solution.py:461
  51.1 1.8 %fusion.8 = bf16[16,512]{1,0:T(8,128)(2,1)} fusion(bf16[528,512]{1,0:T(8,128)(2,1)S(1)} %get-tuple-element.32, bf16[528,512]{1,0:T(8,128)(2,1)S(1)} %get-tuple-element.31, f32[16,512]{1,0:T(8,128)S(1)} %fusion.17, bf16[528,512]{1,0:T(8,128)(2,1)} %copy-done.15, f32[16,512]{1,0:T(8,128)S(1)} %fusion.15, bf16[528,512]{1,0:T(8,128)(2,1)S(1)} %get-tuple-element.29), kind=kOutput, calls=%fused_computation.22 | convolution fusion | flops 16842752 | bytes 1163264 | tf_op jit(solution)/shard_map/dot_general | solution.py:22
  54.1 2.0 %copy.13 = bf16[1,64,8,512]{3,1,2,0:T(8,128)(2,1)} copy(bf16[1,64,8,512]{3,2,1,0:T(8,128)(2,1)} %param.11) | data formatting | bytes 1048576 | tf_op args[3]
  56.1 6.9 %collective-permute-start.9 = (bf16[8,64,512]{2,1,0:T(8,128)(2,1)}, bf16[8,64,512]{2,1,0:T(8,128)(2,1)S(1)}, u32[]{:S(2)}, u32[]{:S(2)}) collective-permute-start(bf16[8,64,512]{2,1,0:T(8,128)(2,1)} %bitcast.14), channel_id=1, source_target_pairs={{8,16},{24,32},{40,48},{56,64},{72,80},{88,96},{104,112},{16,8},{3... | collective-permute-start | bytes 1572872 | tf_op jit(solution)/shard_map/ppermute | solution.py:480
  63.0 1.8 %fusion.10 = bf16[16,512]{1,0:T(8,128)(2,1)} fusion(bf16[16,512]{1,0:T(8,128)(2,1)} %collective-permute-done.5, bf16[528,512]{1,0:T(8,128)(2,1)S(1)} %get-tuple-element.32, bf16[528,512]{1,0:T(8,128)(2,1)S(1)} %get-tuple-element.31, f32[16,512]{1,0:T(8,128)S(1)} %fusion.17, bf16[528,512]{1,0:T(8,128)(2,1)} %copy-done.15, f32[16,512]{1,0:T(8,128)S(1)} %fusion.15, ...), kind=kOutput, calls=%fused_computation.24 | convolution fusion | flops 16842752 | bytes 1179648 | tf_op jit(solution)/shard_map/dot_general | solution.py:22
  66.3 1.8 %fusion.12 = bf16[16,512]{1,0:T(8,128)(2,1)} fusion(bf16[16,512]{1,0:T(8,128)(2,1)S(1)} %add.89, bf16[528,512]{1,0:T(8,128)(2,1)S(1)} %get-tuple-element.32, bf16[528,512]{1,0:T(8,128)(2,1)S(1)} %get-tuple-element.31, f32[16,512]{1,0:T(8,128)} %copy-done.16, bf16[528,512]{1,0:T(8,128)(2,1)} %copy-done.15, f32[16,512]{1,0:T(8,128)S(1)} %fusion.15, ...), kind=kOutput, calls=%fused_computation.26 | convolution fusion | flops 16842752 | bytes 1179648 | tf_op jit(solution)/shard_map/dot_general | solution.py:22
  68.1 1.5 %collective-permute-start.7 = (bf16[16,512]{1,0:T(8,128)(2,1)}, bf16[16,512]{1,0:T(8,128)(2,1)S(1)}, u32[]{:S(2)}, u32[]{:S(2)}) collective-permute-start(bf16[16,512]{1,0:T(8,128)(2,1)} %fusion.12), channel_id=1, source_target_pairs={{2,0},{3,1},{10,8},{11,9},{18,16},{19,17},{26,24},{27,25},{34,32},... | collective-permute-start | bytes 49160 | tf_op jit(solution)/shard_map/ppermute | solution.py:496
  70.8 2.2 %copy-done.3 = bf16[8,512,512]{2,1,0:T(8,128)(2,1)S(1)} copy-done((bf16[8,512,512]{2,1,0:T(8,128)(2,1)S(1)}, bf16[8,512,512]{2,1,0:T(8,128)(2,1)}, u32[]{:S(2)}) %copy-start.3) | copy-done | bytes 4194328
  74.2 4.1 %collective-permute-done.7 = bf16[16,512]{1,0:T(8,128)(2,1)S(1)} collective-permute-done((bf16[16,512]{1,0:T(8,128)(2,1)}, bf16[16,512]{1,0:T(8,128)(2,1)S(1)}, u32[]{:S(2)}, u32[]{:S(2)}) %collective-permute-start.7) | collective-permute-done | bytes 16416 | tf_op jit(solution)/shard_map/ppermute | solution.py:496
  78.6 1.8 %upper_sweep.1 = (f32[8,16,512]{2,1,0:T(8,128)S(1)}, f32[192,128]{1,0:T(8,128)S(1)}) custom-call(bf16[16,512]{1,0:T(8,128)(2,1)S(1)} %fusion.14.carried_ref, f32[8,16,512]{2,1,0:T(8,128)S(1)} %lower_sweep.1.low_ref, f32[8,512]{1,0:T(8,128)S(1)} %copy-done.8, f32[8,16,512]{2,1,0:T(8,128)S(1)} %bitcast.17, f32[8,16,512]{2,1,0:T(8,128)S(1)} %bitcast.20, ...), custom_call_target="tpu_custom_call" | custom-call | flops 67108864 | bytes 4194304 | tf_op jit(solution)/shard_map/upper_sweep/pallas_call | solution.py:273
  80.3 6.1 %collective-permute-done.10 = f32[192,128]{1,0:T(8,128)S(1)} collective-permute-done((f32[192,128]{1,0:T(8,128)S(1)}, f32[192,128]{1,0:T(8,128)S(1)}, u32[]{:S(2)}, u32[]{:S(2)}) %collective-permute-start.10) | collective-permute-done | bytes 98336 | tf_op jit(solution)/shard_map/ppermute | solution.py:504
  86.5 2.4 %collective-permute-start.11 = (f32[192,128]{1,0:T(8,128)S(1)}, f32[192,128]{1,0:T(8,128)S(1)}, u32[]{:S(2)}, u32[]{:S(2)}) collective-permute-start(f32[192,128]{1,0:T(8,128)S(1)} %add.94), channel_id=1, source_target_pairs={{0,2},{1,3},{2,0},{3,1},{4,6},{5,7},{6,4},{7,5},{8,10},{9,11},{10,... | collective-permute-start | bytes 294920 | tf_op jit(solution)/shard_map/ppermute | solution.py:504
  88.9 2.6 %collective-permute-done.11 = f32[192,128]{1,0:T(8,128)S(1)} collective-permute-done((f32[192,128]{1,0:T(8,128)S(1)}, f32[192,128]{1,0:T(8,128)S(1)}, u32[]{:S(2)}, u32[]{:S(2)}) %collective-permute-start.11) | collective-permute-done | bytes 98336 | tf_op jit(solution)/shard_map/ppermute | solution.py:504
  93.0 4.7 %collective-permute-done.12 = f32[192,128]{1,0:T(8,128)S(1)} collective-permute-done((f32[192,128]{1,0:T(8,128)S(1)}, f32[192,128]{1,0:T(8,128)S(1)}, u32[]{:S(2)}, u32[]{:S(2)}) %collective-permute-start.12) | collective-permute-done | bytes 98336 | tf_op jit(solution)/shard_map/ppermute | solution.py:504
  97.7 14.0 %finish.1 = (f32[8,16,512]{2,1,0:T(8,128)}, f32[16,16]{1,0:T(8,128)}, f32[1,16]{1,0:T(1,128)}) custom-call(f32[192,128]{1,0:T(8,128)S(1)} %add.96.products_ref, f32[16,16]{1,0:T(8,128)S(1)} %bitcast.22, f32[8,16,512]{2,1,0:T(8,128)S(1)} %get-tuple-element.25.x_ref, f32[8,16,512]{2,1,0:T(8,128)S(1)} %bitcast.18, f32[8,16,512]{2,1,0:T(8,128)S(1)} %bitcast.21, ...), custom_call_target="tpu_custom_call" | custom-call | tf_op jit(solution)/shard_map/finish/pallas_call | solution.py:429
  (60 shorter events, 18.5 us)
Async XLA Ops:
  2.9 3.4 %copy-start.10 = (bf16[2,8,512,512]{3,2,1,0:T(8,128)(2,1)S(1)}, bf16[2,8,512,512]{3,2,1,0:T(8,128)(2,1)}, u32[]{:S(2)}) copy-start(bf16[2,8,512,512]{3,2,1,0:T(8,128)(2,1)} %piv_ref.3) | copy-start | bytes 25165828
  7.0 15.1 %copy-start.11 = (bf16[2,8,512,512]{3,2,1,0:T(8,128)(2,1)S(1)}, bf16[2,8,512,512]{3,2,1,0:T(8,128)(2,1)}, u32[]{:S(2)}) copy-start(bf16[2,8,512,512]{3,2,1,0:T(8,128)(2,1)} %piv_ref.3) | copy-start | bytes 25165828
  20.1 15.6 %collective-permute-start.1 = (bf16[528,512]{1,0:T(8,128)(2,1)S(1)}, bf16[528,512]{1,0:T(8,128)(2,1)}, u32[]{:S(2)}, u32[]{:S(2)}) collective-permute-start(bf16[528,512]{1,0:T(8,128)(2,1)S(1)} %get-tuple-element.19), channel_id=1, source_target_pairs={{0,1},{1,0},{2,3},{3,2},{4,5},{5,4},{6,7},{7,6},{8,9},{9,8},{10,11... | collective-permute-start | bytes 1622024 | tf_op jit(solution)/shard_map/ppermute | solution.py:461
  22.2 2.2 %copy-start.14 = (bf16[8,512,512]{2,1,0:T(8,128)(2,1)S(1)}, bf16[8,512,512]{2,1,0:T(8,128)(2,1)}, u32[]{:S(2)}) copy-start(bf16[8,512,512]{2,1,0:T(8,128)(2,1)} %copy-done.13) | copy-start | bytes 12582916
  31.6 2.0 %copy-start = (bf16[8,512,512]{2,1,0:T(8,128)(2,1)}, bf16[8,512,512]{2,1,0:T(8,128)(2,1)S(1)}, u32[]{:S(2)}) copy-start(bf16[8,512,512]{2,1,0:T(8,128)(2,1)S(1)} %get-tuple-element.23.q_ref) | copy-start | bytes 12582916
  33.6 15.3 %collective-permute-start = (bf16[528,512]{1,0:T(8,128)(2,1)S(1)}, bf16[528,512]{1,0:T(8,128)(2,1)}, u32[]{:S(2)}, u32[]{:S(2)}) collective-permute-start(bf16[528,512]{1,0:T(8,128)(2,1)S(1)} %get-tuple-element.18), channel_id=1, source_target_pairs={{0,1},{1,0},{2,3},{3,2},{4,5},{5,4},{6,7},{7,6},{8,9},{9,8},{10,11... | collective-permute-start | bytes 1622024 | tf_op jit(solution)/shard_map/ppermute | solution.py:461
  37.1 4.9 %collective-permute-start.2 = (bf16[16,512]{1,0:T(8,128)(2,1)S(1)}, bf16[16,512]{1,0:T(8,128)(2,1)S(1)}, u32[]{:S(2)}, u32[]{:S(2)}) collective-permute-start(bf16[16,512]{1,0:T(8,128)(2,1)S(1)} %fusion.1), channel_id=1, source_target_pairs={{0,2},{1,3},{8,10},{9,11},{16,18},{17,19},{24,26},{25,27},{32,34},... | collective-permute-start | bytes 49160 | tf_op jit(solution)/shard_map/ppermute | solution.py:486
  42.4 0.7 collective-permute-start.3
  43.4 26.7 %copy-start.5 = (f32[1,8,16,512]{3,2,1,0:T(8,128)S(1)}, f32[1,8,16,512]{3,2,1,0:T(8,128)}, u32[]{:S(2)}) copy-start(f32[1,8,16,512]{3,2,1,0:T(8,128)} %param.8) | copy-start | bytes 786436
  43.4 26.7 %copy-start.6 = (f32[1,8,16,512]{3,2,1,0:T(8,128)S(1)}, f32[1,8,16,512]{3,2,1,0:T(8,128)}, u32[]{:S(2)}) copy-start(f32[1,8,16,512]{3,2,1,0:T(8,128)} %param.9) | copy-start | bytes 786436
  43.4 6.7 %collective-permute-start.4 = (bf16[16,512]{1,0:T(8,128)(2,1)S(1)}, bf16[16,512]{1,0:T(8,128)(2,1)S(1)}, u32[]{:S(2)}, u32[]{:S(2)}) collective-permute-start(bf16[16,512]{1,0:T(8,128)(2,1)S(1)} %fusion.5), channel_id=1, source_target_pairs={{4,6},{5,7},{12,14},{13,15},{20,22},{21,23},{28,30},{29,31},{36,38... | collective-permute-start | bytes 49160 | tf_op jit(solution)/shard_map/ppermute | solution.py:486
  51.1 11.9 %copy-start.16 = (f32[16,512]{1,0:T(8,128)}, f32[16,512]{1,0:T(8,128)S(1)}, u32[]{:S(2)}) copy-start(f32[16,512]{1,0:T(8,128)S(1)} %fusion.17) | copy-start | bytes 98308
  52.8 10.2 %collective-permute-start.5 = (bf16[16,512]{1,0:T(8,128)(2,1)}, bf16[16,512]{1,0:T(8,128)(2,1)}, u32[]{:S(2)}, u32[]{:S(2)}) collective-permute-start(bf16[16,512]{1,0:T(8,128)(2,1)} %fusion.8), channel_id=1, source_target_pairs={{6,4},{7,5},{14,12},{15,13},{22,20},{23,21},{30,28},{31,29},{38,36... | collective-permute-start | bytes 49160 | tf_op jit(solution)/shard_map/ppermute | solution.py:496
  56.1 13.6 %collective-permute-start.8 = (bf16[8,64,512]{2,1,0:T(8,128)(2,1)}, bf16[8,64,512]{2,1,0:T(8,128)(2,1)S(1)}, u32[]{:S(2)}, u32[]{:S(2)}) collective-permute-start(bf16[8,64,512]{2,1,0:T(8,128)(2,1)} %bitcast.14), channel_id=1, source_target_pairs={{0,8},{8,0},{16,24},{24,16},{32,40},{40,32},{48,56},{56,48},{64,72... | collective-permute-start | bytes 1572872 | tf_op jit(solution)/shard_map/ppermute | solution.py:479
  56.1 14.0 %collective-permute-start.9 = (bf16[8,64,512]{2,1,0:T(8,128)(2,1)}, bf16[8,64,512]{2,1,0:T(8,128)(2,1)S(1)}, u32[]{:S(2)}, u32[]{:S(2)}) collective-permute-start(bf16[8,64,512]{2,1,0:T(8,128)(2,1)} %bitcast.14), channel_id=1, source_target_pairs={{8,16},{24,32},{40,48},{56,64},{72,80},{88,96},{104,112},{16,8},{3... | collective-permute-start | bytes 1572872 | tf_op jit(solution)/shard_map/ppermute | solution.py:480
  64.8 13.8 %copy-start.8 = (f32[8,512]{1,0:T(8,128)S(1)}, f32[8,512]{1,0:T(8,128)}, u32[]{:S(2)}) copy-start(f32[8,512]{1,0:T(8,128)} %hop_ref.5) | copy-start | bytes 49156
  64.8 0.8 collective-permute-start.6
  68.1 10.4 %copy-start.1 = (bf16[8,512,512]{2,1,0:T(8,128)(2,1)S(1)}, bf16[8,512,512]{2,1,0:T(8,128)(2,1)}, u32[]{:S(2)}) copy-start(bf16[8,512,512]{2,1,0:T(8,128)(2,1)} %copy-done) | copy-start | bytes 12582916
  68.1 10.2 %collective-permute-start.7 = (bf16[16,512]{1,0:T(8,128)(2,1)}, bf16[16,512]{1,0:T(8,128)(2,1)S(1)}, u32[]{:S(2)}, u32[]{:S(2)}) collective-permute-start(bf16[16,512]{1,0:T(8,128)(2,1)} %fusion.12), channel_id=1, source_target_pairs={{2,0},{3,1},{10,8},{11,9},{18,16},{19,17},{26,24},{27,25},{34,32},... | collective-permute-start | bytes 49160 | tf_op jit(solution)/shard_map/ppermute | solution.py:496
  70.8 2.2 %copy-start.3 = (bf16[8,512,512]{2,1,0:T(8,128)(2,1)S(1)}, bf16[8,512,512]{2,1,0:T(8,128)(2,1)}, u32[]{:S(2)}) copy-start(bf16[8,512,512]{2,1,0:T(8,128)(2,1)} %copy-done.2) | copy-start | bytes 12582916
  74.2 23.5 %copy-start.9 = (f32[1,16,16]{2,1,0:T(8,128)S(1)}, f32[1,16,16]{2,1,0:T(8,128)}, u32[]{:S(2)}) copy-start(f32[1,16,16]{2,1,0:T(8,128)} %param.10) | copy-start | bytes 3076
  80.3 6.1 %collective-permute-start.10 = (f32[192,128]{1,0:T(8,128)S(1)}, f32[192,128]{1,0:T(8,128)S(1)}, u32[]{:S(2)}, u32[]{:S(2)}) collective-permute-start(f32[192,128]{1,0:T(8,128)S(1)} %get-tuple-element.24), channel_id=1, source_target_pairs={{0,1},{1,0},{2,3},{3,2},{4,5},{5,4},{6,7},{7,6},{8,9},{9,8},{10,11... | collective-permute-start | bytes 294920 | tf_op jit(solution)/shard_map/ppermute | solution.py:504
  86.5 5.0 %collective-permute-start.11 = (f32[192,128]{1,0:T(8,128)S(1)}, f32[192,128]{1,0:T(8,128)S(1)}, u32[]{:S(2)}, u32[]{:S(2)}) collective-permute-start(f32[192,128]{1,0:T(8,128)S(1)} %add.94), channel_id=1, source_target_pairs={{0,2},{1,3},{2,0},{3,1},{4,6},{5,7},{6,4},{7,5},{8,10},{9,11},{10,... | collective-permute-start | bytes 294920 | tf_op jit(solution)/shard_map/ppermute | solution.py:504
  91.5 6.2 %collective-permute-start.12 = (f32[192,128]{1,0:T(8,128)S(1)}, f32[192,128]{1,0:T(8,128)S(1)}, u32[]{:S(2)}, u32[]{:S(2)}) collective-permute-start(f32[192,128]{1,0:T(8,128)S(1)} %add.95), channel_id=1, source_target_pairs={{0,4},{1,5},{2,6},{3,7},{4,0},{5,1},{6,2},{7,3},{8,12},{9,13},{10,... | collective-permute-start | bytes 294920 | tf_op jit(solution)/shard_map/ppermute | solution.py:504
  (6 other events, 7.2 us)

commit v2 on v1

--- a/solution.py
+++ b/solution.py
@@ -9,9 +9,9 @@
 
 F32 = jnp.float32
 BF16 = jnp.bfloat16
-VMEM_LIMIT = 32 * 1024 * 1024
+VMEM_LIMIT = 56 * 1024 * 1024
 SMALL_LIMIT = 16 * 1024 * 1024
-SECTIONS = 5
+SECTIONS = 4
 
 
 def mm(left, right):
@@ -41,52 +41,75 @@
 def forward_kernel(
     shift_ref, hop_ref, part_ref, cur_ref, piv_ref,
     fg_ref, source_ref, own_ref, w_ref, pp_ref, op_ref,
-    pbuf, in_sem,
+    pbuf, ppbuf, opbuf, in_sem, pp_sem, op_sem,
 ):
     slabs, width = hop_ref.shape
     shift = shift_ref[0]
 
     def fetch(k):
         return pltpu.make_async_copy(piv_ref.at[shift, k], pbuf.at[k], in_sem.at[k])
+
+    def give_pp(k):
+        return pltpu.make_async_copy(ppbuf.at[k], pp_ref.at[k], pp_sem.at[k])
+
+    def give_op(k):
+        return pltpu.make_async_copy(opbuf.at[k], op_ref.at[k], op_sem.at[k])
 
     for k in range(slabs):
         fetch(k).start()
     down = lax.broadcasted_iota(jnp.int32, (width, width), 0)
     across = lax.broadcasted_iota(jnp.int32, (width, width), 1)
-    part_columns = jnp.transpose(part_ref[...].astype(F32)).astype(jnp.int32)
-    hop_columns = jnp.transpose(hop_ref[...])
+    hop_all = -hop_ref[...]
+    hop_high = hop_all.astype(BF16)
+    rest = hop_all - hop_high.astype(F32)
+    hop_mid = rest.astype(BF16)
+    hop_low = (rest - hop_mid.astype(F32)).astype(BF16)
+    hops = jnp.concatenate(
+        [hop_high.astype(F32), hop_mid.astype(F32), hop_low.astype(F32)], axis=0
+    ).astype(BF16)
     response = None
     vectors = None
     for k in range(slabs):
         gather = jnp.where(down == part_ref[k : k + 1, :], 1.0, 0.0).astype(BF16)
-        weight = jnp.sum(
-            jnp.where(across == part_columns[:, k : k + 1], hop_columns[:, k : k + 1], 0.0),
-            axis=0, keepdims=True,
+        spread = mm_t(hops, gather)
+        weight = (
+            spread[k : k + 1]
+            + spread[slabs + k : slabs + k + 1]
+            + spread[2 * slabs + k : 2 * slabs + k + 1]
         )
         w_ref[k : k + 1, :] = weight
         fetch(k).wait()
-        pivot = pbuf[k]
-        permuted = mm(gather, pivot).astype(BF16)
-        pp_ref[k] = permuted
-        source = mm(cur_ref[k].astype(BF16), pivot)
+        mixed = mm(jnp.concatenate([gather, cur_ref[k].astype(BF16)], axis=0), pbuf[k])
+        permuted = mixed[:width].astype(BF16)
+        source = mixed[width:]
+        ppbuf[k] = permuted
+        give_pp(k).start()
         source_ref[k] = source
         if k == 0:
             unit = jnp.where(down == across, weight, 0.0).astype(BF16)
-            response = -mm(unit, permuted)
+            response = mm(unit, permuted)
             vectors = source
         else:
-            response = -mm((response * weight).astype(BF16), permuted)
-            vectors = source - mm((vectors * weight).astype(BF16), permuted)
+            scaled = jnp.concatenate(
+                [(response * weight).astype(BF16), (vectors * weight).astype(BF16)], axis=0
+            )
+            moved = mm(scaled, permuted)
+            response = moved[:width]
+            vectors = source + moved[width:]
         own_ref[k] = vectors
-        op_ref[k] = response.astype(BF16)
+        opbuf[k] = response.astype(BF16)
+        give_op(k).start()
     fg_ref[:width, :] = response.astype(BF16)
     fg_ref[width:, :] = vectors.astype(BF16)
+    for k in range(slabs):
+        give_pp(k).wait()
+        give_op(k).wait()
 
 
 def forward_range(shift_index, hopping, partner, current, pivot_inverse):
     slabs, rows, width = current.shape
     vm = pl.BlockSpec(memory_space=pltpu.VMEM)
-    hbm = pl.BlockSpec(memory_space=pltpu.HBM)
+    hbm = pl.BlockSpec(memory_space=pl.ANY)
     stack = jax.ShapeDtypeStruct((slabs, width, width), BF16)
     vectors = jax.ShapeDtypeStruct((slabs, rows, width), F32)
     return pl.pallas_call(
@@ -100,11 +123,9 @@
             stack,
         ),
         in_specs=[pl.BlockSpec(memory_space=pltpu.SMEM), vm, vm, vm, hbm],
-        out_specs=(vm,) * 6,
-        scratch_shapes=[
-            pltpu.VMEM((slabs, width, width), BF16),
-            pltpu.SemaphoreType.DMA((slabs,)),
-        ],
+        out_specs=(vm, vm, vm, vm, hbm, hbm),
+        scratch_shapes=[pltpu.VMEM((slabs, width, width), BF16)] * 3
+        + [pltpu.SemaphoreType.DMA((slabs,))] * 3,
         compiler_params=pltpu.CompilerParams(vmem_limit_bytes=VMEM_LIMIT),
         cost_estimate=pl.CostEstimate(
             flops=4 * slabs * width**3, bytes_accessed=6 * slabs * width**2, transcendentals=0
@@ -116,67 +137,174 @@
 def backward_kernel(
     shift_ref, hop_ref, part_ref, own_ref, op_ref, piv_ref,
     sh_ref, q_ref,
-    pbuf, in_sem,
+    pbuf, opbuf, qbuf, in_sem, op_sem, q_sem,
 ):
     slabs, width = hop_ref.shape
     shift = shift_ref[0]
 
     def fetch(k):
         return pltpu.make_async_copy(piv_ref.at[shift, k], pbuf.at[k], in_sem.at[k])
+
+    def fetch_op(k):
+        return pltpu.make_async_copy(op_ref.at[k], opbuf.at[k], op_sem.at[k])
+
+    def give_q(k, source):
+        return pltpu.make_async_copy(source.at[k], q_ref.at[k], q_sem.at[k])
 
     last = slabs - 1
     for k in range(last, -1, -1):
         fetch(k).start()
+        fetch_op(k).start()
     across = lax.broadcasted_iota(jnp.int32, (width, width), 1)
     part_columns = jnp.transpose(part_ref[...].astype(F32)).astype(jnp.int32)
 
     def scatter(k):
         return jnp.where(across == part_columns[:, k : k + 1], 1.0, 0.0).astype(BF16)
 
+    def scaled(k):
+        hop = hop_ref[k : k + 1, :]
+        return jnp.concatenate(
+            [(response * hop).astype(BF16), (vectors * hop).astype(BF16)], axis=0
+        )
+
     fetch(last).wait()
-    q_ref[last] = pbuf[last]
-    response = op_ref[last].astype(F32)
+    give_q(last, pbuf).start()
+    fetch_op(last).wait()
+    response = opbuf[last].astype(F32)
     vectors = own_ref[last]
     for k in range(slabs - 2, -1, -1):
         fetch(k).wait()
         permuted = mm(scatter(k + 1), pbuf[k]).astype(BF16)
-        q_ref[k] = permuted
-        hop = hop_ref[k + 1 : k + 2, :]
-        response = op_ref[k].astype(F32) - mm((response * hop).astype(BF16), permuted)
-        vectors = own_ref[k] - mm((vectors * hop).astype(BF16), permuted)
-    hop = hop_ref[0:1, :]
-    spread = scatter(0)
-    sh_ref[:width, :] = mm((response * hop).astype(BF16), spread).astype(BF16)
-    sh_ref[width:, :] = mm((vectors * hop).astype(BF16), spread).astype(BF16)
+        qbuf[k] = permuted
+        give_q(k, qbuf).start()
+        moved = mm(scaled(k + 1), permuted)
+        fetch_op(k).wait()
+        response = opbuf[k].astype(F32) - moved[:width]
+        vectors = own_ref[k] - moved[width:]
+    sh_ref[...] = mm(scaled(0), scatter(0)).astype(BF16)
+    give_q(last, pbuf).wait()
+    for k in range(last):
+        give_q(k, qbuf).wait()
 
 
 def backward_range(shift_index, hopping, partner, own, op, pivot_inverse):
     slabs, rows, width = own.shape
     vm = pl.BlockSpec(memory_space=pltpu.VMEM)
-    hbm = pl.BlockSpec(memory_space=pltpu.HBM)
+    hbm = pl.BlockSpec(memory_space=pl.ANY)
     stack = jax.ShapeDtypeStruct((slabs, width, width), BF16)
     return pl.pallas_call(
         backward_kernel,
         out_shape=(jax.ShapeDtypeStruct((width + rows, width), BF16), stack),
-        in_specs=[pl.BlockSpec(memory_space=pltpu.SMEM), vm, vm, vm, vm, hbm],
-        out_specs=(vm, vm),
-        scratch_shapes=[
-            pltpu.VMEM((slabs, width, width), BF16),
-            pltpu.SemaphoreType.DMA((slabs,)),
-        ],
+        in_specs=[pl.BlockSpec(memory_space=pltpu.SMEM), vm, vm, vm, hbm, hbm],
+        out_specs=(vm, hbm),
+        scratch_shapes=[pltpu.VMEM((slabs, width, width), BF16)] * 3
+        + [pltpu.SemaphoreType.DMA((slabs,))] * 3,
         compiler_params=pltpu.CompilerParams(vmem_limit_bytes=VMEM_LIMIT),
         cost_estimate=pl.CostEstimate(
             flops=4 * slabs * width**3, bytes_accessed=6 * slabs * width**2, transcendentals=0
         ),
         name="backward_range",
     )(shift_index, hopping, partner, own, op, pivot_inverse)
+
+
+def by_order(own_ref, other_ref, run):
+    odd = lax.axis_index("slab") % 2
+
+    @pl.when(odd == 0)
+    def _():
+        run(own_ref, other_ref, 0)
+
+    @pl.when(odd == 1)
+    def _():
+        run(other_ref, own_ref, 1)
+
+
+def through(op_ref, value):
+    width = op_ref.shape[1]
+    return op_ref[width:, :].astype(F32) + mm(value, op_ref[:width, :])
+
+
+def returned(op_ref, value):
+    width = op_ref.shape[1]
+    return mm_t(value, op_ref[:width, :])
+
+
+def start_kernel(own_ref, other_ref, sent_ref):
+    def run(first_ref, second_ref, odd):
+        width = first_ref.shape[1]
+        sent_ref[...] = through(second_ref, first_ref[width:, :]).astype(BF16)
+
+    by_order(own_ref, other_ref, run)
+
+
+def pass_kernel(own_ref, other_ref, into_ref, new_ref, into_out_ref, sent_ref):
+    into = into_ref[...] + new_ref[...]
+    into_out_ref[...] = into
+
+    def run(first_ref, second_ref, odd):
+        middle = through(first_ref, into).astype(BF16)
+        sent_ref[...] = through(second_ref, middle).astype(BF16)
+
+    by_order(own_ref, other_ref, run)
+
+
+def turn_kernel(
+    own_ref, other_ref, own_back_ref, other_back_ref, into_ref, new_ref,
+    inflow_ref, first_back_ref, second_back_ref, sent_ref,
+):
+    into = into_ref[...] + new_ref[...]
+
+    def run(first_ref, second_ref, odd):
+        first_sh, second_sh = (
+            (other_back_ref, own_back_ref) if odd else (own_back_ref, other_back_ref)
+        )
+        middle = through(first_ref, into).astype(BF16)
+        second_back = through(second_sh, middle)
+        first_back = through(first_sh, into)
+        sent = first_back + returned(first_ref, second_back.astype(BF16))
+        sent_ref[...] = sent.astype(BF16)
+        first_back_ref[...] = first_back
+        second_back_ref[...] = second_back
+        inflow_ref[...] = middle if odd else into
+
+    by_order(own_ref, other_ref, run)
+
+
+def back_kernel(
+    own_ref, other_ref, first_back_ref, second_back_ref, to_ref, new_ref, to_out_ref, sent_ref
+):
+    to = to_ref[...] + new_ref[...]
+    to_out_ref[...] = to
+
+    def run(first_ref, second_ref, odd):
+        middle = (second_back_ref[...] + returned(second_ref, to)).astype(BF16)
+        sent_ref[...] = (first_back_ref[...] + returned(first_ref, middle)).astype(BF16)
+
+    by_order(own_ref, other_ref, run)
+
+
+def small_call(kernel, outs, name, *args):
+    width = args[0].shape[1]
+    rows = args[0].shape[0] - width
+    vm = pl.BlockSpec(memory_space=pltpu.VMEM)
+    return pl.pallas_call(
+        kernel,
+        out_shape=tuple(jax.ShapeDtypeStruct((rows, width), t) for t in outs),
+        in_specs=[vm] * len(args),
+        out_specs=(vm,) * len(outs),
+        compiler_params=pltpu.CompilerParams(vmem_limit_bytes=SMALL_LIMIT),
+        cost_estimate=pl.CostEstimate(
+            flops=4 * rows * width**2, bytes_accessed=4 * width**2, transcendentals=0
+        ),
+        name=name,
+    )(*args)
 
 
 def lower_kernel(inflow_ref, source_ref, w_ref, pp_ref, low_ref):
     slabs = source_ref.shape[0]
     value = inflow_ref[...].astype(F32)
     for k in range(slabs):
-        value = source_ref[k] - mm((value * w_ref[k : k + 1, :]).astype(BF16), pp_ref[k])
+        value = source_ref[k] + mm((value * w_ref[k : k + 1, :]).astype(BF16), pp_ref[k])
         low_ref[k] = value
 
 
@@ -236,12 +364,21 @@
 
 
 def upper_kernel(
-    carried_ref, low_ref, hop_ref, cur_ref, prev_ref, below_ref, above_ref, known_ref, q_ref,
-    x_ref, out_ref,
+    own_ref, other_ref, second_back_ref, to_ref, new_ref, low_ref, hop_ref, cur_ref, prev_ref, below_ref, above_ref, known_ref, q_ref,
+    x_ref, out_ref, carried,
 ):
     slabs, rows, width = low_ref.shape
     near = 2 * below_ref.shape[1]
-    push = carried_ref[...]
+    to = to_ref[...] + new_ref[...]
+
+    def run(first_ref, second_ref, odd):
+        if odd:
+            carried[...] = to
+        else:
+            carried[...] = (second_back_ref[...] + returned(second_ref, to)).astype(BF16)
+
+    by_order(own_ref, other_ref, run)
+    push = carried[...]
     total = None
     for k in range(slabs - 1, -1, -1):
         value = low_ref[k] - mm(push, q_ref[k])
@@ -267,7 +404,9 @@
     )
 
 
-def upper_sweep(carried, low, hopping, current, previous, below, above, known, q):
+def upper_sweep(
+    own, other, second_back, to, new, low, hopping, current, previous, below, above, known, q
+):
     slabs, rows, width = low.shape
     vm = pl.BlockSpec(memory_space=pltpu.VMEM)
     return pl.pallas_call(
@@ -276,17 +415,18 @@
             jax.ShapeDtypeStruct((slabs, rows, width), F32),
             jax.ShapeDtypeStruct(known.shape, F32),
         ),
-        in_specs=[vm] * 9,
+        in_specs=[vm] * 13,
         out_specs=(vm, vm),
+        scratch_shapes=[pltpu.VMEM((rows, width), BF16)],
         compiler_params=pltpu.CompilerParams(vmem_limit_bytes=SMALL_LIMIT),
         cost_estimate=pl.CostEstimate(
             flops=2 * slabs * rows * width**2, bytes_accessed=2 * slabs * width**2, transcendentals=0
         ),
         name="upper_sweep",
-    )(carried, low, hopping, current, previous, below, above, known, q)
-
-
-def factor(gram):
+    )(own, other, second_back, to, new, low, hopping, current, previous, below, above, known, q)
+
+
+def factor_steps(gram, done):
     size = gram.shape[0]
     down = lax.broadcasted_iota(jnp.int32, (size, size), 0)
     across = lax.broadcasted_iota(jnp.int32, (size, size), 1)
@@ -303,18 +443,21 @@
             right_row = right[j : j + 1, :]
             left = left - scale * left_row
             right = right - scale * right_row
+            yield
     inverse_root = 1.0 / jnp.sqrt(pivots)
-    upper = jnp.where(across >= down, left * inverse_root, 0.0)
-    return upper, right * inverse_root
-
-
-def tridiagonal(matrix):
+    done.append(jnp.where(across >= down, left * inverse_root, 0.0))
+    done.append(right * inverse_root)
+
+
+def eigenvalue_steps(matrix, done):
     size = matrix.shape[0]
     row = lax.broadcasted_iota(jnp.int32, (1, size), 1)
     down = lax.broadcasted_iota(jnp.int32, (size, size), 0)
     across = lax.broadcasted_iota(jnp.int32, (size, size), 1)
     diagonal = []
     squares = []
+    bound = jnp.max(jnp.sum(jnp.abs(matrix), axis=1, keepdims=True), axis=0, keepdims=True)
+    bound = bound * (1.0 + 2.0**-18)
 
     def upright(value):
         return jnp.sum(jnp.where(down == across, value, 0.0), axis=1, keepdims=True)
@@ -336,18 +479,11 @@
         w_row = p_row - along * v_row
         w_col = upright(w_row)
         matrix = matrix - (v_col * w_row + w_col * v_row)
+        yield
     a = size - 2
     diagonal.append(matrix[a : a + 1, a : a + 1])
     diagonal.append(matrix[a + 1 : a + 2, a + 1 : a + 2])
     squares.append(matrix[a : a + 1, a + 1 : a + 2] * matrix[a : a + 1, a + 1 : a + 2])
-    return diagonal, squares
-
-
-def eigenvalues(matrix):
-    size = matrix.shape[0]
-    diagonal, squares = tridiagonal(matrix)
-    bound = jnp.max(jnp.sum(jnp.abs(matrix), axis=1, keepdims=True), axis=0, keepdims=True)
-    bound = bound * (1.0 + 2.0**-18)
     shape = (8, 128)
     wide_diagonal = [jnp.broadcast_to(value, shape) for value in diagonal]
     wide_squares = [jnp.broadcast_to(value, shape) for value in squares]
@@ -368,6 +504,8 @@
             pivot = wide_diagonal[i] - shifted - wide_squares[i - 1] / pivot
             pivot = jnp.where(jnp.abs(pivot) < tiny, -tiny, pivot)
             count = count + jnp.where(pivot < 0.0, 1, 0)
+            if i % 4 == 0:
+                yield
         passed = jnp.where(count <= rank, 1.0, 0.0)
         all_passed = jnp.sum(passed, axis=1, keepdims=True)
         late_passed = jnp.sum(jnp.where(second_half, passed, 0.0), axis=1, keepdims=True)
@@ -378,7 +516,7 @@
     even = jnp.broadcast_to(middle[:, 0:1], shape)
     odd = jnp.broadcast_to(middle[:, 127:128], shape)
     place = jnp.where(lane == 2 * level, even, jnp.where(lane == 2 * level + 1, odd, 0.0))
-    return jnp.sum(place, axis=0, keepdims=True)[:, :size]
+    done.append(jnp.sum(place, axis=0, keepdims=True)[:, :size])
 
 
 def finish_kernel(
@@ -397,15 +535,24 @@
     x_known = tail[:, rows : 3 * rows]
     among = jnp.concatenate([tail[:, near - 2 * two : near - two], tail[:, near - two :]], axis=0)
     projection_t = tail[:, rows:two]
+    ritz = []
+    eigen = eigenvalue_steps(0.5 * (projection_t + jnp.transpose(projection_t)), ritz)
+    next(eigen)
     fixed = jnp.concatenate([-projection_t, -coupling_ref[...]], axis=1)
     coefficients_t = x_near + exact(fixed, known_near)
+    next(eigen)
     with_known = x_known + exact(fixed, among) - exact_t(coefficients_t, known_near)
     with_near = coefficients_t - exact(coefficients_t, near_near)
+    next(eigen)
     gram = x_x + exact_t(fixed, x_known) - exact_t(coefficients_t, x_near)
     gram = gram + exact_t(with_known, fixed) - exact_t(with_near, coefficients_t)
-    upper, inverse_t = factor(gram)
+    next(eigen)
+    factors = []
+    for _ in factor_steps(gram, factors):
+        next(eigen)
+    upper, inverse_t = factors
     upper_ref[...] = upper
-    ritz_ref[...] = eigenvalues(0.5 * (projection_t + jnp.transpose(projection_t)))
+    next(eigen)
     down = lax.broadcasted_iota(jnp.int32, (rows, rows), 0)
     across = lax.broadcasted_iota(jnp.int32, (rows, rows), 1)
     unit = jnp.where(down == across, 1.0, 0.0)
@@ -422,6 +569,10 @@
         rest = jnp.concatenate([x_low, cur_low, prev_low], axis=0)
         main = mm(both, stack)
         next_ref[k] = main[:rows] + main[rows:] + mm(weight_high[:, : 3 * rows], rest)
+        next(eigen, None)
+    for _ in eigen:
+        pass
+    ritz_ref[...] = ritz[0]
 
 
 def finish(scale, products, coupling, x, current, previous, below, above):
@@ -450,27 +601,18 @@
 ):
     devices = lax.axis_size("slab")
     slices = lax.axis_size("cuts")
-    odd = lax.axis_index("slab") % 2 == 1
     current = current_block[0]
     previous = previous_block[0]
     slabs, rows, width = current.shape
     scale = 1.0 / (slabs * devices * width)
     swap = [(i, i ^ 1) for i in range(devices)]
 
-    def both(value):
-        other = lax.ppermute(value, "slab", swap)
-        return jnp.where(odd, other, value), jnp.where(odd, value, other)
-
     fg, source, own, weights, pp, op = forward_range(
         shift_index, hopping, partner, current, pivot_inverse
     )
-    fg_first, fg_second = both(fg)
+    fg_other = lax.ppermute(fg, "slab", swap)
     sh, q = backward_range(shift_index, hopping, partner, own, op, pivot_inverse)
-    sh_first, sh_second = both(sh)
-    f_first, g_first = fg_first[:width], fg_first[width:].astype(F32)
-    f_second, g_second = fg_second[:width], fg_second[width:].astype(F32)
-    s_first, h_first = sh_first[:width], sh_first[width:].astype(F32)
-    s_second, h_second = sh_second[:width], sh_second[width:].astype(F32)
+    sh_other = lax.ppermute(sh, "slab", swap)
 
     locked = jnp.swapaxes(locked_vectors[0], 0, 1)
     even_pairs = [(i, i ^ 1) for i in range(slices)]
@@ -479,25 +621,32 @@
     below = lax.ppermute(locked, "cuts", even_pairs)
     above = lax.ppermute(locked, "cuts", odd_pairs)
 
-    into_first = jnp.zeros((rows, width), BF16)
-    for r in range(0, devices - 2, 2):
-        into_second = (g_first + mm(into_first, f_first)).astype(BF16)
-        sent = (g_second + mm(into_second, f_second)).astype(BF16)
-        into_first = into_first + lax.ppermute(sent, "slab", [(r, r + 2), (r + 1, r + 3)])
-    into_second = (g_first + mm(into_first, f_first)).astype(BF16)
-    back_second = h_second + mm(into_second, s_second)
-    back_first = h_first + mm(into_first, s_first)
-    low = lower_sweep(jnp.where(odd, into_second, into_first), source, weights, pp)
+    def up(value, r):
+        return lax.ppermute(value, "slab", [(r, r + 2), (r + 1, r + 3)])
+
+    def back(value, r):
+        return lax.ppermute(value, "slab", [(r, r - 2), (r + 1, r - 1)])
+
+    (sent,) = small_call(start_kernel, (BF16,), "start", fg, fg_other)
+    into = jnp.zeros((rows, width), BF16)
+    new = up(sent, 0)
+    for r in range(2, devices - 2, 2):
+        into, sent = small_call(pass_kernel, (BF16, BF16), "pass_on", fg, fg_other, into, new)
+        new = up(sent, r)
+    inflow, first_back, second_back, sent = small_call(
+        turn_kernel, (BF16, F32, F32, BF16), "turn", fg, fg_other, sh, sh_other, into, new
+    )
+    low = lower_sweep(inflow, source, weights, pp)
     known = known_products(current, previous, below, above)
-    to_second = jnp.zeros((rows, width), BF16)
-    for r in range(devices - 2, 0, -2):
-        to_first = (back_second + mm_t(to_second, f_second)).astype(BF16)
-        sent = (back_first + mm_t(to_first, f_first)).astype(BF16)
-        to_second = to_second + lax.ppermute(sent, "slab", [(r, r - 2), (r + 1, r - 1)])
-    to_first = (back_second + mm_t(to_second, f_second)).astype(BF16)
-    carried = jnp.where(odd, to_second, to_first)
+    to = jnp.zeros((rows, width), BF16)
+    new = back(sent, devices - 2)
+    for r in range(devices - 4, 0, -2):
+        to, sent = small_call(
+            back_kernel, (BF16, BF16), "pass_back", fg, fg_other, first_back, second_back, to, new
+        )
+        new = back(sent, r)
     x, products = upper_sweep(
-        carried, low, hopping, current, previous, below, above, known, q
+        fg, fg_other, second_back, to, new, low, hopping, current, previous, below, above, known, q
     )
     step = 1
     while step < devices:

time: 113 us -> 95.4 us (0.84)
  local copies, waits for them, and re-layouts: 18.6 us -> 0.21 us
  Pallas kernels: 33.9 us -> 41.5 us
  matrix products: 7.08 us -> 0 us
  waiting for transfers between devices: 24.8 us -> 31.4 us
  other arithmetic: 3.01 us -> 0.04 us
  starting transfers between devices: 22.9 us -> 20.5 us
    unnamed x35 -> x23, local copies, waits for them, and re-layouts: 18.6 us -> 0.21 us
    dot_general x10 -> x0, matrix products: 7.08 us -> none  [the longest x4 5.58 us: mm_t(): lax.dot_general(left, right, (((1,), (1,)), ((), ())), preferred_element_...]
    ppermute x1, waiting for transfers between devices: 0.38 us -> 4.08 us  [per_device(): above = lax.ppermute(locked, 'cuts', odd_pairs)]
    pallas_call x1, Pallas kernels: 7.18 us -> 10.4 us  [backward_range(): pl.pallas_call(backward_kernel, out_shape=(jax.ShapeDtypeStruct((width +...]
    select_n x2 -> x0, other arithmetic: 2.24 us -> none  [both(): return (jnp.where(odd, other, value), jnp.where(odd, value, other))]
    pallas_call x0 -> x6, Pallas kernels: none -> 2.22 us  [small_call(): pl.pallas_call(kernel, out_shape=tuple((jax.ShapeDtypeStruct((rows, width...]
    pallas_call x1, Pallas kernels: 9 us -> 11.1 us  [forward_range(): pl.pallas_call(forward_kernel, out_shape=(jax.ShapeDtypeStruct((width + r...]
    ppermute x8, waiting for transfers between devices: 10.9 us -> 13 us  [the longest x3 11.3 us: back(): return lax.ppermute(value, 'slab', [(r, r - 2), (r + 1, r - 1)])]
  transfers between devices with their start and end apart: 13 -> 13, of which waited for: 8 -> 7; matrix products, arithmetic and copies ran while one was open for 8% -> 0% of each run, Pallas kernels for 8% -> 15%
where the time goes in v2:
time: 95.4 us; the launch traced here: 95.1 us
  Pallas kernels  41.5 us (44%)
  waiting for transfers between devices  31.4 us (33%)
  starting transfers between devices  20.5 us (21%)
  between operations  1.51 us (2%)
    ppermute x3, waiting for transfers between devices, per_device(): lax.ppermute(products, 'slab', [(i, i ^ step) for i in range(devices)])  14.3 us
    pallas_call x1, Pallas kernels, finish(): pl.pallas_call(functools.partial(finish_kernel, scale), out_shape=(jax.Sh...  13.8 us
    ppermute x3, waiting for transfers between devices, back(): return lax.ppermute(value, 'slab', [(r, r - 2), (r + 1, r - 1)])  11.3 us
    pallas_call x1, Pallas kernels, forward_range(): pl.pallas_call(forward_kernel, out_shape=(jax.ShapeDtypeStruct((width + r...  11.1 us
    pallas_call x1, Pallas kernels, backward_range(): pl.pallas_call(backward_kernel, out_shape=(jax.ShapeDtypeStruct((width +...  10.4 us
    ppermute x1, starting transfers between devices, per_device(): above = lax.ppermute(locked, 'cuts', odd_pairs)  6.01 us
    ppermute x3, starting transfers between devices, up(): return lax.ppermute(value, 'slab', [(r, r + 2), (r + 1, r + 3)])  5.13 us
    ppermute x1, waiting for transfers between devices, per_device(): above = lax.ppermute(locked, 'cuts', odd_pairs)  4.08 us
  transfers between devices with their start and end apart: 13, of which 7 were waited for; matrix products, arithmetic and copies ran while one was open for 0% of the time, Pallas kernels for 15%

profile of v2, /device:TPU:2, one launch (start us, length us, event | category | flops | bytes accessed | tf_op | source)
XLA Modules:
  0.0 95.1 jit_solution(7059998370465778248)
XLA Ops:
  1.3 11.1 %forward_range.1 = (bf16[528,512]{1,0:T(8,128)(2,1)}, f32[8,16,512]{2,1,0:T(8,128)}, f32[8,16,512]{2,1,0:T(8,128)}, f32[8,512]{1,0:T(8,128)}, bf16[8,512,512]{2,...) custom-call(s32[1]{0:T(128)S(6)} %copy.14.shift_ref, f32[8,512]{1,0:T(8,128)} %hop_ref.5, s32[8,512]{1,0:T(8,128)} %part_ref.3, ...), custom_call_target="tpu_custom_call" | custom-call | flops 4294967296 | bytes 12582912 | tf_op jit(solution)/shard_map/forward_range/pallas_call | solution.py:115
  12.4 2.2 %collective-permute-start = (bf16[528,512]{1,0:T(8,128)(2,1)}, bf16[528,512]{1,0:T(8,128)(2,1)S(1)}, u32[]{:S(2)}, u32[]{:S(2)}) collective-permute-start(bf16[528,512]{1,0:T(8,128)(2,1)} %get-tuple-element.28.own_ref), channel_id=1, source_target_pairs={{0,1},{1,0},{2,3},{3,2},{4,5},{5,4},{6,7},{7,6},{8,9},{9,8},{10,11... | collective-permute-start | bytes 1622024 | tf_op jit(solution)/shard_map/ppermute | solution.py:613
  14.6 10.4 %backward_range.1 = (bf16[528,512]{1,0:T(8,128)(2,1)}, bf16[8,512,512]{2,1,0:T(8,128)(2,1)}) custom-call(s32[1]{0:T(128)S(6)} %copy.14.shift_ref, f32[8,512]{1,0:T(8,128)} %hop_ref.5, s32[8,512]{1,0:T(8,128)} %part_ref.3, f32[8,16,512]{2,1,0:T(8,128)} %get-tuple-element.29.own_ref, bf16[8,512,512]{2,1,0:T(8,128)(2,1)} %get-tuple-element.30.op_ref, ...), custom_call_target="tpu_custom_call" | custom-call | flops 4294967296 | bytes 12582912 | tf_op jit(solution)/shard_map/backward_range/pallas_call | solution.py:195
  25.1 1.5 %collective-permute-start.1 = (bf16[528,512]{1,0:T(8,128)(2,1)}, bf16[528,512]{1,0:T(8,128)(2,1)S(1)}, u32[]{:S(2)}, u32[]{:S(2)}) collective-permute-start(bf16[528,512]{1,0:T(8,128)(2,1)} %get-tuple-element.31.own_back_ref), channel_id=1, source_target_pairs={{0,1},{1,0},{2,3},{3,2},{4,5},{5,4},{6,7},{7,6},{8,9},{9,8},{10,11... | collective-permute-start | bytes 1622024 | tf_op jit(solution)/shard_map/ppermute | solution.py:615
  26.8 6.0 %collective-permute-start.9 = (bf16[8,64,512]{2,1,0:T(8,128)(2,1)S(1)}, bf16[8,64,512]{2,1,0:T(8,128)(2,1)S(1)}, u32[]{:S(2)}, u32[]{:S(2)}) collective-permute-start(bf16[8,64,512]{2,1,0:T(8,128)(2,1)S(1)} %bitcast.19), channel_id=1, source_target_pairs={{8,16},{24,32},{40,48},{56,64},{72,80},{88,96},{104,112},{16,8},{3... | collective-permute-start | bytes 1572872 | tf_op jit(solution)/shard_map/ppermute | solution.py:622
  33.1 3.5 %collective-permute-start.2 = (bf16[16,512]{1,0:T(8,128)(2,1)S(1)}, bf16[16,512]{1,0:T(8,128)(2,1)S(1)}, u32[]{:S(2)}, u32[]{:S(2)}) collective-permute-start(bf16[16,512]{1,0:T(8,128)(2,1)S(1)} %start.1), channel_id=1, source_target_pairs={{0,2},{1,3},{8,10},{9,11},{16,18},{17,19},{24,26},{25,27},{32,34},... | collective-permute-start | bytes 49160 | tf_op jit(solution)/shard_map/ppermute | solution.py:625
  36.6 1.4 %collective-permute-done.2.new_ref = bf16[16,512]{1,0:T(8,128)(2,1)S(1)} collective-permute-done((bf16[16,512]{1,0:T(8,128)(2,1)S(1)}, bf16[16,512]{1,0:T(8,128)(2,1)S(1)}, u32[]{:S(2)}, u32[]{:S(2)}) %collective-permute-start.2) | collective-permute-done | bytes 16416 | tf_op jit(solution)/shard_map/ppermute | solution.py:625
  38.3 1.0 %collective-permute-start.3 = (bf16[16,512]{1,0:T(8,128)(2,1)S(1)}, bf16[16,512]{1,0:T(8,128)(2,1)S(1)}, u32[]{:S(2)}, u32[]{:S(2)}) collective-permute-start(bf16[16,512]{1,0:T(8,128)(2,1)S(1)} %get-tuple-element.33), channel_id=1, source_target_pairs={{2,4},{3,5},{10,12},{11,13},{18,20},{19,21},{26,28},{27,29},{34,36... | collective-permute-start | bytes 49160 | tf_op jit(solution)/shard_map/ppermute | solution.py:625
  39.7 0.7 collective-permute-start.4
  40.6 0.5 turn.1
  41.1 0.7 collective-permute-start.5
  42.3 0.8 collective-permute-start.6
  43.5 1.3 %collective-permute-start.7 = (bf16[16,512]{1,0:T(8,128)(2,1)S(1)}, bf16[16,512]{1,0:T(8,128)(2,1)S(1)}, u32[]{:S(2)}, u32[]{:S(2)}) collective-permute-start(bf16[16,512]{1,0:T(8,128)(2,1)S(1)} %get-tuple-element.42), channel_id=1, source_target_pairs={{2,0},{3,1},{10,8},{11,9},{18,16},{19,17},{26,24},{27,25},{34,32},... | collective-permute-start | bytes 49160 | tf_op jit(solution)/shard_map/ppermute | solution.py:628
  44.9 4.1 %collective-permute-done.9.above_ref = bf16[8,64,512]{2,1,0:T(8,128)(2,1)S(1)} collective-permute-done((bf16[8,64,512]{2,1,0:T(8,128)(2,1)S(1)}, bf16[8,64,512]{2,1,0:T(8,128)(2,1)S(1)}, u32[]{:S(2)}, u32[]{:S(2)}) %collective-permute-start.9) | collective-permute-done | bytes 524320 | tf_op jit(solution)/shard_map/ppermute | solution.py:622
  48.9 0.7 known_products.1.known_ref
  49.7 1.2 %lower_sweep.1.low_ref = f32[8,16,512]{2,1,0:T(8,128)S(1)} custom-call(bf16[16,512]{1,0:T(8,128)(2,1)S(1)} %get-tuple-element.43.inflow_ref, f32[8,16,512]{2,1,0:T(8,128)S(1)} %copy-done.6, f32[8,512]{1,0:T(8,128)S(1)} %copy-done.8, bf16[8,512,512]{2,1,0:T(8,128)(2,1)S(1)} %copy-done.2), custom_call_target="tpu_custom_call" | custom-call | flops 67108864 | bytes 4194304 | tf_op jit(solution)/shard_map/lower_sweep/pallas_call | solution.py:314
  50.9 11.3 %collective-permute-done.7.new_ref = bf16[16,512]{1,0:T(8,128)(2,1)S(1)} collective-permute-done((bf16[16,512]{1,0:T(8,128)(2,1)S(1)}, bf16[16,512]{1,0:T(8,128)(2,1)S(1)}, u32[]{:S(2)}, u32[]{:S(2)}) %collective-permute-start.7) | collective-permute-done | bytes 16416 | tf_op jit(solution)/shard_map/ppermute | solution.py:628
  62.3 2.0 %upper_sweep.1 = (f32[8,16,512]{2,1,0:T(8,128)S(1)}, f32[192,128]{1,0:T(8,128)S(1)}) custom-call(bf16[528,512]{1,0:T(8,128)(2,1)S(1)} %copy-done, bf16[528,512]{1,0:T(8,128)(2,1)S(1)} %collective-permute-done.other_ref, f32[16,512]{1,0:T(8,128)S(1)} %get-tuple-element.36.second_back_ref, bf16[16,512]{1,0:T(8,128)(2,1)S(1)} %get-tuple-element.41.to_ref, ...), custom_call_target="tpu_custom_call" | custom-call | flops 67108864 | bytes 4194304 | tf_op jit(solution)/shard_map/upper_sweep/pallas_call | solution.py:412
  64.3 2.2 %collective-permute-start.10 = (f32[192,128]{1,0:T(8,128)S(1)}, f32[192,128]{1,0:T(8,128)S(1)}, u32[]{:S(2)}, u32[]{:S(2)}) collective-permute-start(f32[192,128]{1,0:T(8,128)S(1)} %get-tuple-element.48), channel_id=1, source_target_pairs={{0,1},{1,0},{2,3},{3,2},{4,5},{5,4},{6,7},{7,6},{8,9},{9,8},{10,11... | collective-permute-start | bytes 294920 | tf_op jit(solution)/shard_map/ppermute | solution.py:653
  66.5 3.9 %collective-permute-done.10 = f32[192,128]{1,0:T(8,128)S(1)} collective-permute-done((f32[192,128]{1,0:T(8,128)S(1)}, f32[192,128]{1,0:T(8,128)S(1)}, u32[]{:S(2)}, u32[]{:S(2)}) %collective-permute-start.10) | collective-permute-done | bytes 98336 | tf_op jit(solution)/shard_map/ppermute | solution.py:653
  70.4 0.5 collective-permute-start.11
  70.9 4.2 %collective-permute-done.11 = f32[192,128]{1,0:T(8,128)S(1)} collective-permute-done((f32[192,128]{1,0:T(8,128)S(1)}, f32[192,128]{1,0:T(8,128)S(1)}, u32[]{:S(2)}, u32[]{:S(2)}) %collective-permute-start.11) | collective-permute-done | bytes 98336 | tf_op jit(solution)/shard_map/ppermute | solution.py:653
  75.2 6.1 %collective-permute-done.12 = f32[192,128]{1,0:T(8,128)S(1)} collective-permute-done((f32[192,128]{1,0:T(8,128)S(1)}, f32[192,128]{1,0:T(8,128)S(1)}, u32[]{:S(2)}, u32[]{:S(2)}) %collective-permute-start.12) | collective-permute-done | bytes 98336 | tf_op jit(solution)/shard_map/ppermute | solution.py:653
  81.4 13.8 %finish.1 = (f32[8,16,512]{2,1,0:T(8,128)}, f32[16,16]{1,0:T(8,128)}, f32[1,16]{1,0:T(1,128)}) custom-call(f32[192,128]{1,0:T(8,128)S(1)} %add.11.products_ref, f32[16,16]{1,0:T(8,128)S(1)} %bitcast.17, f32[8,16,512]{2,1,0:T(8,128)S(1)} %get-tuple-element.49.x_ref, f32[8,16,512]{2,1,0:T(8,128)S(1)} %bitcast.13, f32[8,16,512]{2,1,0:T(8,128)S(1)} %bitcast.16, ...), custom_call_target="tpu_custom_call" | custom-call | tf_op jit(solution)/shard_map/finish/pallas_call | solution.py:580
  (41 shorter events, 2.4 us)
Async XLA Ops:
  12.4 20.4 %collective-permute-start = (bf16[528,512]{1,0:T(8,128)(2,1)}, bf16[528,512]{1,0:T(8,128)(2,1)S(1)}, u32[]{:S(2)}, u32[]{:S(2)}) collective-permute-start(bf16[528,512]{1,0:T(8,128)(2,1)} %get-tuple-element.28.own_ref), channel_id=1, source_target_pairs={{0,1},{1,0},{2,3},{3,2},{4,5},{5,4},{6,7},{7,6},{8,9},{9,8},{10,11... | collective-permute-start | bytes 1622024 | tf_op jit(solution)/shard_map/ppermute | solution.py:613
  14.6 11.9 %copy-start.10 = (bf16[1,64,8,512]{3,2,1,0:T(8,128)(2,1)S(1)}, bf16[1,64,8,512]{3,2,1,0:T(8,128)(2,1)}, u32[]{:S(2)}) copy-start(bf16[1,64,8,512]{3,2,1,0:T(8,128)(2,1)} %param.11) | copy-start | bytes 1572868
  14.6 18.2 %copy-start = (bf16[528,512]{1,0:T(8,128)(2,1)S(1)}, bf16[528,512]{1,0:T(8,128)(2,1)}, u32[]{:S(2)}) copy-start(bf16[528,512]{1,0:T(8,128)(2,1)} %get-tuple-element.28.own_ref) | copy-start | bytes 1622020
  25.1 15.6 %copy-start.5 = (bf16[528,512]{1,0:T(8,128)(2,1)S(1)}, bf16[528,512]{1,0:T(8,128)(2,1)}, u32[]{:S(2)}) copy-start(bf16[528,512]{1,0:T(8,128)(2,1)} %get-tuple-element.31.own_back_ref) | copy-start | bytes 1622020
  25.1 15.5 %collective-permute-start.1 = (bf16[528,512]{1,0:T(8,128)(2,1)}, bf16[528,512]{1,0:T(8,128)(2,1)S(1)}, u32[]{:S(2)}, u32[]{:S(2)}) collective-permute-start(bf16[528,512]{1,0:T(8,128)(2,1)} %get-tuple-element.31.own_back_ref), channel_id=1, source_target_pairs={{0,1},{1,0},{2,3},{3,2},{4,5},{5,4},{6,7},{7,6},{8,9},{9,8},{10,11... | collective-permute-start | bytes 1622024 | tf_op jit(solution)/shard_map/ppermute | solution.py:615
  26.7 22.2 %copy-start.3 = (f32[1,8,16,512]{3,2,1,0:T(8,128)S(1)}, f32[1,8,16,512]{3,2,1,0:T(8,128)}, u32[]{:S(2)}) copy-start(f32[1,8,16,512]{3,2,1,0:T(8,128)} %param.8) | copy-start | bytes 786436
  26.7 22.2 %copy-start.4 = (f32[1,8,16,512]{3,2,1,0:T(8,128)S(1)}, f32[1,8,16,512]{3,2,1,0:T(8,128)}, u32[]{:S(2)}) copy-start(f32[1,8,16,512]{3,2,1,0:T(8,128)} %param.9) | copy-start | bytes 786436
  26.7 18.1 %collective-permute-start.8 = (bf16[8,64,512]{2,1,0:T(8,128)(2,1)S(1)}, bf16[8,64,512]{2,1,0:T(8,128)(2,1)S(1)}, u32[]{:S(2)}, u32[]{:S(2)}) collective-permute-start(bf16[8,64,512]{2,1,0:T(8,128)(2,1)S(1)} %bitcast.18), channel_id=1, source_target_pairs={{0,8},{8,0},{16,24},{24,16},{32,40},{40,32},{48,56},{56,48},{64,72... | collective-permute-start | bytes 1572872 | tf_op jit(solution)/shard_map/ppermute | solution.py:621
  26.8 22.1 %collective-permute-start.9 = (bf16[8,64,512]{2,1,0:T(8,128)(2,1)S(1)}, bf16[8,64,512]{2,1,0:T(8,128)(2,1)S(1)}, u32[]{:S(2)}, u32[]{:S(2)}) collective-permute-start(bf16[8,64,512]{2,1,0:T(8,128)(2,1)S(1)} %bitcast.19), channel_id=1, source_target_pairs={{8,16},{24,32},{40,48},{56,64},{72,80},{88,96},{104,112},{16,8},{3... | collective-permute-start | bytes 1572872 | tf_op jit(solution)/shard_map/ppermute | solution.py:622
  33.1 4.9 %collective-permute-start.2 = (bf16[16,512]{1,0:T(8,128)(2,1)S(1)}, bf16[16,512]{1,0:T(8,128)(2,1)S(1)}, u32[]{:S(2)}, u32[]{:S(2)}) collective-permute-start(bf16[16,512]{1,0:T(8,128)(2,1)S(1)} %start.1), channel_id=1, source_target_pairs={{0,2},{1,3},{8,10},{9,11},{16,18},{17,19},{24,26},{25,27},{32,34},... | collective-permute-start | bytes 49160 | tf_op jit(solution)/shard_map/ppermute | solution.py:625
  38.0 11.7 %copy-start.2 = (bf16[8,512,512]{2,1,0:T(8,128)(2,1)S(1)}, bf16[8,512,512]{2,1,0:T(8,128)(2,1)}, u32[]{:S(2)}) copy-start(bf16[8,512,512]{2,1,0:T(8,128)(2,1)} %get-tuple-element.46.pp_ref) | copy-start | bytes 12582916
  38.0 11.7 %copy-start.6 = (f32[8,16,512]{2,1,0:T(8,128)S(1)}, f32[8,16,512]{2,1,0:T(8,128)}, u32[]{:S(2)}) copy-start(f32[8,16,512]{2,1,0:T(8,128)} %get-tuple-element.44.source_ref) | copy-start | bytes 786436
  38.0 11.7 %copy-start.8 = (f32[8,512]{1,0:T(8,128)S(1)}, f32[8,512]{1,0:T(8,128)}, u32[]{:S(2)}) copy-start(f32[8,512]{1,0:T(8,128)} %get-tuple-element.45.w_ref) | copy-start | bytes 49156
  38.3 1.0 %collective-permute-start.3 = (bf16[16,512]{1,0:T(8,128)(2,1)S(1)}, bf16[16,512]{1,0:T(8,128)(2,1)S(1)}, u32[]{:S(2)}, u32[]{:S(2)}) collective-permute-start(bf16[16,512]{1,0:T(8,128)(2,1)S(1)} %get-tuple-element.33), channel_id=1, source_target_pairs={{2,4},{3,5},{10,12},{11,13},{18,20},{19,21},{26,28},{27,29},{34,36... | collective-permute-start | bytes 49160 | tf_op jit(solution)/shard_map/ppermute | solution.py:625
  39.7 1.0 %collective-permute-start.4 = (bf16[16,512]{1,0:T(8,128)(2,1)S(1)}, bf16[16,512]{1,0:T(8,128)(2,1)S(1)}, u32[]{:S(2)}, u32[]{:S(2)}) collective-permute-start(bf16[16,512]{1,0:T(8,128)(2,1)S(1)} %get-tuple-element.35), channel_id=1, source_target_pairs={{4,6},{5,7},{12,14},{13,15},{20,22},{21,23},{28,30},{29,31},{36,38... | collective-permute-start | bytes 49160 | tf_op jit(solution)/shard_map/ppermute | solution.py:625
  41.1 0.7 collective-permute-start.5
  41.8 20.4 %copy-start.1 = (bf16[8,512,512]{2,1,0:T(8,128)(2,1)S(1)}, bf16[8,512,512]{2,1,0:T(8,128)(2,1)}, u32[]{:S(2)}) copy-start(bf16[8,512,512]{2,1,0:T(8,128)(2,1)} %get-tuple-element.47.q_ref) | copy-start | bytes 12582916
  41.8 20.4 %copy-start.7 = (f32[8,512]{1,0:T(8,128)S(1)}, f32[8,512]{1,0:T(8,128)}, u32[]{:S(2)}) copy-start(f32[8,512]{1,0:T(8,128)} %hop_ref.5) | copy-start | bytes 49156
  42.3 0.8 collective-permute-start.6
  43.5 18.7 %collective-permute-start.7 = (bf16[16,512]{1,0:T(8,128)(2,1)S(1)}, bf16[16,512]{1,0:T(8,128)(2,1)S(1)}, u32[]{:S(2)}, u32[]{:S(2)}) collective-permute-start(bf16[16,512]{1,0:T(8,128)(2,1)S(1)} %get-tuple-element.42), channel_id=1, source_target_pairs={{2,0},{3,1},{10,8},{11,9},{18,16},{19,17},{26,24},{27,25},{34,32},... | collective-permute-start | bytes 49160 | tf_op jit(solution)/shard_map/ppermute | solution.py:628
  50.9 30.4 %copy-start.9 = (f32[1,16,16]{2,1,0:T(8,128)S(1)}, f32[1,16,16]{2,1,0:T(8,128)}, u32[]{:S(2)}) copy-start(f32[1,16,16]{2,1,0:T(8,128)} %param.10) | copy-start | bytes 3076
  64.3 6.1 %collective-permute-start.10 = (f32[192,128]{1,0:T(8,128)S(1)}, f32[192,128]{1,0:T(8,128)S(1)}, u32[]{:S(2)}, u32[]{:S(2)}) collective-permute-start(f32[192,128]{1,0:T(8,128)S(1)} %get-tuple-element.48), channel_id=1, source_target_pairs={{0,1},{1,0},{2,3},{3,2},{4,5},{5,4},{6,7},{7,6},{8,9},{9,8},{10,11... | collective-permute-start | bytes 294920 | tf_op jit(solution)/shard_map/ppermute | solution.py:653
  70.4 4.7 %collective-permute-start.11 = (f32[192,128]{1,0:T(8,128)S(1)}, f32[192,128]{1,0:T(8,128)S(1)}, u32[]{:S(2)}, u32[]{:S(2)}) collective-permute-start(f32[192,128]{1,0:T(8,128)S(1)} %add.9), channel_id=1, source_target_pairs={{0,2},{1,3},{2,0},{3,1},{4,6},{5,7},{6,4},{7,5},{8,10},{9,11},{10,... | collective-permute-start | bytes 294920 | tf_op jit(solution)/shard_map/ppermute | solution.py:653
  75.2 6.2 %collective-permute-start.12 = (f32[192,128]{1,0:T(8,128)S(1)}, f32[192,128]{1,0:T(8,128)S(1)}, u32[]{:S(2)}, u32[]{:S(2)}) collective-permute-start(f32[192,128]{1,0:T(8,128)S(1)} %add.10), channel_id=1, source_target_pairs={{0,4},{1,5},{2,6},{3,7},{4,0},{5,1},{6,2},{7,3},{8,12},{9,13},{10,... | collective-permute-start | bytes 294920 | tf_op jit(solution)/shard_map/ppermute | solution.py:653

commit v3 on v2

--- a/solution.py
+++ b/solution.py
@@ -12,6 +12,7 @@
 VMEM_LIMIT = 56 * 1024 * 1024
 SMALL_LIMIT = 16 * 1024 * 1024
 SECTIONS = 4
+AHEAD = 3
 
 
 def mm(left, right):
@@ -40,8 +41,8 @@
 
 def forward_kernel(
     shift_ref, hop_ref, part_ref, cur_ref, piv_ref,
-    fg_ref, source_ref, own_ref, w_ref, pp_ref, op_ref,
-    pbuf, ppbuf, opbuf, in_sem, pp_sem, op_sem,
+    fg_ref, own_ref, op_ref,
+    pbuf, opbuf, hops, parts, sources, in_sem, op_sem, small_sem,
 ):
     slabs, width = hop_ref.shape
     shift = shift_ref[0]
@@ -49,60 +50,44 @@
     def fetch(k):
         return pltpu.make_async_copy(piv_ref.at[shift, k], pbuf.at[k], in_sem.at[k])
 
-    def give_pp(k):
-        return pltpu.make_async_copy(ppbuf.at[k], pp_ref.at[k], pp_sem.at[k])
-
     def give_op(k):
         return pltpu.make_async_copy(opbuf.at[k], op_ref.at[k], op_sem.at[k])
 
-    for k in range(slabs):
+    small = [
+        pltpu.make_async_copy(part_ref, parts, small_sem.at[0]),
+        pltpu.make_async_copy(hop_ref, hops, small_sem.at[1]),
+        pltpu.make_async_copy(cur_ref, sources, small_sem.at[2]),
+    ]
+    for copy in small:
+        copy.start()
+    for k in range(AHEAD):
         fetch(k).start()
     down = lax.broadcasted_iota(jnp.int32, (width, width), 0)
-    across = lax.broadcasted_iota(jnp.int32, (width, width), 1)
-    hop_all = -hop_ref[...]
-    hop_high = hop_all.astype(BF16)
-    rest = hop_all - hop_high.astype(F32)
-    hop_mid = rest.astype(BF16)
-    hop_low = (rest - hop_mid.astype(F32)).astype(BF16)
-    hops = jnp.concatenate(
-        [hop_high.astype(F32), hop_mid.astype(F32), hop_low.astype(F32)], axis=0
-    ).astype(BF16)
-    response = None
+    for copy in small:
+        copy.wait()
     vectors = None
     for k in range(slabs):
-        gather = jnp.where(down == part_ref[k : k + 1, :], 1.0, 0.0).astype(BF16)
-        spread = mm_t(hops, gather)
-        weight = (
-            spread[k : k + 1]
-            + spread[slabs + k : slabs + k + 1]
-            + spread[2 * slabs + k : 2 * slabs + k + 1]
-        )
-        w_ref[k : k + 1, :] = weight
+        gather = jnp.where(
+            down == parts[k : k + 1, :], -hops[k : k + 1, :], 0.0
+        ).astype(BF16)
         fetch(k).wait()
-        mixed = mm(jnp.concatenate([gather, cur_ref[k].astype(BF16)], axis=0), pbuf[k])
-        permuted = mixed[:width].astype(BF16)
+        if k + AHEAD < slabs:
+            fetch(k + AHEAD).start()
+        mixed = mm(jnp.concatenate([gather, sources[k].astype(BF16)], axis=0), pbuf[k])
+        step = mixed[:width].astype(BF16)
         source = mixed[width:]
-        ppbuf[k] = permuted
-        give_pp(k).start()
-        source_ref[k] = source
         if k == 0:
-            unit = jnp.where(down == across, weight, 0.0).astype(BF16)
-            response = mm(unit, permuted)
+            opbuf[k] = step
             vectors = source
         else:
-            scaled = jnp.concatenate(
-                [(response * weight).astype(BF16), (vectors * weight).astype(BF16)], axis=0
-            )
-            moved = mm(scaled, permuted)
-            response = moved[:width]
+            moved = mm(jnp.concatenate([opbuf[k - 1], vectors.astype(BF16)], axis=0), step)
+            opbuf[k] = moved[:width].astype(BF16)
             vectors = source + moved[width:]
+        give_op(k).start()
         own_ref[k] = vectors
-        opbuf[k] = response.astype(BF16)
-        give_op(k).start()
-    fg_ref[:width, :] = response.astype(BF16)
+    fg_ref[:width, :] = opbuf[slabs - 1]
     fg_ref[width:, :] = vectors.astype(BF16)
     for k in range(slabs):
-        give_pp(k).wait()
         give_op(k).wait()
 
 
@@ -110,22 +95,25 @@
     slabs, rows, width = current.shape
     vm = pl.BlockSpec(memory_space=pltpu.VMEM)
     hbm = pl.BlockSpec(memory_space=pl.ANY)
-    stack = jax.ShapeDtypeStruct((slabs, width, width), BF16)
-    vectors = jax.ShapeDtypeStruct((slabs, rows, width), F32)
     return pl.pallas_call(
         forward_kernel,
         out_shape=(
             jax.ShapeDtypeStruct((width + rows, width), BF16),
-            vectors,
-            vectors,
-            jax.ShapeDtypeStruct((slabs, width), F32),
-            stack,
-            stack,
-        ),
-        in_specs=[pl.BlockSpec(memory_space=pltpu.SMEM), vm, vm, vm, hbm],
-        out_specs=(vm, vm, vm, vm, hbm, hbm),
-        scratch_shapes=[pltpu.VMEM((slabs, width, width), BF16)] * 3
-        + [pltpu.SemaphoreType.DMA((slabs,))] * 3,
+            jax.ShapeDtypeStruct((slabs, rows, width), F32),
+            jax.ShapeDtypeStruct((slabs, width, width), BF16),
+        ),
+        in_specs=[pl.BlockSpec(memory_space=pltpu.SMEM), hbm, hbm, hbm, hbm],
+        out_specs=(vm, vm, hbm),
+        scratch_shapes=[
+            pltpu.VMEM((slabs, width, width), BF16),
+            pltpu.VMEM((slabs, width, width), BF16),
+            pltpu.VMEM((slabs, width), F32),
+            pltpu.VMEM((slabs, width), jnp.int32),
+            pltpu.VMEM((slabs, rows, width), F32),
+            pltpu.SemaphoreType.DMA((slabs,)),
+            pltpu.SemaphoreType.DMA((slabs,)),
+            pltpu.SemaphoreType.DMA((3,)),
+        ],
         compiler_params=pltpu.CompilerParams(vmem_limit_bytes=VMEM_LIMIT),
         cost_estimate=pl.CostEstimate(
             flops=4 * slabs * width**3, bytes_accessed=6 * slabs * width**2, transcendentals=0
@@ -300,28 +288,46 @@
     )(*args)
 
 
-def lower_kernel(inflow_ref, source_ref, w_ref, pp_ref, low_ref):
-    slabs = source_ref.shape[0]
+def lower_kernel(shift_ref, inflow_ref, cur_ref, hop_ref, part_ref, piv_ref, low_ref, pbuf, sem):
+    slabs, rows, width = cur_ref.shape
+    shift = shift_ref[0]
+
+    def fetch(k):
+        return pltpu.make_async_copy(piv_ref.at[shift, k], pbuf.at[k], sem.at[k])
+
+    for k in range(slabs):
+        fetch(k).start()
+    down = lax.broadcasted_iota(jnp.int32, (width, width), 0)
     value = inflow_ref[...].astype(F32)
     for k in range(slabs):
-        value = source_ref[k] + mm((value * w_ref[k : k + 1, :]).astype(BF16), pp_ref[k])
+        bonds = jnp.where(down == part_ref[k : k + 1, :], 1.0, 0.0).astype(BF16)
+        high, low = halves(value)
+        pulled = mm(jnp.concatenate([high, low], axis=0), bonds)
+        reduced = cur_ref[k] - hop_ref[k : k + 1, :] * (pulled[:rows] + pulled[rows:])
+        fetch(k).wait()
+        value = mm(reduced.astype(BF16), pbuf[k])
         low_ref[k] = value
 
 
-def lower_sweep(inflow, source, weights, pp):
-    slabs, rows, width = source.shape
+def lower_sweep(shift_index, inflow, current, hopping, partner, pivot_inverse):
+    slabs, rows, width = current.shape
     vm = pl.BlockSpec(memory_space=pltpu.VMEM)
     return pl.pallas_call(
         lower_kernel,
         out_shape=jax.ShapeDtypeStruct((slabs, rows, width), F32),
-        in_specs=[vm] * 4,
+        in_specs=[pl.BlockSpec(memory_space=pltpu.SMEM), vm, vm, vm, vm]
+        + [pl.BlockSpec(memory_space=pl.ANY)],
         out_specs=vm,
+        scratch_shapes=[
+            pltpu.VMEM((slabs, width, width), BF16),
+            pltpu.SemaphoreType.DMA((slabs,)),
+        ],
         compiler_params=pltpu.CompilerParams(vmem_limit_bytes=SMALL_LIMIT),
         cost_estimate=pl.CostEstimate(
             flops=2 * slabs * rows * width**2, bytes_accessed=2 * slabs * width**2, transcendentals=0
         ),
         name="lower_sweep",
-    )(inflow, source, weights, pp)
+    )(shift_index, inflow, current, hopping, partner, pivot_inverse)
 
 
 def known_kernel(cur_ref, prev_ref, below_ref, above_ref, out_ref):
@@ -451,39 +457,60 @@
 
 def eigenvalue_steps(matrix, done):
     size = matrix.shape[0]
-    row = lax.broadcasted_iota(jnp.int32, (1, size), 1)
-    down = lax.broadcasted_iota(jnp.int32, (size, size), 0)
-    across = lax.broadcasted_iota(jnp.int32, (size, size), 1)
+    full = (size, 128)
+    down = lax.broadcasted_iota(jnp.int32, full, 0)
+    across = lax.broadcasted_iota(jnp.int32, full, 1)
+    bound = jnp.max(jnp.sum(jnp.abs(matrix), axis=1, keepdims=True), axis=0, keepdims=True)
+    bound = bound * (1.0 + 2.0**-18)
+    matrix = jnp.concatenate([matrix, jnp.zeros((size, 128 - size), F32)], axis=1)
     diagonal = []
     squares = []
-    bound = jnp.max(jnp.sum(jnp.abs(matrix), axis=1, keepdims=True), axis=0, keepdims=True)
-    bound = bound * (1.0 + 2.0**-18)
 
     def upright(value):
-        return jnp.sum(jnp.where(down == across, value, 0.0), axis=1, keepdims=True)
-
+        return jnp.broadcast_to(
+            jnp.sum(jnp.where(down == across, value, 0.0), axis=1, keepdims=True), full
+        )
+
+    def line(value, i):
+        return jnp.broadcast_to(value[i : i + 1, :], full)
+
+    def total(value):
+        return jnp.broadcast_to(jnp.sum(value, axis=0, keepdims=True), full)
+
+    row = line(matrix, 0)
+    col = upright(row)
     for j in range(size - 2):
-        diagonal.append(matrix[j : j + 1, j : j + 1])
-        beside = jnp.where(row > j, matrix[j : j + 1, :], 0.0)
-        square = jnp.sum(beside * beside, axis=1, keepdims=True)
-        squares.append(square)
+        diagonal.append(col[j : j + 1, :])
+        next_row = line(matrix, j + 1)
+        next_col = upright(next_row)
+        below = jnp.where(down > j, col, 0.0)
+        beside = jnp.where(across > j, row, 0.0)
+        image_row = total(matrix * below)
+        image_col = upright(image_row)
+        square = total(below * below)
+        squares.append(square[0:1, :])
         length = jnp.sqrt(square)
-        lead = matrix[j : j + 1, j + 1 : j + 2]
+        lead = line(col, j + 1)
         signed = jnp.where(lead >= 0.0, length, -length)
         half = square + length * jnp.abs(lead)
         scale = jnp.where(half > 0.0, 1.0 / jnp.where(half > 0.0, half, 1.0), 0.0)
-        v_row = beside + jnp.where(row == j + 1, signed, 0.0)
-        v_col = upright(v_row)
-        p_row = scale * jnp.sum(matrix * v_col, axis=0, keepdims=True)
-        along = 0.5 * scale * jnp.sum(p_row * v_row, axis=1, keepdims=True)
-        w_row = p_row - along * v_row
-        w_col = upright(w_row)
+        v_row = beside + jnp.where(across == j + 1, signed, 0.0)
+        v_col = below + jnp.where(down == j + 1, signed, 0.0)
+        q_row = image_row + signed * next_row
+        q_col = image_col + signed * next_col
+        along = 0.5 * scale * (scale * total(q_col * v_col))
+        w_row = scale * q_row - along * v_row
+        w_col = scale * q_col - along * v_col
         matrix = matrix - (v_col * w_row + w_col * v_row)
+        lead_v = line(v_col, j + 1)
+        lead_w = line(w_col, j + 1)
+        row = next_row - (v_row * lead_w + w_row * lead_v)
+        col = next_col - (v_col * lead_w + w_col * lead_v)
         yield
     a = size - 2
-    diagonal.append(matrix[a : a + 1, a : a + 1])
-    diagonal.append(matrix[a + 1 : a + 2, a + 1 : a + 2])
-    squares.append(matrix[a : a + 1, a + 1 : a + 2] * matrix[a : a + 1, a + 1 : a + 2])
+    diagonal.append(col[a : a + 1, :])
+    squares.append(col[a + 1 : a + 2, :] * col[a + 1 : a + 2, :])
+    diagonal.append(upright(line(matrix, a + 1))[a + 1 : a + 2, :])
     shape = (8, 128)
     wide_diagonal = [jnp.broadcast_to(value, shape) for value in diagonal]
     wide_squares = [jnp.broadcast_to(value, shape) for value in squares]
@@ -607,7 +634,7 @@
     scale = 1.0 / (slabs * devices * width)
     swap = [(i, i ^ 1) for i in range(devices)]
 
-    fg, source, own, weights, pp, op = forward_range(
+    fg, own, op = forward_range(
         shift_index, hopping, partner, current, pivot_inverse
     )
     fg_other = lax.ppermute(fg, "slab", swap)
@@ -636,7 +663,7 @@
     inflow, first_back, second_back, sent = small_call(
         turn_kernel, (BF16, F32, F32, BF16), "turn", fg, fg_other, sh, sh_other, into, new
     )
-    low = lower_sweep(inflow, source, weights, pp)
+    low = lower_sweep(shift_index, inflow, current, hopping, partner, pivot_inverse)
     known = known_products(current, previous, below, above)
     to = jnp.zeros((rows, width), BF16)
     new = back(sent, devices - 2)

time: 95.4 us -> 88.2 us (0.925)
  Pallas kernels: 41.5 us -> 32.5 us
  waiting for transfers between devices: 31.4 us -> 23.2 us
  starting transfers between devices: 20.5 us -> 26.6 us
  local copies, waits for them, and re-layouts: 0.21 us -> 3.58 us
    pallas_call x1, Pallas kernels: 13.8 us -> 3.79 us  [finish(): pl.pallas_call(functools.partial(finish_kernel, scale), out_shape=(jax.Sh...]
    ppermute x3, starting transfers between devices: 2.75 us -> 9.28 us  [per_device(): lax.ppermute(products, 'slab', [(i, i ^ step) for i in range(devices)])]
    ppermute x3, waiting for transfers between devices: 11.3 us -> 5.49 us  [back(): return lax.ppermute(value, 'slab', [(r, r - 2), (r + 1, r - 1)])]
    unnamed x23 -> x21, local copies, waits for them, and re-layouts: 0.21 us -> 3.57 us
    ppermute x3, waiting for transfers between devices: 14.3 us -> 11.5 us  [per_device(): lax.ppermute(products, 'slab', [(i, i ^ step) for i in range(devices)])]
    pallas_call x1, Pallas kernels: 1.24 us -> 3.25 us  [lower_sweep(): pl.pallas_call(lower_kernel, out_shape=jax.ShapeDtypeStruct((slabs, rows,...]
    pallas_call x1, Pallas kernels: 11.1 us -> 10.1 us  [forward_range(): pl.pallas_call(forward_kernel, out_shape=(jax.ShapeDtypeStruct((width + r...]
  transfers between devices with their start and end apart: 13 -> 13, of which waited for: 7 -> 7; matrix products, arithmetic and copies ran while one was open for 0% -> 0% of each run, Pallas kernels for 15% -> 19%
where the time goes in v3:
time: 88.2 us; the launch traced here: 87.4 us
  Pallas kernels  32.5 us (37%)
  starting transfers between devices  26.6 us (30%)
  waiting for transfers between devices  23.2 us (26%)
  local copies, waits for them, and re-layouts  3.58 us (4%)
  between operations  1.5 us (2%)
    ppermute x3, waiting for transfers between devices, per_device(): lax.ppermute(products, 'slab', [(i, i ^ step) for i in range(devices)])  11.5 us
    pallas_call x1, Pallas kernels, backward_range(): pl.pallas_call(backward_kernel, out_shape=(jax.ShapeDtypeStruct((width +...  10.4 us
    pallas_call x1, Pallas kernels, forward_range(): pl.pallas_call(forward_kernel, out_shape=(jax.ShapeDtypeStruct((width + r...  10.1 us
    ppermute x3, starting transfers between devices, per_device(): lax.ppermute(products, 'slab', [(i, i ^ step) for i in range(devices)])  9.28 us
    ppermute x1, starting transfers between devices, per_device(): above = lax.ppermute(locked, 'cuts', odd_pairs)  6.01 us
    ppermute x3, waiting for transfers between devices, back(): return lax.ppermute(value, 'slab', [(r, r - 2), (r + 1, r - 1)])  5.49 us
    ppermute x3, starting transfers between devices, up(): return lax.ppermute(value, 'slab', [(r, r + 2), (r + 1, r + 3)])  4.89 us
    ppermute x1, waiting for transfers between devices, per_device(): above = lax.ppermute(locked, 'cuts', odd_pairs)  4.21 us
  transfers between devices with their start and end apart: 13, of which 7 were waited for; matrix products, arithmetic and copies ran while one was open for 0% of the time, Pallas kernels for 19%

profile of v3, /device:TPU:2, one launch (start us, length us, event | category | flops | bytes accessed | tf_op | source)
XLA Modules:
  0.0 87.4 jit_solution(11698396132029843624)
XLA Ops:
  1.3 10.1 %forward_range.1 = (bf16[528,512]{1,0:T(8,128)(2,1)}, f32[8,16,512]{2,1,0:T(8,128)}, bf16[8,512,512]{2,1,0:T(8,128)(2,1)}) custom-call(s32[1]{0:T(128)S(6)} %copy.14.shift_ref, f32[8,512]{1,0:T(8,128)} %hop_ref.7, s32[8,512]{1,0:T(8,128)} %part_ref.5, f32[8,16,512]{2,1,0:T(8,128)} %bitcast.10, bf16[2,8,512,512]{3,2,1,0:T(8,128)(2,1)} %piv_ref.5), custom_call_target="tpu_custom_call" | custom-call | flops 4294967296 | bytes 12582912 | tf_op jit(solution)/shard_map/forward_range/pallas_call | solution.py:98
  11.4 2.2 %collective-permute-start = (bf16[528,512]{1,0:T(8,128)(2,1)}, bf16[528,512]{1,0:T(8,128)(2,1)S(1)}, u32[]{:S(2)}, u32[]{:S(2)}) collective-permute-start(bf16[528,512]{1,0:T(8,128)(2,1)} %get-tuple-element.25.own_ref), channel_id=1, source_target_pairs={{0,1},{1,0},{2,3},{3,2},{4,5},{5,4},{6,7},{7,6},{8,9},{9,8},{10,11... | collective-permute-start | bytes 1622024 | tf_op jit(solution)/shard_map/ppermute | solution.py:640
  13.6 10.4 %backward_range.1 = (bf16[528,512]{1,0:T(8,128)(2,1)}, bf16[8,512,512]{2,1,0:T(8,128)(2,1)}) custom-call(s32[1]{0:T(128)S(6)} %copy.14.shift_ref, f32[8,512]{1,0:T(8,128)} %hop_ref.7, s32[8,512]{1,0:T(8,128)} %part_ref.5, f32[8,16,512]{2,1,0:T(8,128)} %get-tuple-element.26.own_ref, bf16[8,512,512]{2,1,0:T(8,128)(2,1)} %get-tuple-element.27.op_ref, ...), custom_call_target="tpu_custom_call" | custom-call | flops 4294967296 | bytes 12582912 | tf_op jit(solution)/shard_map/backward_range/pallas_call | solution.py:183
  24.0 1.5 %collective-permute-start.1 = (bf16[528,512]{1,0:T(8,128)(2,1)}, bf16[528,512]{1,0:T(8,128)(2,1)S(1)}, u32[]{:S(2)}, u32[]{:S(2)}) collective-permute-start(bf16[528,512]{1,0:T(8,128)(2,1)} %get-tuple-element.28.own_back_ref), channel_id=1, source_target_pairs={{0,1},{1,0},{2,3},{3,2},{4,5},{5,4},{6,7},{7,6},{8,9},{9,8},{10,11... | collective-permute-start | bytes 1622024 | tf_op jit(solution)/shard_map/ppermute | solution.py:642
  25.8 6.0 %collective-permute-start.9 = (bf16[8,64,512]{2,1,0:T(8,128)(2,1)S(1)}, bf16[8,64,512]{2,1,0:T(8,128)(2,1)S(1)}, u32[]{:S(2)}, u32[]{:S(2)}) collective-permute-start(bf16[8,64,512]{2,1,0:T(8,128)(2,1)S(1)} %bitcast.20), channel_id=1, source_target_pairs={{8,16},{24,32},{40,48},{56,64},{72,80},{88,96},{104,112},{16,8},{3... | collective-permute-start | bytes 1572872 | tf_op jit(solution)/shard_map/ppermute | solution.py:649
  32.0 3.5 %collective-permute-start.2 = (bf16[16,512]{1,0:T(8,128)(2,1)S(1)}, bf16[16,512]{1,0:T(8,128)(2,1)S(1)}, u32[]{:S(2)}, u32[]{:S(2)}) collective-permute-start(bf16[16,512]{1,0:T(8,128)(2,1)S(1)} %start.1), channel_id=1, source_target_pairs={{0,2},{1,3},{8,10},{9,11},{16,18},{17,19},{24,26},{25,27},{32,34},... | collective-permute-start | bytes 49160 | tf_op jit(solution)/shard_map/ppermute | solution.py:652
  35.5 1.4 %collective-permute-done.2.new_ref = bf16[16,512]{1,0:T(8,128)(2,1)S(1)} collective-permute-done((bf16[16,512]{1,0:T(8,128)(2,1)S(1)}, bf16[16,512]{1,0:T(8,128)(2,1)S(1)}, u32[]{:S(2)}, u32[]{:S(2)}) %collective-permute-start.2) | collective-permute-done | bytes 16416 | tf_op jit(solution)/shard_map/ppermute | solution.py:652
  38.3 0.7 collective-permute-start.4
  40.1 0.7 collective-permute-start.5
  41.2 0.7 collective-permute-start.6
  42.3 1.3 %collective-permute-start.7 = (bf16[16,512]{1,0:T(8,128)(2,1)S(1)}, bf16[16,512]{1,0:T(8,128)(2,1)S(1)}, u32[]{:S(2)}, u32[]{:S(2)}) collective-permute-start(bf16[16,512]{1,0:T(8,128)(2,1)S(1)} %get-tuple-element.39), channel_id=1, source_target_pairs={{2,0},{3,1},{10,8},{11,9},{18,16},{19,17},{26,24},{27,25},{34,32},... | collective-permute-start | bytes 49160 | tf_op jit(solution)/shard_map/ppermute | solution.py:655
  43.7 4.2 %collective-permute-done.9.above_ref = bf16[8,64,512]{2,1,0:T(8,128)(2,1)S(1)} collective-permute-done((bf16[8,64,512]{2,1,0:T(8,128)(2,1)S(1)}, bf16[8,64,512]{2,1,0:T(8,128)(2,1)S(1)}, u32[]{:S(2)}, u32[]{:S(2)}) %collective-permute-start.9) | collective-permute-done | bytes 524320 | tf_op jit(solution)/shard_map/ppermute | solution.py:649
  47.9 0.7 known_products.1.known_ref
  48.6 3.4 %copy-done.1 = bf16[2,8,512,512]{3,2,1,0:T(8,128)(2,1)S(1)} copy-done((bf16[2,8,512,512]{3,2,1,0:T(8,128)(2,1)S(1)}, bf16[2,8,512,512]{3,2,1,0:T(8,128)(2,1)}, u32[]{:S(2)}) %copy-start.1) | copy-done | bytes 8388632
  52.0 3.2 %lower_sweep.1.low_ref = f32[8,16,512]{2,1,0:T(8,128)S(1)} custom-call(s32[1]{0:T(128)S(6)} %copy.14.shift_ref, bf16[16,512]{1,0:T(8,128)(2,1)S(1)} %get-tuple-element.40.inflow_ref, f32[8,16,512]{2,1,0:T(8,128)S(1)} %bitcast.12, f32[8,512]{1,0:T(8,128)S(1)} %copy-done.6, s32[8,512]{1,0:T(8,128)S(1)} %copy-done.7, bf16[2,8,512,512]{3,2,1,0:T(8,128)(2,1)S(1)} %copy-done.1), custom_call_target="tpu_custom_call" | custom-call | flops 67108864 | bytes 4194304 | tf_op jit(solution)/shard_map/lower_sweep/pallas_call | solution.py:315
  55.3 5.5 %collective-permute-done.7.new_ref = bf16[16,512]{1,0:T(8,128)(2,1)S(1)} collective-permute-done((bf16[16,512]{1,0:T(8,128)(2,1)S(1)}, bf16[16,512]{1,0:T(8,128)(2,1)S(1)}, u32[]{:S(2)}, u32[]{:S(2)}) %collective-permute-start.7) | collective-permute-done | bytes 16416 | tf_op jit(solution)/shard_map/ppermute | solution.py:655
  60.8 2.0 %upper_sweep.1 = (f32[8,16,512]{2,1,0:T(8,128)S(1)}, f32[192,128]{1,0:T(8,128)S(1)}) custom-call(bf16[528,512]{1,0:T(8,128)(2,1)S(1)} %copy-done, bf16[528,512]{1,0:T(8,128)(2,1)S(1)} %collective-permute-done.other_ref, f32[16,512]{1,0:T(8,128)S(1)} %get-tuple-element.33.second_back_ref, bf16[16,512]{1,0:T(8,128)(2,1)S(1)} %get-tuple-element.38.to_ref, ...), custom_call_target="tpu_custom_call" | custom-call | flops 67108864 | bytes 4194304 | tf_op jit(solution)/shard_map/upper_sweep/pallas_call | solution.py:418
  62.8 2.2 %collective-permute-start.10 = (f32[192,128]{1,0:T(8,128)S(1)}, f32[192,128]{1,0:T(8,128)S(1)}, u32[]{:S(2)}, u32[]{:S(2)}) collective-permute-start(f32[192,128]{1,0:T(8,128)S(1)} %get-tuple-element.42), channel_id=1, source_target_pairs={{0,1},{1,0},{2,3},{3,2},{4,5},{5,4},{6,7},{7,6},{8,9},{9,8},{10,11... | collective-permute-start | bytes 294920 | tf_op jit(solution)/shard_map/ppermute | solution.py:680
  65.0 4.0 %collective-permute-done.10 = f32[192,128]{1,0:T(8,128)S(1)} collective-permute-done((f32[192,128]{1,0:T(8,128)S(1)}, f32[192,128]{1,0:T(8,128)S(1)}, u32[]{:S(2)}, u32[]{:S(2)}) %collective-permute-start.10) | collective-permute-done | bytes 98336 | tf_op jit(solution)/shard_map/ppermute | solution.py:680
  68.9 5.8 %collective-permute-start.11 = (f32[192,128]{1,0:T(8,128)S(1)}, f32[192,128]{1,0:T(8,128)S(1)}, u32[]{:S(2)}, u32[]{:S(2)}) collective-permute-start(f32[192,128]{1,0:T(8,128)S(1)} %add.9), channel_id=1, source_target_pairs={{0,2},{1,3},{2,0},{3,1},{4,6},{5,7},{6,4},{7,5},{8,10},{9,11},{10,... | collective-permute-start | bytes 294920 | tf_op jit(solution)/shard_map/ppermute | solution.py:680
  74.8 2.6 %collective-permute-done.11 = f32[192,128]{1,0:T(8,128)S(1)} collective-permute-done((f32[192,128]{1,0:T(8,128)S(1)}, f32[192,128]{1,0:T(8,128)S(1)}, u32[]{:S(2)}, u32[]{:S(2)}) %collective-permute-start.11) | collective-permute-done | bytes 98336 | tf_op jit(solution)/shard_map/ppermute | solution.py:680
  77.4 1.2 %collective-permute-start.12 = (f32[192,128]{1,0:T(8,128)S(1)}, f32[192,128]{1,0:T(8,128)S(1)}, u32[]{:S(2)}, u32[]{:S(2)}) collective-permute-start(f32[192,128]{1,0:T(8,128)S(1)} %add.10), channel_id=1, source_target_pairs={{0,4},{1,5},{2,6},{3,7},{4,0},{5,1},{6,2},{7,3},{8,12},{9,13},{10,... | collective-permute-start | bytes 294920 | tf_op jit(solution)/shard_map/ppermute | solution.py:680
  78.6 5.0 %collective-permute-done.12 = f32[192,128]{1,0:T(8,128)S(1)} collective-permute-done((f32[192,128]{1,0:T(8,128)S(1)}, f32[192,128]{1,0:T(8,128)S(1)}, u32[]{:S(2)}, u32[]{:S(2)}) %collective-permute-start.12) | collective-permute-done | bytes 98336 | tf_op jit(solution)/shard_map/ppermute | solution.py:680
  83.6 3.8 %finish.1 = (f32[8,16,512]{2,1,0:T(8,128)}, f32[16,16]{1,0:T(8,128)}, f32[1,16]{1,0:T(1,128)}) custom-call(f32[192,128]{1,0:T(8,128)S(1)} %add.11.products_ref, f32[16,16]{1,0:T(8,128)S(1)} %bitcast.18, f32[8,16,512]{2,1,0:T(8,128)S(1)} %get-tuple-element.43.x_ref, f32[8,16,512]{2,1,0:T(8,128)S(1)} %bitcast.14, f32[8,16,512]{2,1,0:T(8,128)S(1)} %bitcast.17, ...), custom_call_target="tpu_custom_call" | custom-call | tf_op jit(solution)/shard_map/finish/pallas_call | solution.py:607
  (39 shorter events, 3.7 us)
Async XLA Ops:
  11.4 20.4 %collective-permute-start = (bf16[528,512]{1,0:T(8,128)(2,1)}, bf16[528,512]{1,0:T(8,128)(2,1)S(1)}, u32[]{:S(2)}, u32[]{:S(2)}) collective-permute-start(bf16[528,512]{1,0:T(8,128)(2,1)} %get-tuple-element.25.own_ref), channel_id=1, source_target_pairs={{0,1},{1,0},{2,3},{3,2},{4,5},{5,4},{6,7},{7,6},{8,9},{9,8},{10,11... | collective-permute-start | bytes 1622024 | tf_op jit(solution)/shard_map/ppermute | solution.py:640
  13.6 11.9 %copy-start.9 = (bf16[1,64,8,512]{3,2,1,0:T(8,128)(2,1)S(1)}, bf16[1,64,8,512]{3,2,1,0:T(8,128)(2,1)}, u32[]{:S(2)}) copy-start(bf16[1,64,8,512]{3,2,1,0:T(8,128)(2,1)} %param.11) | copy-start | bytes 1572868
  13.6 18.3 %copy-start = (bf16[528,512]{1,0:T(8,128)(2,1)S(1)}, bf16[528,512]{1,0:T(8,128)(2,1)}, u32[]{:S(2)}) copy-start(bf16[528,512]{1,0:T(8,128)(2,1)} %get-tuple-element.25.own_ref) | copy-start | bytes 1622020
  24.0 15.5 %copy-start.5 = (bf16[528,512]{1,0:T(8,128)(2,1)S(1)}, bf16[528,512]{1,0:T(8,128)(2,1)}, u32[]{:S(2)}) copy-start(bf16[528,512]{1,0:T(8,128)(2,1)} %get-tuple-element.28.own_back_ref) | copy-start | bytes 1622020
  24.0 15.5 %collective-permute-start.1 = (bf16[528,512]{1,0:T(8,128)(2,1)}, bf16[528,512]{1,0:T(8,128)(2,1)S(1)}, u32[]{:S(2)}, u32[]{:S(2)}) collective-permute-start(bf16[528,512]{1,0:T(8,128)(2,1)} %get-tuple-element.28.own_back_ref), channel_id=1, source_target_pairs={{0,1},{1,0},{2,3},{3,2},{4,5},{5,4},{6,7},{7,6},{8,9},{9,8},{10,11... | collective-permute-start | bytes 1622024 | tf_op jit(solution)/shard_map/ppermute | solution.py:642
  25.7 22.2 %copy-start.2 = (f32[1,8,16,512]{3,2,1,0:T(8,128)S(1)}, f32[1,8,16,512]{3,2,1,0:T(8,128)}, u32[]{:S(2)}) copy-start(f32[1,8,16,512]{3,2,1,0:T(8,128)} %param.8) | copy-start | bytes 786436
  25.7 22.2 %copy-start.4 = (f32[1,8,16,512]{3,2,1,0:T(8,128)S(1)}, f32[1,8,16,512]{3,2,1,0:T(8,128)}, u32[]{:S(2)}) copy-start(f32[1,8,16,512]{3,2,1,0:T(8,128)} %param.9) | copy-start | bytes 786436
  25.7 18.0 %collective-permute-start.8 = (bf16[8,64,512]{2,1,0:T(8,128)(2,1)S(1)}, bf16[8,64,512]{2,1,0:T(8,128)(2,1)S(1)}, u32[]{:S(2)}, u32[]{:S(2)}) collective-permute-start(bf16[8,64,512]{2,1,0:T(8,128)(2,1)S(1)} %bitcast.19), channel_id=1, source_target_pairs={{0,8},{8,0},{16,24},{24,16},{32,40},{40,32},{48,56},{56,48},{64,72... | collective-permute-start | bytes 1572872 | tf_op jit(solution)/shard_map/ppermute | solution.py:648
  25.8 22.1 %collective-permute-start.9 = (bf16[8,64,512]{2,1,0:T(8,128)(2,1)S(1)}, bf16[8,64,512]{2,1,0:T(8,128)(2,1)S(1)}, u32[]{:S(2)}, u32[]{:S(2)}) collective-permute-start(bf16[8,64,512]{2,1,0:T(8,128)(2,1)S(1)} %bitcast.20), channel_id=1, source_target_pairs={{8,16},{24,32},{40,48},{56,64},{72,80},{88,96},{104,112},{16,8},{3... | collective-permute-start | bytes 1572872 | tf_op jit(solution)/shard_map/ppermute | solution.py:649
  32.0 4.9 %collective-permute-start.2 = (bf16[16,512]{1,0:T(8,128)(2,1)S(1)}, bf16[16,512]{1,0:T(8,128)(2,1)S(1)}, u32[]{:S(2)}, u32[]{:S(2)}) collective-permute-start(bf16[16,512]{1,0:T(8,128)(2,1)S(1)} %start.1), channel_id=1, source_target_pairs={{0,2},{1,3},{8,10},{9,11},{16,18},{17,19},{24,26},{25,27},{32,34},... | collective-permute-start | bytes 49160 | tf_op jit(solution)/shard_map/ppermute | solution.py:652
  37.0 11.7 %copy-start.6 = (f32[8,512]{1,0:T(8,128)S(1)}, f32[8,512]{1,0:T(8,128)}, u32[]{:S(2)}) copy-start(f32[8,512]{1,0:T(8,128)} %hop_ref.7) | copy-start | bytes 49156
  37.0 11.7 %copy-start.7 = (s32[8,512]{1,0:T(8,128)S(1)}, s32[8,512]{1,0:T(8,128)}, u32[]{:S(2)}) copy-start(s32[8,512]{1,0:T(8,128)} %part_ref.5) | copy-start | bytes 49156
  37.3 0.7 collective-permute-start.3
  38.3 1.3 %collective-permute-start.4 = (bf16[16,512]{1,0:T(8,128)(2,1)S(1)}, bf16[16,512]{1,0:T(8,128)(2,1)S(1)}, u32[]{:S(2)}, u32[]{:S(2)}) collective-permute-start(bf16[16,512]{1,0:T(8,128)(2,1)S(1)} %get-tuple-element.32), channel_id=1, source_target_pairs={{4,6},{5,7},{12,14},{13,15},{20,22},{21,23},{28,30},{29,31},{36,38... | collective-permute-start | bytes 49160 | tf_op jit(solution)/shard_map/ppermute | solution.py:652
  40.1 0.7 collective-permute-start.5
  41.2 0.7 collective-permute-start.6
  42.3 18.4 %collective-permute-start.7 = (bf16[16,512]{1,0:T(8,128)(2,1)S(1)}, bf16[16,512]{1,0:T(8,128)(2,1)S(1)}, u32[]{:S(2)}, u32[]{:S(2)}) collective-permute-start(bf16[16,512]{1,0:T(8,128)(2,1)S(1)} %get-tuple-element.39), channel_id=1, source_target_pairs={{2,0},{3,1},{10,8},{11,9},{18,16},{19,17},{26,24},{27,25},{34,32},... | collective-permute-start | bytes 49160 | tf_op jit(solution)/shard_map/ppermute | solution.py:655
  48.6 3.4 %copy-start.1 = (bf16[2,8,512,512]{3,2,1,0:T(8,128)(2,1)S(1)}, bf16[2,8,512,512]{3,2,1,0:T(8,128)(2,1)}, u32[]{:S(2)}) copy-start(bf16[2,8,512,512]{3,2,1,0:T(8,128)(2,1)} %piv_ref.5) | copy-start | bytes 25165828
  52.0 8.8 %copy-start.3 = (bf16[8,512,512]{2,1,0:T(8,128)(2,1)S(1)}, bf16[8,512,512]{2,1,0:T(8,128)(2,1)}, u32[]{:S(2)}) copy-start(bf16[8,512,512]{2,1,0:T(8,128)(2,1)} %get-tuple-element.41.q_ref) | copy-start | bytes 12582916
  55.3 28.3 %copy-start.8 = (f32[1,16,16]{2,1,0:T(8,128)S(1)}, f32[1,16,16]{2,1,0:T(8,128)}, u32[]{:S(2)}) copy-start(f32[1,16,16]{2,1,0:T(8,128)} %param.10) | copy-start | bytes 3076
  62.8 6.1 %collective-permute-start.10 = (f32[192,128]{1,0:T(8,128)S(1)}, f32[192,128]{1,0:T(8,128)S(1)}, u32[]{:S(2)}, u32[]{:S(2)}) collective-permute-start(f32[192,128]{1,0:T(8,128)S(1)} %get-tuple-element.42), channel_id=1, source_target_pairs={{0,1},{1,0},{2,3},{3,2},{4,5},{5,4},{6,7},{7,6},{8,9},{9,8},{10,11... | collective-permute-start | bytes 294920 | tf_op jit(solution)/shard_map/ppermute | solution.py:680
  68.9 8.4 %collective-permute-start.11 = (f32[192,128]{1,0:T(8,128)S(1)}, f32[192,128]{1,0:T(8,128)S(1)}, u32[]{:S(2)}, u32[]{:S(2)}) collective-permute-start(f32[192,128]{1,0:T(8,128)S(1)} %add.9), channel_id=1, source_target_pairs={{0,2},{1,3},{2,0},{3,1},{4,6},{5,7},{6,4},{7,5},{8,10},{9,11},{10,... | collective-permute-start | bytes 294920 | tf_op jit(solution)/shard_map/ppermute | solution.py:680
  77.4 6.2 %collective-permute-start.12 = (f32[192,128]{1,0:T(8,128)S(1)}, f32[192,128]{1,0:T(8,128)S(1)}, u32[]{:S(2)}, u32[]{:S(2)}) collective-permute-start(f32[192,128]{1,0:T(8,128)S(1)} %add.10), channel_id=1, source_target_pairs={{0,4},{1,5},{2,6},{3,7},{4,0},{5,1},{6,2},{7,3},{8,12},{9,13},{10,... | collective-permute-start | bytes 294920 | tf_op jit(solution)/shard_map/ppermute | solution.py:680

commit v4 on v3

--- a/solution.py
+++ b/solution.py
@@ -11,6 +11,7 @@
 BF16 = jnp.bfloat16
 VMEM_LIMIT = 56 * 1024 * 1024
 SMALL_LIMIT = 16 * 1024 * 1024
+LOWER_LIMIT = 50 * 1024 * 1024
 SECTIONS = 4
 AHEAD = 3
 
@@ -62,14 +63,16 @@
         copy.start()
     for k in range(AHEAD):
         fetch(k).start()
-    down = lax.broadcasted_iota(jnp.int32, (width, width), 0)
+    down = lax.broadcasted_iota(jnp.int32, (width, width), 0).astype(jnp.int16)
     for copy in small:
         copy.wait()
+    places = parts[...].astype(jnp.int16)
+    weights = (-hops[...]).astype(BF16)
     vectors = None
     for k in range(slabs):
         gather = jnp.where(
-            down == parts[k : k + 1, :], -hops[k : k + 1, :], 0.0
-        ).astype(BF16)
+            down == places[k : k + 1, :], weights[k : k + 1, :], jnp.zeros((), BF16)
+        )
         fetch(k).wait()
         if k + AHEAD < slabs:
             fetch(k + AHEAD).start()
@@ -297,10 +300,11 @@
 
     for k in range(slabs):
         fetch(k).start()
-    down = lax.broadcasted_iota(jnp.int32, (width, width), 0)
+    down = lax.broadcasted_iota(jnp.int32, (width, width), 0).astype(jnp.int16)
+    places = part_ref[...].astype(jnp.int16)
     value = inflow_ref[...].astype(F32)
     for k in range(slabs):
-        bonds = jnp.where(down == part_ref[k : k + 1, :], 1.0, 0.0).astype(BF16)
+        bonds = jnp.where(down == places[k : k + 1, :], jnp.ones((), BF16), jnp.zeros((), BF16))
         high, low = halves(value)
         pulled = mm(jnp.concatenate([high, low], axis=0), bonds)
         reduced = cur_ref[k] - hop_ref[k : k + 1, :] * (pulled[:rows] + pulled[rows:])
@@ -322,7 +326,7 @@
             pltpu.VMEM((slabs, width, width), BF16),
             pltpu.SemaphoreType.DMA((slabs,)),
         ],
-        compiler_params=pltpu.CompilerParams(vmem_limit_bytes=SMALL_LIMIT),
+        compiler_params=pltpu.CompilerParams(vmem_limit_bytes=LOWER_LIMIT),
         cost_estimate=pl.CostEstimate(
             flops=2 * slabs * rows * width**2, bytes_accessed=2 * slabs * width**2, transcendentals=0
         ),

time: 88.2 us -> 84.7 us (0.960)
  local copies, waits for them, and re-layouts: 3.58 us -> 0.2 us
  waiting for transfers between devices: 23.2 us -> 25.7 us
  starting transfers between devices: 26.6 us -> 24.2 us
    unnamed x21 -> x19, local copies, waits for them, and re-layouts: 3.57 us -> 0.2 us
    ppermute x3, waiting for transfers between devices: 5.49 us -> 8.12 us  [back(): return lax.ppermute(value, 'slab', [(r, r - 2), (r + 1, r - 1)])]
    ppermute x3, starting transfers between devices: 9.28 us -> 6.76 us  [per_device(): lax.ppermute(products, 'slab', [(i, i ^ step) for i in range(devices)])]
    pallas_call x1, Pallas kernels: 10.1 us -> 9.18 us  [forward_range(): pl.pallas_call(forward_kernel, out_shape=(jax.ShapeDtypeStruct((width + r...]
  transfers between devices with their start and end apart: 13 -> 13, of which waited for: 7 -> 7; matrix products, arithmetic and copies ran while one was open for 0% -> 0% of each run, Pallas kernels for 19% -> 21%
where the time goes in v4:
time: 84.7 us; the launch traced here: 83.9 us
  Pallas kernels  32.3 us (38%)
  waiting for transfers between devices  25.7 us (30%)
  starting transfers between devices  24.2 us (29%)
  between operations  1.49 us (2%)
    ppermute x3, waiting for transfers between devices, per_device(): lax.ppermute(products, 'slab', [(i, i ^ step) for i in range(devices)])  11.5 us
    pallas_call x1, Pallas kernels, backward_range(): pl.pallas_call(backward_kernel, out_shape=(jax.ShapeDtypeStruct((width +...  10.5 us
    pallas_call x1, Pallas kernels, forward_range(): pl.pallas_call(forward_kernel, out_shape=(jax.ShapeDtypeStruct((width + r...  9.18 us
    ppermute x3, waiting for transfers between devices, back(): return lax.ppermute(value, 'slab', [(r, r - 2), (r + 1, r - 1)])  8.12 us
    ppermute x3, starting transfers between devices, per_device(): lax.ppermute(products, 'slab', [(i, i ^ step) for i in range(devices)])  6.76 us
    ppermute x1, starting transfers between devices, per_device(): above = lax.ppermute(locked, 'cuts', odd_pairs)  6.01 us
    ppermute x3, starting transfers between devices, up(): return lax.ppermute(value, 'slab', [(r, r + 2), (r + 1, r + 3)])  4.81 us
    ppermute x1, waiting for transfers between devices, per_device(): above = lax.ppermute(locked, 'cuts', odd_pairs)  4.03 us
  transfers between devices with their start and end apart: 13, of which 7 were waited for; matrix products, arithmetic and copies ran while one was open for 0% of the time, Pallas kernels for 21%

profile of v4, /device:TPU:2, one launch (start us, length us, event | category | flops | bytes accessed | tf_op | source)
XLA Modules:
  0.0 83.9 jit_solution(12810540593335214494)
XLA Ops:
  1.3 9.2 %forward_range.1 = (bf16[528,512]{1,0:T(8,128)(2,1)}, f32[8,16,512]{2,1,0:T(8,128)}, bf16[8,512,512]{2,1,0:T(8,128)(2,1)}) custom-call(s32[1]{0:T(128)S(6)} %copy.14.shift_ref, f32[8,512]{1,0:T(8,128)} %hop_ref.7, s32[8,512]{1,0:T(8,128)} %part_ref.5, f32[8,16,512]{2,1,0:T(8,128)} %bitcast.10, bf16[2,8,512,512]{3,2,1,0:T(8,128)(2,1)} %piv_ref.5), custom_call_target="tpu_custom_call" | custom-call | flops 4294967296 | bytes 12582912 | tf_op jit(solution)/shard_map/forward_range/pallas_call | solution.py:101
  10.5 2.2 %collective-permute-start = (bf16[528,512]{1,0:T(8,128)(2,1)}, bf16[528,512]{1,0:T(8,128)(2,1)S(1)}, u32[]{:S(2)}, u32[]{:S(2)}) collective-permute-start(bf16[528,512]{1,0:T(8,128)(2,1)} %get-tuple-element.25.own_ref), channel_id=1, source_target_pairs={{0,1},{1,0},{2,3},{3,2},{4,5},{5,4},{6,7},{7,6},{8,9},{9,8},{10,11... | collective-permute-start | bytes 1622024 | tf_op jit(solution)/shard_map/ppermute | solution.py:644
  12.7 10.5 %backward_range.1 = (bf16[528,512]{1,0:T(8,128)(2,1)}, bf16[8,512,512]{2,1,0:T(8,128)(2,1)}) custom-call(s32[1]{0:T(128)S(6)} %copy.14.shift_ref, f32[8,512]{1,0:T(8,128)} %hop_ref.7, s32[8,512]{1,0:T(8,128)} %part_ref.5, f32[8,16,512]{2,1,0:T(8,128)} %get-tuple-element.26.own_ref, bf16[8,512,512]{2,1,0:T(8,128)(2,1)} %get-tuple-element.27.op_ref, ...), custom_call_target="tpu_custom_call" | custom-call | flops 4294967296 | bytes 12582912 | tf_op jit(solution)/shard_map/backward_range/pallas_call | solution.py:186
  23.1 1.5 %collective-permute-start.1 = (bf16[528,512]{1,0:T(8,128)(2,1)}, bf16[528,512]{1,0:T(8,128)(2,1)S(1)}, u32[]{:S(2)}, u32[]{:S(2)}) collective-permute-start(bf16[528,512]{1,0:T(8,128)(2,1)} %get-tuple-element.28.own_back_ref), channel_id=1, source_target_pairs={{0,1},{1,0},{2,3},{3,2},{4,5},{5,4},{6,7},{7,6},{8,9},{9,8},{10,11... | collective-permute-start | bytes 1622024 | tf_op jit(solution)/shard_map/ppermute | solution.py:646
  24.9 6.0 %collective-permute-start.9 = (bf16[8,64,512]{2,1,0:T(8,128)(2,1)S(1)}, bf16[8,64,512]{2,1,0:T(8,128)(2,1)S(1)}, u32[]{:S(2)}, u32[]{:S(2)}) collective-permute-start(bf16[8,64,512]{2,1,0:T(8,128)(2,1)S(1)} %bitcast.20), channel_id=1, source_target_pairs={{8,16},{24,32},{40,48},{56,64},{72,80},{88,96},{104,112},{16,8},{3... | collective-permute-start | bytes 1572872 | tf_op jit(solution)/shard_map/ppermute | solution.py:653
  31.1 3.5 %collective-permute-start.2 = (bf16[16,512]{1,0:T(8,128)(2,1)S(1)}, bf16[16,512]{1,0:T(8,128)(2,1)S(1)}, u32[]{:S(2)}, u32[]{:S(2)}) collective-permute-start(bf16[16,512]{1,0:T(8,128)(2,1)S(1)} %start.1), channel_id=1, source_target_pairs={{0,2},{1,3},{8,10},{9,11},{16,18},{17,19},{24,26},{25,27},{32,34},... | collective-permute-start | bytes 49160 | tf_op jit(solution)/shard_map/ppermute | solution.py:656
  34.6 1.4 %collective-permute-done.2.new_ref = bf16[16,512]{1,0:T(8,128)(2,1)S(1)} collective-permute-done((bf16[16,512]{1,0:T(8,128)(2,1)S(1)}, bf16[16,512]{1,0:T(8,128)(2,1)S(1)}, u32[]{:S(2)}, u32[]{:S(2)}) %collective-permute-start.2) | collective-permute-done | bytes 16416 | tf_op jit(solution)/shard_map/ppermute | solution.py:656
  36.4 0.7 collective-permute-start.3
  37.4 0.7 collective-permute-start.4
  39.2 0.7 collective-permute-start.5
  40.3 0.7 collective-permute-start.6
  41.4 1.5 %collective-permute-start.7 = (bf16[16,512]{1,0:T(8,128)(2,1)S(1)}, bf16[16,512]{1,0:T(8,128)(2,1)S(1)}, u32[]{:S(2)}, u32[]{:S(2)}) collective-permute-start(bf16[16,512]{1,0:T(8,128)(2,1)S(1)} %get-tuple-element.39), channel_id=1, source_target_pairs={{2,0},{3,1},{10,8},{11,9},{18,16},{19,17},{26,24},{27,25},{34,32},... | collective-permute-start | bytes 49160 | tf_op jit(solution)/shard_map/ppermute | solution.py:659
  43.0 4.0 %collective-permute-done.9.above_ref = bf16[8,64,512]{2,1,0:T(8,128)(2,1)S(1)} collective-permute-done((bf16[8,64,512]{2,1,0:T(8,128)(2,1)S(1)}, bf16[8,64,512]{2,1,0:T(8,128)(2,1)S(1)}, u32[]{:S(2)}, u32[]{:S(2)}) %collective-permute-start.9) | collective-permute-done | bytes 524320 | tf_op jit(solution)/shard_map/ppermute | solution.py:653
  47.0 0.7 known_products.1.known_ref
  47.7 3.9 %lower_sweep.1.low_ref = f32[8,16,512]{2,1,0:T(8,128)S(1)} custom-call(s32[1]{0:T(128)S(6)} %copy.14.shift_ref, bf16[16,512]{1,0:T(8,128)(2,1)S(1)} %get-tuple-element.40.inflow_ref, f32[8,16,512]{2,1,0:T(8,128)S(1)} %bitcast.12, f32[8,512]{1,0:T(8,128)S(1)} %copy-done.5, s32[8,512]{1,0:T(8,128)S(1)} %copy-done.6, bf16[2,8,512,512]{3,2,1,0:T(8,128)(2,1)} %piv_ref.5), custom_call_target="tpu_custom_call" | custom-call | flops 67108864 | bytes 4194304 | tf_op jit(solution)/shard_map/lower_sweep/pallas_call | solution.py:319
  51.7 8.1 %collective-permute-done.7.new_ref = bf16[16,512]{1,0:T(8,128)(2,1)S(1)} collective-permute-done((bf16[16,512]{1,0:T(8,128)(2,1)S(1)}, bf16[16,512]{1,0:T(8,128)(2,1)S(1)}, u32[]{:S(2)}, u32[]{:S(2)}) %collective-permute-start.7) | collective-permute-done | bytes 16416 | tf_op jit(solution)/shard_map/ppermute | solution.py:659
  59.8 2.0 %upper_sweep.1 = (f32[8,16,512]{2,1,0:T(8,128)S(1)}, f32[192,128]{1,0:T(8,128)S(1)}) custom-call(bf16[528,512]{1,0:T(8,128)(2,1)S(1)} %copy-done, bf16[528,512]{1,0:T(8,128)(2,1)S(1)} %collective-permute-done.other_ref, f32[16,512]{1,0:T(8,128)S(1)} %get-tuple-element.33.second_back_ref, bf16[16,512]{1,0:T(8,128)(2,1)S(1)} %get-tuple-element.38.to_ref, ...), custom_call_target="tpu_custom_call" | custom-call | flops 67108864 | bytes 4194304 | tf_op jit(solution)/shard_map/upper_sweep/pallas_call | solution.py:422
  61.8 2.2 %collective-permute-start.10 = (f32[192,128]{1,0:T(8,128)S(1)}, f32[192,128]{1,0:T(8,128)S(1)}, u32[]{:S(2)}, u32[]{:S(2)}) collective-permute-start(f32[192,128]{1,0:T(8,128)S(1)} %get-tuple-element.42), channel_id=1, source_target_pairs={{0,1},{1,0},{2,3},{3,2},{4,5},{5,4},{6,7},{7,6},{8,9},{9,8},{10,11... | collective-permute-start | bytes 294920 | tf_op jit(solution)/shard_map/ppermute | solution.py:684
  64.0 3.9 %collective-permute-done.10 = f32[192,128]{1,0:T(8,128)S(1)} collective-permute-done((f32[192,128]{1,0:T(8,128)S(1)}, f32[192,128]{1,0:T(8,128)S(1)}, u32[]{:S(2)}, u32[]{:S(2)}) %collective-permute-start.10) | collective-permute-done | bytes 98336 | tf_op jit(solution)/shard_map/ppermute | solution.py:684
  67.9 3.3 %collective-permute-start.11 = (f32[192,128]{1,0:T(8,128)S(1)}, f32[192,128]{1,0:T(8,128)S(1)}, u32[]{:S(2)}, u32[]{:S(2)}) collective-permute-start(f32[192,128]{1,0:T(8,128)S(1)} %add.9), channel_id=1, source_target_pairs={{0,2},{1,3},{2,0},{3,1},{4,6},{5,7},{6,4},{7,5},{8,10},{9,11},{10,... | collective-permute-start | bytes 294920 | tf_op jit(solution)/shard_map/ppermute | solution.py:684
  71.3 2.6 %collective-permute-done.11 = f32[192,128]{1,0:T(8,128)S(1)} collective-permute-done((f32[192,128]{1,0:T(8,128)S(1)}, f32[192,128]{1,0:T(8,128)S(1)}, u32[]{:S(2)}, u32[]{:S(2)}) %collective-permute-start.11) | collective-permute-done | bytes 98336 | tf_op jit(solution)/shard_map/ppermute | solution.py:684
  73.9 1.3 %collective-permute-start.12 = (f32[192,128]{1,0:T(8,128)S(1)}, f32[192,128]{1,0:T(8,128)S(1)}, u32[]{:S(2)}, u32[]{:S(2)}) collective-permute-start(f32[192,128]{1,0:T(8,128)S(1)} %add.10), channel_id=1, source_target_pairs={{0,4},{1,5},{2,6},{3,7},{4,0},{5,1},{6,2},{7,3},{8,12},{9,13},{10,... | collective-permute-start | bytes 294920 | tf_op jit(solution)/shard_map/ppermute | solution.py:684
  75.1 4.9 %collective-permute-done.12 = f32[192,128]{1,0:T(8,128)S(1)} collective-permute-done((f32[192,128]{1,0:T(8,128)S(1)}, f32[192,128]{1,0:T(8,128)S(1)}, u32[]{:S(2)}, u32[]{:S(2)}) %collective-permute-start.12) | collective-permute-done | bytes 98336 | tf_op jit(solution)/shard_map/ppermute | solution.py:684
  80.1 3.8 %finish.1 = (f32[8,16,512]{2,1,0:T(8,128)}, f32[16,16]{1,0:T(8,128)}, f32[1,16]{1,0:T(1,128)}) custom-call(f32[192,128]{1,0:T(8,128)S(1)} %add.11.products_ref, f32[16,16]{1,0:T(8,128)S(1)} %bitcast.18, f32[8,16,512]{2,1,0:T(8,128)S(1)} %get-tuple-element.43.x_ref, f32[8,16,512]{2,1,0:T(8,128)S(1)} %bitcast.14, f32[8,16,512]{2,1,0:T(8,128)S(1)} %bitcast.17, ...), custom_call_target="tpu_custom_call" | custom-call | tf_op jit(solution)/shard_map/finish/pallas_call | solution.py:611
  (37 shorter events, 3.2 us)
Async XLA Ops:
  10.5 20.5 %collective-permute-start = (bf16[528,512]{1,0:T(8,128)(2,1)}, bf16[528,512]{1,0:T(8,128)(2,1)S(1)}, u32[]{:S(2)}, u32[]{:S(2)}) collective-permute-start(bf16[528,512]{1,0:T(8,128)(2,1)} %get-tuple-element.25.own_ref), channel_id=1, source_target_pairs={{0,1},{1,0},{2,3},{3,2},{4,5},{5,4},{6,7},{7,6},{8,9},{9,8},{10,11... | collective-permute-start | bytes 1622024 | tf_op jit(solution)/shard_map/ppermute | solution.py:644
  12.7 12.0 %copy-start.8 = (bf16[1,64,8,512]{3,2,1,0:T(8,128)(2,1)S(1)}, bf16[1,64,8,512]{3,2,1,0:T(8,128)(2,1)}, u32[]{:S(2)}) copy-start(bf16[1,64,8,512]{3,2,1,0:T(8,128)(2,1)} %param.11) | copy-start | bytes 1572868
  12.7 18.3 %copy-start = (bf16[528,512]{1,0:T(8,128)(2,1)S(1)}, bf16[528,512]{1,0:T(8,128)(2,1)}, u32[]{:S(2)}) copy-start(bf16[528,512]{1,0:T(8,128)(2,1)} %get-tuple-element.25.own_ref) | copy-start | bytes 1622020
  23.1 15.5 %copy-start.4 = (bf16[528,512]{1,0:T(8,128)(2,1)S(1)}, bf16[528,512]{1,0:T(8,128)(2,1)}, u32[]{:S(2)}) copy-start(bf16[528,512]{1,0:T(8,128)(2,1)} %get-tuple-element.28.own_back_ref) | copy-start | bytes 1622020
  23.1 15.5 %collective-permute-start.1 = (bf16[528,512]{1,0:T(8,128)(2,1)}, bf16[528,512]{1,0:T(8,128)(2,1)S(1)}, u32[]{:S(2)}, u32[]{:S(2)}) collective-permute-start(bf16[528,512]{1,0:T(8,128)(2,1)} %get-tuple-element.28.own_back_ref), channel_id=1, source_target_pairs={{0,1},{1,0},{2,3},{3,2},{4,5},{5,4},{6,7},{7,6},{8,9},{9,8},{10,11... | collective-permute-start | bytes 1622024 | tf_op jit(solution)/shard_map/ppermute | solution.py:646
  24.8 22.2 %copy-start.1 = (f32[1,8,16,512]{3,2,1,0:T(8,128)S(1)}, f32[1,8,16,512]{3,2,1,0:T(8,128)}, u32[]{:S(2)}) copy-start(f32[1,8,16,512]{3,2,1,0:T(8,128)} %param.8) | copy-start | bytes 786436
  24.8 22.2 %copy-start.3 = (f32[1,8,16,512]{3,2,1,0:T(8,128)S(1)}, f32[1,8,16,512]{3,2,1,0:T(8,128)}, u32[]{:S(2)}) copy-start(f32[1,8,16,512]{3,2,1,0:T(8,128)} %param.9) | copy-start | bytes 786436
  24.8 18.1 %collective-permute-start.8 = (bf16[8,64,512]{2,1,0:T(8,128)(2,1)S(1)}, bf16[8,64,512]{2,1,0:T(8,128)(2,1)S(1)}, u32[]{:S(2)}, u32[]{:S(2)}) collective-permute-start(bf16[8,64,512]{2,1,0:T(8,128)(2,1)S(1)} %bitcast.19), channel_id=1, source_target_pairs={{0,8},{8,0},{16,24},{24,16},{32,40},{40,32},{48,56},{56,48},{64,72... | collective-permute-start | bytes 1572872 | tf_op jit(solution)/shard_map/ppermute | solution.py:652
  24.9 22.1 %collective-permute-start.9 = (bf16[8,64,512]{2,1,0:T(8,128)(2,1)S(1)}, bf16[8,64,512]{2,1,0:T(8,128)(2,1)S(1)}, u32[]{:S(2)}, u32[]{:S(2)}) collective-permute-start(bf16[8,64,512]{2,1,0:T(8,128)(2,1)S(1)} %bitcast.20), channel_id=1, source_target_pairs={{8,16},{24,32},{40,48},{56,64},{72,80},{88,96},{104,112},{16,8},{3... | collective-permute-start | bytes 1572872 | tf_op jit(solution)/shard_map/ppermute | solution.py:653
  31.1 4.9 %collective-permute-start.2 = (bf16[16,512]{1,0:T(8,128)(2,1)S(1)}, bf16[16,512]{1,0:T(8,128)(2,1)S(1)}, u32[]{:S(2)}, u32[]{:S(2)}) collective-permute-start(bf16[16,512]{1,0:T(8,128)(2,1)S(1)} %start.1), channel_id=1, source_target_pairs={{0,2},{1,3},{8,10},{9,11},{16,18},{17,19},{24,26},{25,27},{32,34},... | collective-permute-start | bytes 49160 | tf_op jit(solution)/shard_map/ppermute | solution.py:656
  36.0 11.7 %copy-start.5 = (f32[8,512]{1,0:T(8,128)S(1)}, f32[8,512]{1,0:T(8,128)}, u32[]{:S(2)}) copy-start(f32[8,512]{1,0:T(8,128)} %hop_ref.7) | copy-start | bytes 49156
  36.0 11.7 %copy-start.6 = (s32[8,512]{1,0:T(8,128)S(1)}, s32[8,512]{1,0:T(8,128)}, u32[]{:S(2)}) copy-start(s32[8,512]{1,0:T(8,128)} %part_ref.5) | copy-start | bytes 49156
  36.4 0.7 collective-permute-start.3
  37.4 1.3 %collective-permute-start.4 = (bf16[16,512]{1,0:T(8,128)(2,1)S(1)}, bf16[16,512]{1,0:T(8,128)(2,1)S(1)}, u32[]{:S(2)}, u32[]{:S(2)}) collective-permute-start(bf16[16,512]{1,0:T(8,128)(2,1)S(1)} %get-tuple-element.32), channel_id=1, source_target_pairs={{4,6},{5,7},{12,14},{13,15},{20,22},{21,23},{28,30},{29,31},{36,38... | collective-permute-start | bytes 49160 | tf_op jit(solution)/shard_map/ppermute | solution.py:656
  39.2 0.7 collective-permute-start.5
  40.3 0.7 collective-permute-start.6
  41.4 18.3 %collective-permute-start.7 = (bf16[16,512]{1,0:T(8,128)(2,1)S(1)}, bf16[16,512]{1,0:T(8,128)(2,1)S(1)}, u32[]{:S(2)}, u32[]{:S(2)}) collective-permute-start(bf16[16,512]{1,0:T(8,128)(2,1)S(1)} %get-tuple-element.39), channel_id=1, source_target_pairs={{2,0},{3,1},{10,8},{11,9},{18,16},{19,17},{26,24},{27,25},{34,32},... | collective-permute-start | bytes 49160 | tf_op jit(solution)/shard_map/ppermute | solution.py:659
  47.7 12.0 %copy-start.2 = (bf16[8,512,512]{2,1,0:T(8,128)(2,1)S(1)}, bf16[8,512,512]{2,1,0:T(8,128)(2,1)}, u32[]{:S(2)}) copy-start(bf16[8,512,512]{2,1,0:T(8,128)(2,1)} %get-tuple-element.41.q_ref) | copy-start | bytes 12582916
  51.6 28.4 %copy-start.7 = (f32[1,16,16]{2,1,0:T(8,128)S(1)}, f32[1,16,16]{2,1,0:T(8,128)}, u32[]{:S(2)}) copy-start(f32[1,16,16]{2,1,0:T(8,128)} %param.10) | copy-start | bytes 3076
  61.8 6.1 %collective-permute-start.10 = (f32[192,128]{1,0:T(8,128)S(1)}, f32[192,128]{1,0:T(8,128)S(1)}, u32[]{:S(2)}, u32[]{:S(2)}) collective-permute-start(f32[192,128]{1,0:T(8,128)S(1)} %get-tuple-element.42), channel_id=1, source_target_pairs={{0,1},{1,0},{2,3},{3,2},{4,5},{5,4},{6,7},{7,6},{8,9},{9,8},{10,11... | collective-permute-start | bytes 294920 | tf_op jit(solution)/shard_map/ppermute | solution.py:684
  67.9 5.9 %collective-permute-start.11 = (f32[192,128]{1,0:T(8,128)S(1)}, f32[192,128]{1,0:T(8,128)S(1)}, u32[]{:S(2)}, u32[]{:S(2)}) collective-permute-start(f32[192,128]{1,0:T(8,128)S(1)} %add.9), channel_id=1, source_target_pairs={{0,2},{1,3},{2,0},{3,1},{4,6},{5,7},{6,4},{7,5},{8,10},{9,11},{10,... | collective-permute-start | bytes 294920 | tf_op jit(solution)/shard_map/ppermute | solution.py:684
  73.9 6.2 %collective-permute-start.12 = (f32[192,128]{1,0:T(8,128)S(1)}, f32[192,128]{1,0:T(8,128)S(1)}, u32[]{:S(2)}, u32[]{:S(2)}) collective-permute-start(f32[192,128]{1,0:T(8,128)S(1)} %add.10), channel_id=1, source_target_pairs={{0,4},{1,5},{2,6},{3,7},{4,0},{5,1},{6,2},{7,3},{8,12},{9,13},{10,... | collective-permute-start | bytes 294920 | tf_op jit(solution)/shard_map/ppermute | solution.py:684

commit v5 on v4

--- a/solution.py
+++ b/solution.py
@@ -649,7 +649,6 @@
     even_pairs = [(i, i ^ 1) for i in range(slices)]
     odd_pairs = [(i, i + 1) for i in range(1, slices - 1, 2)]
     odd_pairs = odd_pairs + [(j, i) for i, j in odd_pairs]
-    below = lax.ppermute(locked, "cuts", even_pairs)
     above = lax.ppermute(locked, "cuts", odd_pairs)
 
     def up(value, r):
@@ -663,6 +662,9 @@
     new = up(sent, 0)
     for r in range(2, devices - 2, 2):
         into, sent = small_call(pass_kernel, (BF16, BF16), "pass_on", fg, fg_other, into, new)
+        if r == 4:
+            near, sent = lax.optimization_barrier((locked, sent))
+            below = lax.ppermute(near, "cuts", even_pairs)
         new = up(sent, r)
     inflow, first_back, second_back, sent = small_call(
         turn_kernel, (BF16, F32, F32, BF16), "turn", fg, fg_other, sh, sh_other, into, new
@@ -671,6 +673,7 @@
     known = known_products(current, previous, below, above)
     to = jnp.zeros((rows, width), BF16)
     new = back(sent, devices - 2)
+    low, new = lax.optimization_barrier((low, new))
     for r in range(devices - 4, 0, -2):
         to, sent = small_call(
             back_kernel, (BF16, BF16), "pass_back", fg, fg_other, first_back, second_back, to, new

time: 84.7 us -> 80.4 us (0.949)
  the two profiles are of different devices: /device:TPU:2 before, /device:TPU:96 now
where the time goes in v5:
time: 80.4 us; the launch traced here: 80.2 us
  Pallas kernels  32.2 us (40%)
  waiting for transfers between devices  31.1 us (39%)
  starting transfers between devices  15 us (19%)
  between operations  1.53 us (2%)
    ppermute x3, waiting for transfers between devices, per_device(): lax.ppermute(products, 'slab', [(i, i ^ step) for i in range(devices)])  15.5 us
    pallas_call x1, Pallas kernels, backward_range(): pl.pallas_call(backward_kernel, out_shape=(jax.ShapeDtypeStruct((width +...  10.4 us
    pallas_call x1, Pallas kernels, forward_range(): pl.pallas_call(forward_kernel, out_shape=(jax.ShapeDtypeStruct((width + r...  9.18 us
    ppermute x3, waiting for transfers between devices, back(): return lax.ppermute(value, 'slab', [(r, r - 2), (r + 1, r - 1)])  7.41 us
    ppermute x1, waiting for transfers between devices, per_device(): sh_other = lax.ppermute(sh, 'slab', swap)  5.14 us
    ppermute x3, starting transfers between devices, up(): return lax.ppermute(value, 'slab', [(r, r + 2), (r + 1, r + 3)])  4.8 us
    pallas_call x1, Pallas kernels, lower_sweep(): pl.pallas_call(lower_kernel, out_shape=jax.ShapeDtypeStruct((slabs, rows,...  3.9 us
    pallas_call x1, Pallas kernels, finish(): pl.pallas_call(functools.partial(finish_kernel, scale), out_shape=(jax.Sh...  3.79 us
  transfers between devices with their start and end apart: 13, of which 7 were waited for; matrix products, arithmetic and copies ran while one was open for 0% of the time, Pallas kernels for 22%

profile of v5, /device:TPU:96, one launch (start us, length us, event | category | flops | bytes accessed | tf_op | source)
XLA Modules:
  0.0 80.2 jit_solution(6555311070277542743)
XLA Ops:
  1.3 9.2 %forward_range.1 = (bf16[528,512]{1,0:T(8,128)(2,1)}, f32[8,16,512]{2,1,0:T(8,128)}, bf16[8,512,512]{2,1,0:T(8,128)(2,1)}) custom-call(s32[1]{0:T(128)S(6)} %copy.14.shift_ref, f32[8,512]{1,0:T(8,128)} %hop_ref.7, s32[8,512]{1,0:T(8,128)} %part_ref.5, f32[8,16,512]{2,1,0:T(8,128)} %bitcast.10, bf16[2,8,512,512]{3,2,1,0:T(8,128)(2,1)} %piv_ref.5), custom_call_target="tpu_custom_call" | custom-call | flops 4294967296 | bytes 12582912 | tf_op jit(solution)/shard_map/forward_range/pallas_call | solution.py:101
  10.5 3.1 %collective-permute-start = (bf16[528,512]{1,0:T(8,128)(2,1)}, bf16[528,512]{1,0:T(8,128)(2,1)S(1)}, u32[]{:S(2)}, u32[]{:S(2)}) collective-permute-start(bf16[528,512]{1,0:T(8,128)(2,1)} %get-tuple-element.29.own_ref), channel_id=1, source_target_pairs={{0,1},{1,0},{2,3},{3,2},{4,5},{5,4},{6,7},{7,6},{8,9},{9,8},{10,11... | collective-permute-start | bytes 1622024 | tf_op jit(solution)/shard_map/ppermute | solution.py:644
  13.6 10.4 %backward_range.1 = (bf16[528,512]{1,0:T(8,128)(2,1)}, bf16[8,512,512]{2,1,0:T(8,128)(2,1)}) custom-call(s32[1]{0:T(128)S(6)} %copy.14.shift_ref, f32[8,512]{1,0:T(8,128)} %hop_ref.7, s32[8,512]{1,0:T(8,128)} %part_ref.5, f32[8,16,512]{2,1,0:T(8,128)} %get-tuple-element.30.own_ref, bf16[8,512,512]{2,1,0:T(8,128)(2,1)} %get-tuple-element.31.op_ref, ...), custom_call_target="tpu_custom_call" | custom-call | flops 4294967296 | bytes 12582912 | tf_op jit(solution)/shard_map/backward_range/pallas_call | solution.py:186
  24.1 0.6 collective-permute-start.1
  24.7 1.6 %collective-permute-done.other_ref = bf16[528,512]{1,0:T(8,128)(2,1)S(1)} collective-permute-done((bf16[528,512]{1,0:T(8,128)(2,1)}, bf16[528,512]{1,0:T(8,128)(2,1)S(1)}, u32[]{:S(2)}, u32[]{:S(2)}) %collective-permute-start) | collective-permute-done | bytes 540704 | tf_op jit(solution)/shard_map/ppermute | solution.py:644
  26.5 3.5 %collective-permute-start.2 = (bf16[16,512]{1,0:T(8,128)(2,1)S(1)}, bf16[16,512]{1,0:T(8,128)(2,1)S(1)}, u32[]{:S(2)}, u32[]{:S(2)}) collective-permute-start(bf16[16,512]{1,0:T(8,128)(2,1)S(1)} %start.1), channel_id=1, source_target_pairs={{0,2},{1,3},{8,10},{9,11},{16,18},{17,19},{24,26},{25,27},{32,34},... | collective-permute-start | bytes 49160 | tf_op jit(solution)/shard_map/ppermute | solution.py:655
  29.9 1.4 %collective-permute-done.2.new_ref = bf16[16,512]{1,0:T(8,128)(2,1)S(1)} collective-permute-done((bf16[16,512]{1,0:T(8,128)(2,1)S(1)}, bf16[16,512]{1,0:T(8,128)(2,1)S(1)}, u32[]{:S(2)}, u32[]{:S(2)}) %collective-permute-start.2) | collective-permute-done | bytes 16416 | tf_op jit(solution)/shard_map/ppermute | solution.py:655
  31.7 0.7 collective-permute-start.3
  32.6 1.9 %collective-permute-start.9 = (bf16[8,64,512]{2,1,0:T(8,128)(2,1)S(1)}, bf16[8,64,512]{2,1,0:T(8,128)(2,1)S(1)}, u32[]{:S(2)}, u32[]{:S(2)}) collective-permute-start(bf16[8,64,512]{2,1,0:T(8,128)(2,1)S(1)} %bitcast.19), channel_id=1, source_target_pairs={{8,16},{24,32},{40,48},{56,64},{72,80},{88,96},{104,112},{16,8},{3... | collective-permute-start | bytes 1572872 | tf_op jit(solution)/shard_map/ppermute | solution.py:652
  35.1 0.7 collective-permute-start.4
  35.7 5.1 %collective-permute-done.1.other_back_ref = bf16[528,512]{1,0:T(8,128)(2,1)S(1)} collective-permute-done((bf16[528,512]{1,0:T(8,128)(2,1)}, bf16[528,512]{1,0:T(8,128)(2,1)S(1)}, u32[]{:S(2)}, u32[]{:S(2)}) %collective-permute-start.1) | collective-permute-done | bytes 540704 | tf_op jit(solution)/shard_map/ppermute | solution.py:646
  40.9 0.5 turn.1
  41.4 0.9 %collective-permute-start.5 = (bf16[16,512]{1,0:T(8,128)(2,1)S(1)}, bf16[16,512]{1,0:T(8,128)(2,1)S(1)}, u32[]{:S(2)}, u32[]{:S(2)}) collective-permute-start(bf16[16,512]{1,0:T(8,128)(2,1)S(1)} %get-tuple-element.41), channel_id=1, source_target_pairs={{6,4},{7,5},{14,12},{15,13},{22,20},{23,21},{30,28},{31,29},{38,36... | collective-permute-start | bytes 49160 | tf_op jit(solution)/shard_map/ppermute | solution.py:658
  42.3 3.9 %lower_sweep.1.low_ref = f32[8,16,512]{2,1,0:T(8,128)S(1)} custom-call(s32[1]{0:T(128)S(6)} %copy.14.shift_ref, bf16[16,512]{1,0:T(8,128)(2,1)S(1)} %get-tuple-element.40.inflow_ref, f32[8,16,512]{2,1,0:T(8,128)S(1)} %bitcast.11, f32[8,512]{1,0:T(8,128)S(1)} %copy-done.5, s32[8,512]{1,0:T(8,128)S(1)} %copy-done.6, bf16[2,8,512,512]{3,2,1,0:T(8,128)(2,1)} %piv_ref.5), custom_call_target="tpu_custom_call" | custom-call | flops 67108864 | bytes 4194304 | tf_op jit(solution)/shard_map/lower_sweep/pallas_call | solution.py:319
  46.6 0.7 collective-permute-start.6
  47.8 1.3 %collective-permute-start.7 = (bf16[16,512]{1,0:T(8,128)(2,1)S(1)}, bf16[16,512]{1,0:T(8,128)(2,1)S(1)}, u32[]{:S(2)}, u32[]{:S(2)}) collective-permute-start(bf16[16,512]{1,0:T(8,128)(2,1)S(1)} %get-tuple-element.46), channel_id=1, source_target_pairs={{2,0},{3,1},{10,8},{11,9},{18,16},{19,17},{26,24},{27,25},{34,32},... | collective-permute-start | bytes 49160 | tf_op jit(solution)/shard_map/ppermute | solution.py:658
  49.1 0.7 known_products.1.known_ref
  49.9 7.4 %collective-permute-done.7.new_ref = bf16[16,512]{1,0:T(8,128)(2,1)S(1)} collective-permute-done((bf16[16,512]{1,0:T(8,128)(2,1)S(1)}, bf16[16,512]{1,0:T(8,128)(2,1)S(1)}, u32[]{:S(2)}, u32[]{:S(2)}) %collective-permute-start.7) | collective-permute-done | bytes 16416 | tf_op jit(solution)/shard_map/ppermute | solution.py:658
  57.3 2.0 %upper_sweep.1 = (f32[8,16,512]{2,1,0:T(8,128)S(1)}, f32[192,128]{1,0:T(8,128)S(1)}) custom-call(bf16[528,512]{1,0:T(8,128)(2,1)S(1)} %copy-done, bf16[528,512]{1,0:T(8,128)(2,1)S(1)} %collective-permute-done.other_ref, f32[16,512]{1,0:T(8,128)S(1)} %get-tuple-element.38.second_back_ref, bf16[16,512]{1,0:T(8,128)(2,1)S(1)} %get-tuple-element.45.to_ref, ...), custom_call_target="tpu_custom_call" | custom-call | flops 67108864 | bytes 4194304 | tf_op jit(solution)/shard_map/upper_sweep/pallas_call | solution.py:422
  59.3 1.4 %collective-permute-start.10 = (f32[192,128]{1,0:T(8,128)S(1)}, f32[192,128]{1,0:T(8,128)S(1)}, u32[]{:S(2)}, u32[]{:S(2)}) collective-permute-start(f32[192,128]{1,0:T(8,128)S(1)} %get-tuple-element.50), channel_id=1, source_target_pairs={{0,1},{1,0},{2,3},{3,2},{4,5},{5,4},{6,7},{7,6},{8,9},{9,8},{10,11... | collective-permute-start | bytes 294920 | tf_op jit(solution)/shard_map/ppermute | solution.py:687
  60.6 4.8 %collective-permute-done.10 = f32[192,128]{1,0:T(8,128)S(1)} collective-permute-done((f32[192,128]{1,0:T(8,128)S(1)}, f32[192,128]{1,0:T(8,128)S(1)}, u32[]{:S(2)}, u32[]{:S(2)}) %collective-permute-start.10) | collective-permute-done | bytes 98336 | tf_op jit(solution)/shard_map/ppermute | solution.py:687
  65.5 4.6 %collective-permute-done.11 = f32[192,128]{1,0:T(8,128)S(1)} collective-permute-done((f32[192,128]{1,0:T(8,128)S(1)}, f32[192,128]{1,0:T(8,128)S(1)}, u32[]{:S(2)}, u32[]{:S(2)}) %collective-permute-start.11) | collective-permute-done | bytes 98336 | tf_op jit(solution)/shard_map/ppermute | solution.py:687
  70.2 6.1 %collective-permute-done.12 = f32[192,128]{1,0:T(8,128)S(1)} collective-permute-done((f32[192,128]{1,0:T(8,128)S(1)}, f32[192,128]{1,0:T(8,128)S(1)}, u32[]{:S(2)}, u32[]{:S(2)}) %collective-permute-start.12) | collective-permute-done | bytes 98336 | tf_op jit(solution)/shard_map/ppermute | solution.py:687
  76.4 3.8 %finish.1 = (f32[8,16,512]{2,1,0:T(8,128)}, f32[16,16]{1,0:T(8,128)}, f32[1,16]{1,0:T(1,128)}) custom-call(f32[192,128]{1,0:T(8,128)S(1)} %add.11.products_ref, f32[16,16]{1,0:T(8,128)S(1)} %bitcast.18, f32[8,16,512]{2,1,0:T(8,128)S(1)} %get-tuple-element.51.x_ref, f32[8,16,512]{2,1,0:T(8,128)S(1)} %bitcast.14, f32[8,16,512]{2,1,0:T(8,128)S(1)} %bitcast.17, ...), custom_call_target="tpu_custom_call" | custom-call | tf_op jit(solution)/shard_map/finish/pallas_call | solution.py:611
  (37 shorter events, 2.3 us)
Async XLA Ops:
  10.5 15.8 %collective-permute-start = (bf16[528,512]{1,0:T(8,128)(2,1)}, bf16[528,512]{1,0:T(8,128)(2,1)S(1)}, u32[]{:S(2)}, u32[]{:S(2)}) collective-permute-start(bf16[528,512]{1,0:T(8,128)(2,1)} %get-tuple-element.29.own_ref), channel_id=1, source_target_pairs={{0,1},{1,0},{2,3},{3,2},{4,5},{5,4},{6,7},{7,6},{8,9},{9,8},{10,11... | collective-permute-start | bytes 1622024 | tf_op jit(solution)/shard_map/ppermute | solution.py:644
  13.6 12.7 %copy-start = (bf16[528,512]{1,0:T(8,128)(2,1)S(1)}, bf16[528,512]{1,0:T(8,128)(2,1)}, u32[]{:S(2)}) copy-start(bf16[528,512]{1,0:T(8,128)(2,1)} %get-tuple-element.29.own_ref) | copy-start | bytes 1622020
  13.6 18.8 %copy-start.8 = (bf16[1,64,8,512]{3,2,1,0:T(8,128)(2,1)S(1)}, bf16[1,64,8,512]{3,2,1,0:T(8,128)(2,1)}, u32[]{:S(2)}) copy-start(bf16[1,64,8,512]{3,2,1,0:T(8,128)(2,1)} %param.11) | copy-start | bytes 1572868
  24.0 16.8 %copy-start.4 = (bf16[528,512]{1,0:T(8,128)(2,1)S(1)}, bf16[528,512]{1,0:T(8,128)(2,1)}, u32[]{:S(2)}) copy-start(bf16[528,512]{1,0:T(8,128)(2,1)} %get-tuple-element.32.own_back_ref) | copy-start | bytes 1622020
  24.0 18.2 %copy-start.1 = (f32[1,8,16,512]{3,2,1,0:T(8,128)S(1)}, f32[1,8,16,512]{3,2,1,0:T(8,128)}, u32[]{:S(2)}) copy-start(f32[1,8,16,512]{3,2,1,0:T(8,128)} %param.8) | copy-start | bytes 786436
  24.0 18.2 %copy-start.5 = (f32[8,512]{1,0:T(8,128)S(1)}, f32[8,512]{1,0:T(8,128)}, u32[]{:S(2)}) copy-start(f32[8,512]{1,0:T(8,128)} %hop_ref.7) | copy-start | bytes 49156
  24.1 18.2 %copy-start.6 = (s32[8,512]{1,0:T(8,128)S(1)}, s32[8,512]{1,0:T(8,128)}, u32[]{:S(2)}) copy-start(s32[8,512]{1,0:T(8,128)} %part_ref.5) | copy-start | bytes 49156
  24.1 16.8 %collective-permute-start.1 = (bf16[528,512]{1,0:T(8,128)(2,1)}, bf16[528,512]{1,0:T(8,128)(2,1)S(1)}, u32[]{:S(2)}, u32[]{:S(2)}) collective-permute-start(bf16[528,512]{1,0:T(8,128)(2,1)} %get-tuple-element.32.own_back_ref), channel_id=1, source_target_pairs={{0,1},{1,0},{2,3},{3,2},{4,5},{5,4},{6,7},{7,6},{8,9},{9,8},{10,11... | collective-permute-start | bytes 1622024 | tf_op jit(solution)/shard_map/ppermute | solution.py:646
  26.5 4.9 %collective-permute-start.2 = (bf16[16,512]{1,0:T(8,128)(2,1)S(1)}, bf16[16,512]{1,0:T(8,128)(2,1)S(1)}, u32[]{:S(2)}, u32[]{:S(2)}) collective-permute-start(bf16[16,512]{1,0:T(8,128)(2,1)S(1)} %start.1), channel_id=1, source_target_pairs={{0,2},{1,3},{8,10},{9,11},{16,18},{17,19},{24,26},{25,27},{32,34},... | collective-permute-start | bytes 49160 | tf_op jit(solution)/shard_map/ppermute | solution.py:655
  31.7 2.8 %collective-permute-start.3 = (bf16[16,512]{1,0:T(8,128)(2,1)S(1)}, bf16[16,512]{1,0:T(8,128)(2,1)S(1)}, u32[]{:S(2)}, u32[]{:S(2)}) collective-permute-start(bf16[16,512]{1,0:T(8,128)(2,1)S(1)} %get-tuple-element.34), channel_id=1, source_target_pairs={{2,4},{3,5},{10,12},{11,13},{18,20},{19,21},{26,28},{27,29},{34,36... | collective-permute-start | bytes 49160 | tf_op jit(solution)/shard_map/ppermute | solution.py:655
  32.6 16.5 %collective-permute-start.9 = (bf16[8,64,512]{2,1,0:T(8,128)(2,1)S(1)}, bf16[8,64,512]{2,1,0:T(8,128)(2,1)S(1)}, u32[]{:S(2)}, u32[]{:S(2)}) collective-permute-start(bf16[8,64,512]{2,1,0:T(8,128)(2,1)S(1)} %bitcast.19), channel_id=1, source_target_pairs={{8,16},{24,32},{40,48},{56,64},{72,80},{88,96},{104,112},{16,8},{3... | collective-permute-start | bytes 1572872 | tf_op jit(solution)/shard_map/ppermute | solution.py:652
  34.8 14.3 %collective-permute-start.8 = (bf16[8,64,512]{2,1,0:T(8,128)(2,1)S(1)}, bf16[8,64,512]{2,1,0:T(8,128)(2,1)S(1)}, u32[]{:S(2)}, u32[]{:S(2)}) collective-permute-start(bf16[8,64,512]{2,1,0:T(8,128)(2,1)S(1)} %bitcast.20), channel_id=1, source_target_pairs={{0,8},{8,0},{16,24},{24,16},{32,40},{40,32},{48,56},{56,48},{64,72... | collective-permute-start | bytes 1572872 | tf_op jit(solution)/shard_map/ppermute | solution.py:667
  35.1 5.8 %collective-permute-start.4 = (bf16[16,512]{1,0:T(8,128)(2,1)S(1)}, bf16[16,512]{1,0:T(8,128)(2,1)S(1)}, u32[]{:S(2)}, u32[]{:S(2)}) collective-permute-start(bf16[16,512]{1,0:T(8,128)(2,1)S(1)} %get-tuple-element.37), channel_id=1, source_target_pairs={{4,6},{5,7},{12,14},{13,15},{20,22},{21,23},{28,30},{29,31},{36,38... | collective-permute-start | bytes 49160 | tf_op jit(solution)/shard_map/ppermute | solution.py:655
  41.4 4.8 %collective-permute-start.5 = (bf16[16,512]{1,0:T(8,128)(2,1)S(1)}, bf16[16,512]{1,0:T(8,128)(2,1)S(1)}, u32[]{:S(2)}, u32[]{:S(2)}) collective-permute-start(bf16[16,512]{1,0:T(8,128)(2,1)S(1)} %get-tuple-element.41), channel_id=1, source_target_pairs={{6,4},{7,5},{14,12},{15,13},{22,20},{23,21},{30,28},{31,29},{38,36... | collective-permute-start | bytes 49160 | tf_op jit(solution)/shard_map/ppermute | solution.py:658
  42.3 6.8 %copy-start.3 = (f32[1,8,16,512]{3,2,1,0:T(8,128)S(1)}, f32[1,8,16,512]{3,2,1,0:T(8,128)}, u32[]{:S(2)}) copy-start(f32[1,8,16,512]{3,2,1,0:T(8,128)} %param.9) | copy-start | bytes 786436
  42.3 15.0 %copy-start.2 = (bf16[8,512,512]{2,1,0:T(8,128)(2,1)S(1)}, bf16[8,512,512]{2,1,0:T(8,128)(2,1)}, u32[]{:S(2)}) copy-start(bf16[8,512,512]{2,1,0:T(8,128)(2,1)} %get-tuple-element.49.q_ref) | copy-start | bytes 12582916
  46.6 0.7 collective-permute-start.6
  47.8 9.5 %collective-permute-start.7 = (bf16[16,512]{1,0:T(8,128)(2,1)S(1)}, bf16[16,512]{1,0:T(8,128)(2,1)S(1)}, u32[]{:S(2)}, u32[]{:S(2)}) collective-permute-start(bf16[16,512]{1,0:T(8,128)(2,1)S(1)} %get-tuple-element.46), channel_id=1, source_target_pairs={{2,0},{3,1},{10,8},{11,9},{18,16},{19,17},{26,24},{27,25},{34,32},... | collective-permute-start | bytes 49160 | tf_op jit(solution)/shard_map/ppermute | solution.py:658
  49.9 26.5 %copy-start.7 = (f32[1,16,16]{2,1,0:T(8,128)S(1)}, f32[1,16,16]{2,1,0:T(8,128)}, u32[]{:S(2)}) copy-start(f32[1,16,16]{2,1,0:T(8,128)} %param.10) | copy-start | bytes 3076
  59.3 6.1 %collective-permute-start.10 = (f32[192,128]{1,0:T(8,128)S(1)}, f32[192,128]{1,0:T(8,128)S(1)}, u32[]{:S(2)}, u32[]{:S(2)}) collective-permute-start(f32[192,128]{1,0:T(8,128)S(1)} %get-tuple-element.50), channel_id=1, source_target_pairs={{0,1},{1,0},{2,3},{3,2},{4,5},{5,4},{6,7},{7,6},{8,9},{9,8},{10,11... | collective-permute-start | bytes 294920 | tf_op jit(solution)/shard_map/ppermute | solution.py:687
  65.4 4.7 %collective-permute-start.11 = (f32[192,128]{1,0:T(8,128)S(1)}, f32[192,128]{1,0:T(8,128)S(1)}, u32[]{:S(2)}, u32[]{:S(2)}) collective-permute-start(f32[192,128]{1,0:T(8,128)S(1)} %add.9), channel_id=1, source_target_pairs={{0,2},{1,3},{2,0},{3,1},{4,6},{5,7},{6,4},{7,5},{8,10},{9,11},{10,... | collective-permute-start | bytes 294920 | tf_op jit(solution)/shard_map/ppermute | solution.py:687
  70.1 6.2 %collective-permute-start.12 = (f32[192,128]{1,0:T(8,128)S(1)}, f32[192,128]{1,0:T(8,128)S(1)}, u32[]{:S(2)}, u32[]{:S(2)}) collective-permute-start(f32[192,128]{1,0:T(8,128)S(1)} %add.10), channel_id=1, source_target_pairs={{0,4},{1,5},{2,6},{3,7},{4,0},{5,1},{6,2},{7,3},{8,12},{9,13},{10,... | collective-permute-start | bytes 294920 | tf_op jit(solution)/shard_map/ppermute | solution.py:687

commit v6 on v5

--- a/solution.py
+++ b/solution.py
@@ -68,24 +68,28 @@
         copy.wait()
     places = parts[...].astype(jnp.int16)
     weights = (-hops[...]).astype(BF16)
-    vectors = None
-    for k in range(slabs):
+    def mixed(k):
         gather = jnp.where(
             down == places[k : k + 1, :], weights[k : k + 1, :], jnp.zeros((), BF16)
         )
         fetch(k).wait()
         if k + AHEAD < slabs:
             fetch(k + AHEAD).start()
-        mixed = mm(jnp.concatenate([gather, sources[k].astype(BF16)], axis=0), pbuf[k])
-        step = mixed[:width].astype(BF16)
-        source = mixed[width:]
-        if k == 0:
-            opbuf[k] = step
-            vectors = source
-        else:
-            moved = mm(jnp.concatenate([opbuf[k - 1], vectors.astype(BF16)], axis=0), step)
-            opbuf[k] = moved[:width].astype(BF16)
-            vectors = source + moved[width:]
+        product = mm(jnp.concatenate([gather, sources[k].astype(BF16)], axis=0), pbuf[k])
+        return product[:width].astype(BF16), product[width:]
+
+    step, vectors = mixed(0)
+    opbuf[0] = step
+    give_op(0).start()
+    own_ref[0] = vectors
+    following = mixed(1)
+    for k in range(1, slabs):
+        step, source = following
+        if k + 1 < slabs:
+            following = mixed(k + 1)
+        moved = mm(jnp.concatenate([opbuf[k - 1], vectors.astype(BF16)], axis=0), step)
+        opbuf[k] = moved[:width].astype(BF16)
+        vectors = source + moved[width:]
         give_op(k).start()
         own_ref[k] = vectors
     fg_ref[:width, :] = opbuf[slabs - 1]
@@ -163,11 +167,18 @@
     fetch_op(last).wait()
     response = opbuf[last].astype(F32)
     vectors = own_ref[last]
-    for k in range(slabs - 2, -1, -1):
+    def turned(k):
         fetch(k).wait()
         permuted = mm(scatter(k + 1), pbuf[k]).astype(BF16)
         qbuf[k] = permuted
         give_q(k, qbuf).start()
+        return permuted
+
+    following = turned(last - 1)
+    for k in range(slabs - 2, -1, -1):
+        permuted = following
+        if k > 0:
+            following = turned(k - 1)
         moved = mm(scaled(k + 1), permuted)
         fetch_op(k).wait()
         response = opbuf[k].astype(F32) - moved[:width]
@@ -351,11 +362,22 @@
     second = total[near + two :]
     among = first[:, near : near + two] + first[:, near + two :]
     among = among + second[:, near : near + two] + second[:, near + two :]
-    out_ref[:near, :] = total[:near, :near]
-    out_ref[near : near + two, :] = first[:, :near] + second[:, :near]
-    out_ref[near + two : near + two + rows, :] = jnp.zeros((rows, near), F32)
-    out_ref[near + two + rows :, :] = jnp.concatenate(
+    half = near // 2
+    down = lax.broadcasted_iota(jnp.int32, (half, half), 0)
+    across = lax.broadcasted_iota(jnp.int32, (half, half), 1)
+    low_block = total[:half, :half]
+    high_block = total[half:near, half:near]
+    edge = jnp.sum(jnp.where(down == across, high_block, 0.0), axis=0, keepdims=True)
+    out_ref[:half, :] = jnp.concatenate(
+        [jnp.where(across >= down, low_block, high_block), total[:half, half:near]], axis=1
+    )
+    out_ref[half : half + two, :] = first[:, :near] + second[:, :near]
+    out_ref[half + two : half + two + rows, :] = jnp.zeros((rows, near), F32)
+    out_ref[half + two + rows : half + two + 2 * rows, :] = jnp.concatenate(
         [jnp.zeros((rows, near - 2 * two), F32), among[:rows], among[rows:]], axis=1
+    )
+    out_ref[half + two + 2 * rows :, :] = jnp.broadcast_to(
+        jnp.concatenate([edge, jnp.zeros((1, near - half), F32)], axis=1), (8, near)
     )
 
 
@@ -364,7 +386,7 @@
     near = 2 * below.shape[1]
     return pl.pallas_call(
         known_kernel,
-        out_shape=jax.ShapeDtypeStruct((near + 4 * rows, near), F32),
+        out_shape=jax.ShapeDtypeStruct((near // 2 + 4 * rows + 8, near), F32),
         compiler_params=pltpu.CompilerParams(vmem_limit_bytes=SMALL_LIMIT),
         cost_estimate=pl.CostEstimate(
             flops=2 * slabs * 192 * 192 * width, bytes_accessed=3 * 2**19, transcendentals=0
@@ -406,12 +428,14 @@
     joined = total[:rows] + total[rows:]
     three = 3 * rows
     own = joined[:, near : near + three] + joined[:, near + three :]
-    top = near + 2 * rows
+    top = near // 2 + 2 * rows
+    last = top + 2 * rows
     out_ref[:top, :] = known_ref[:top, :]
     out_ref[top : top + rows, :] = joined[:, :near]
-    out_ref[top + rows :, :] = known_ref[top + rows :, :] + jnp.concatenate(
+    out_ref[top + rows : last, :] = known_ref[top + rows : last, :] + jnp.concatenate(
         [own, jnp.zeros((rows, near - three), F32)], axis=1
     )
+    out_ref[last:, :] = known_ref[last:, :]
 
 
 def upper_sweep(
@@ -558,10 +582,25 @@
     near = products_ref.shape[1]
     two = 2 * rows
     products = products_ref[...] * scale
-    near_near = products[:near]
-    known_near = products[near : near + two]
-    x_near = products[near + two : near + two + rows]
-    tail = products[near + two + rows :]
+    half = near // 2
+    down = lax.broadcasted_iota(jnp.int32, (half, half), 0)
+    across = lax.broadcasted_iota(jnp.int32, (half, half), 1)
+    folded = products[:half, :half]
+    turned = jnp.transpose(folded)
+    between = products[:half, half:]
+    edge = products[half + two + 2 * rows : half + two + 2 * rows + 1, :half]
+    low_block = jnp.where(across >= down, folded, turned)
+    high_block = jnp.where(across == down, edge, jnp.where(across < down, folded, turned))
+    near_near = jnp.concatenate(
+        [
+            jnp.concatenate([low_block, between], axis=1),
+            jnp.concatenate([jnp.transpose(between), high_block], axis=1),
+        ],
+        axis=0,
+    )
+    known_near = products[half : half + two]
+    x_near = products[half + two : half + two + rows]
+    tail = products[half + two + rows : half + two + 2 * rows]
     x_x = tail[:, :rows]
     x_known = tail[:, rows : 3 * rows]
     among = jnp.concatenate([tail[:, near - 2 * two : near - two], tail[:, near - two :]], axis=0)

time: 80.4 us -> 78.7 us (0.979)
  waiting for transfers between devices: 31.1 us -> 29.5 us
    ppermute x3, waiting for transfers between devices: 15.5 us -> 13.7 us  [per_device(): lax.ppermute(products, 'slab', [(i, i ^ step) for i in range(devices)])]
    ppermute x1, waiting for transfers between devices: 5.14 us -> 3.99 us  [per_device(): sh_other = lax.ppermute(sh, 'slab', swap)]
    ppermute x3, starting transfers between devices: 1.53 us -> 2.39 us  [per_device(): lax.ppermute(products, 'slab', [(i, i ^ step) for i in range(devices)])]
  transfers between devices with their start and end apart: 13 -> 13, of which waited for: 7 -> 7; matrix products, arithmetic and copies ran while one was open for 0% -> 0% of each run, Pallas kernels for 22% -> 21%
where the time goes in v6:
time: 78.7 us; the launch traced here: 78.4 us
  Pallas kernels  31.4 us (40%)
  waiting for transfers between devices  29.5 us (37%)
  starting transfers between devices  15.7 us (20%)
  between operations  1.54 us (2%)
    ppermute x3, waiting for transfers between devices, per_device(): lax.ppermute(products, 'slab', [(i, i ^ step) for i in range(devices)])  13.7 us
    pallas_call x1, Pallas kernels, backward_range(): pl.pallas_call(backward_kernel, out_shape=(jax.ShapeDtypeStruct((width +...  10 us
    pallas_call x1, Pallas kernels, forward_range(): pl.pallas_call(forward_kernel, out_shape=(jax.ShapeDtypeStruct((width + r...  8.71 us
    ppermute x3, waiting for transfers between devices, back(): return lax.ppermute(value, 'slab', [(r, r - 2), (r + 1, r - 1)])  8.06 us
    ppermute x3, starting transfers between devices, up(): return lax.ppermute(value, 'slab', [(r, r + 2), (r + 1, r + 3)])  4.81 us
    ppermute x1, waiting for transfers between devices, per_device(): sh_other = lax.ppermute(sh, 'slab', swap)  3.99 us
    pallas_call x1, Pallas kernels, lower_sweep(): pl.pallas_call(lower_kernel, out_shape=jax.ShapeDtypeStruct((slabs, rows,...  3.9 us
    pallas_call x1, Pallas kernels, finish(): pl.pallas_call(functools.partial(finish_kernel, scale), out_shape=(jax.Sh...  3.84 us
  transfers between devices with their start and end apart: 13, of which 7 were waited for; matrix products, arithmetic and copies ran while one was open for 0% of the time, Pallas kernels for 21%

profile of v6, /device:TPU:96, one launch (start us, length us, event | category | flops | bytes accessed | tf_op | source)
XLA Modules:
  0.0 78.4 jit_solution(81886746698401521)
XLA Ops:
  1.3 8.7 %forward_range.1 = (bf16[528,512]{1,0:T(8,128)(2,1)}, f32[8,16,512]{2,1,0:T(8,128)}, bf16[8,512,512]{2,1,0:T(8,128)(2,1)}) custom-call(s32[1]{0:T(128)S(6)} %copy.14.shift_ref, f32[8,512]{1,0:T(8,128)} %hop_ref.7, s32[8,512]{1,0:T(8,128)} %part_ref.5, f32[8,16,512]{2,1,0:T(8,128)} %bitcast.10, bf16[2,8,512,512]{3,2,1,0:T(8,128)(2,1)} %piv_ref.5), custom_call_target="tpu_custom_call" | custom-call | flops 4294967296 | bytes 12582912 | tf_op jit(solution)/shard_map/forward_range/pallas_call | solution.py:105
  10.0 3.1 %collective-permute-start = (bf16[528,512]{1,0:T(8,128)(2,1)}, bf16[528,512]{1,0:T(8,128)(2,1)S(1)}, u32[]{:S(2)}, u32[]{:S(2)}) collective-permute-start(bf16[528,512]{1,0:T(8,128)(2,1)} %get-tuple-element.29.own_ref), channel_id=1, source_target_pairs={{0,1},{1,0},{2,3},{3,2},{4,5},{5,4},{6,7},{7,6},{8,9},{9,8},{10,11... | collective-permute-start | bytes 1622024 | tf_op jit(solution)/shard_map/ppermute | solution.py:683
  13.1 10.0 %backward_range.1 = (bf16[528,512]{1,0:T(8,128)(2,1)}, bf16[8,512,512]{2,1,0:T(8,128)(2,1)}) custom-call(s32[1]{0:T(128)S(6)} %copy.14.shift_ref, f32[8,512]{1,0:T(8,128)} %hop_ref.7, s32[8,512]{1,0:T(8,128)} %part_ref.5, f32[8,16,512]{2,1,0:T(8,128)} %get-tuple-element.30.own_ref, bf16[8,512,512]{2,1,0:T(8,128)(2,1)} %get-tuple-element.31.op_ref, ...), custom_call_target="tpu_custom_call" | custom-call | flops 4294967296 | bytes 12582912 | tf_op jit(solution)/shard_map/backward_range/pallas_call | solution.py:197
  23.2 0.6 collective-permute-start.1
  23.8 2.3 %collective-permute-done.other_ref = bf16[528,512]{1,0:T(8,128)(2,1)S(1)} collective-permute-done((bf16[528,512]{1,0:T(8,128)(2,1)}, bf16[528,512]{1,0:T(8,128)(2,1)S(1)}, u32[]{:S(2)}, u32[]{:S(2)}) %collective-permute-start) | collective-permute-done | bytes 540704 | tf_op jit(solution)/shard_map/ppermute | solution.py:683
  26.3 3.5 %collective-permute-start.2 = (bf16[16,512]{1,0:T(8,128)(2,1)S(1)}, bf16[16,512]{1,0:T(8,128)(2,1)S(1)}, u32[]{:S(2)}, u32[]{:S(2)}) collective-permute-start(bf16[16,512]{1,0:T(8,128)(2,1)S(1)} %start.1), channel_id=1, source_target_pairs={{0,2},{1,3},{8,10},{9,11},{16,18},{17,19},{24,26},{25,27},{32,34},... | collective-permute-start | bytes 49160 | tf_op jit(solution)/shard_map/ppermute | solution.py:694
  29.8 1.4 %collective-permute-done.2.new_ref = bf16[16,512]{1,0:T(8,128)(2,1)S(1)} collective-permute-done((bf16[16,512]{1,0:T(8,128)(2,1)S(1)}, bf16[16,512]{1,0:T(8,128)(2,1)S(1)}, u32[]{:S(2)}, u32[]{:S(2)}) %collective-permute-start.2) | collective-permute-done | bytes 16416 | tf_op jit(solution)/shard_map/ppermute | solution.py:694
  31.5 0.7 collective-permute-start.3
  32.4 1.9 %collective-permute-start.9 = (bf16[8,64,512]{2,1,0:T(8,128)(2,1)S(1)}, bf16[8,64,512]{2,1,0:T(8,128)(2,1)S(1)}, u32[]{:S(2)}, u32[]{:S(2)}) collective-permute-start(bf16[8,64,512]{2,1,0:T(8,128)(2,1)S(1)} %bitcast.19), channel_id=1, source_target_pairs={{8,16},{24,32},{40,48},{56,64},{72,80},{88,96},{104,112},{16,8},{3... | collective-permute-start | bytes 1572872 | tf_op jit(solution)/shard_map/ppermute | solution.py:691
  34.6 0.7 collective-permute-start.4
  35.3 4.0 %collective-permute-done.1.other_back_ref = bf16[528,512]{1,0:T(8,128)(2,1)S(1)} collective-permute-done((bf16[528,512]{1,0:T(8,128)(2,1)}, bf16[528,512]{1,0:T(8,128)(2,1)S(1)}, u32[]{:S(2)}, u32[]{:S(2)}) %collective-permute-start.1) | collective-permute-done | bytes 540704 | tf_op jit(solution)/shard_map/ppermute | solution.py:685
  39.3 0.5 turn.1
  39.9 0.9 %collective-permute-start.5 = (bf16[16,512]{1,0:T(8,128)(2,1)S(1)}, bf16[16,512]{1,0:T(8,128)(2,1)S(1)}, u32[]{:S(2)}, u32[]{:S(2)}) collective-permute-start(bf16[16,512]{1,0:T(8,128)(2,1)S(1)} %get-tuple-element.41), channel_id=1, source_target_pairs={{6,4},{7,5},{14,12},{15,13},{22,20},{23,21},{30,28},{31,29},{38,36... | collective-permute-start | bytes 49160 | tf_op jit(solution)/shard_map/ppermute | solution.py:697
  40.8 3.9 %lower_sweep.1.low_ref = f32[8,16,512]{2,1,0:T(8,128)S(1)} custom-call(s32[1]{0:T(128)S(6)} %copy.14.shift_ref, bf16[16,512]{1,0:T(8,128)(2,1)S(1)} %get-tuple-element.40.inflow_ref, f32[8,16,512]{2,1,0:T(8,128)S(1)} %bitcast.11, f32[8,512]{1,0:T(8,128)S(1)} %copy-done.5, s32[8,512]{1,0:T(8,128)S(1)} %copy-done.6, bf16[2,8,512,512]{3,2,1,0:T(8,128)(2,1)} %piv_ref.5), custom_call_target="tpu_custom_call" | custom-call | flops 67108864 | bytes 4194304 | tf_op jit(solution)/shard_map/lower_sweep/pallas_call | solution.py:330
  45.1 0.7 collective-permute-start.6
  46.2 1.3 %collective-permute-start.7 = (bf16[16,512]{1,0:T(8,128)(2,1)S(1)}, bf16[16,512]{1,0:T(8,128)(2,1)S(1)}, u32[]{:S(2)}, u32[]{:S(2)}) collective-permute-start(bf16[16,512]{1,0:T(8,128)(2,1)S(1)} %get-tuple-element.46), channel_id=1, source_target_pairs={{2,0},{3,1},{10,8},{11,9},{18,16},{19,17},{26,24},{27,25},{34,32},... | collective-permute-start | bytes 49160 | tf_op jit(solution)/shard_map/ppermute | solution.py:697
  47.6 0.7 known_products.1.known_ref
  48.3 8.1 %collective-permute-done.7.new_ref = bf16[16,512]{1,0:T(8,128)(2,1)S(1)} collective-permute-done((bf16[16,512]{1,0:T(8,128)(2,1)S(1)}, bf16[16,512]{1,0:T(8,128)(2,1)S(1)}, u32[]{:S(2)}, u32[]{:S(2)}) %collective-permute-start.7) | collective-permute-done | bytes 16416 | tf_op jit(solution)/shard_map/ppermute | solution.py:697
  56.4 2.0 %upper_sweep.1 = (f32[8,16,512]{2,1,0:T(8,128)S(1)}, f32[136,128]{1,0:T(8,128)S(1)}) custom-call(bf16[528,512]{1,0:T(8,128)(2,1)S(1)} %copy-done, bf16[528,512]{1,0:T(8,128)(2,1)S(1)} %collective-permute-done.other_ref, f32[16,512]{1,0:T(8,128)S(1)} %get-tuple-element.38.second_back_ref, bf16[16,512]{1,0:T(8,128)(2,1)S(1)} %get-tuple-element.45.to_ref, ...), custom_call_target="tpu_custom_call" | custom-call | flops 67108864 | bytes 4194304 | tf_op jit(solution)/shard_map/upper_sweep/pallas_call | solution.py:446
  58.4 2.2 %collective-permute-start.10 = (f32[136,128]{1,0:T(8,128)S(1)}, f32[136,128]{1,0:T(8,128)S(1)}, u32[]{:S(2)}, u32[]{:S(2)}) collective-permute-start(f32[136,128]{1,0:T(8,128)S(1)} %get-tuple-element.50), channel_id=1, source_target_pairs={{0,1},{1,0},{2,3},{3,2},{4,5},{5,4},{6,7},{7,6},{8,9},{9,8},{10,11... | collective-permute-start | bytes 208904 | tf_op jit(solution)/shard_map/ppermute | solution.py:726
  60.6 3.6 %collective-permute-done.10 = f32[136,128]{1,0:T(8,128)S(1)} collective-permute-done((f32[136,128]{1,0:T(8,128)S(1)}, f32[136,128]{1,0:T(8,128)S(1)}, u32[]{:S(2)}, u32[]{:S(2)}) %collective-permute-start.10) | collective-permute-done | bytes 69664 | tf_op jit(solution)/shard_map/ppermute | solution.py:726
  64.3 4.3 %collective-permute-done.11 = f32[136,128]{1,0:T(8,128)S(1)} collective-permute-done((f32[136,128]{1,0:T(8,128)S(1)}, f32[136,128]{1,0:T(8,128)S(1)}, u32[]{:S(2)}, u32[]{:S(2)}) %collective-permute-start.11) | collective-permute-done | bytes 69664 | tf_op jit(solution)/shard_map/ppermute | solution.py:726
  68.7 5.8 %collective-permute-done.12 = f32[136,128]{1,0:T(8,128)S(1)} collective-permute-done((f32[136,128]{1,0:T(8,128)S(1)}, f32[136,128]{1,0:T(8,128)S(1)}, u32[]{:S(2)}, u32[]{:S(2)}) %collective-permute-start.12) | collective-permute-done | bytes 69664 | tf_op jit(solution)/shard_map/ppermute | solution.py:726
  74.5 3.8 %finish.1 = (f32[8,16,512]{2,1,0:T(8,128)}, f32[16,16]{1,0:T(8,128)}, f32[1,16]{1,0:T(1,128)}) custom-call(f32[136,128]{1,0:T(8,128)S(1)} %add.11.products_ref, f32[16,16]{1,0:T(8,128)S(1)} %bitcast.18, f32[8,16,512]{2,1,0:T(8,128)S(1)} %get-tuple-element.51.x_ref, f32[8,16,512]{2,1,0:T(8,128)S(1)} %bitcast.14, f32[8,16,512]{2,1,0:T(8,128)S(1)} %bitcast.17, ...), custom_call_target="tpu_custom_call" | custom-call | tf_op jit(solution)/shard_map/finish/pallas_call | solution.py:650
  (37 shorter events, 2.1 us)
Async XLA Ops:
  10.0 16.1 %collective-permute-start = (bf16[528,512]{1,0:T(8,128)(2,1)}, bf16[528,512]{1,0:T(8,128)(2,1)S(1)}, u32[]{:S(2)}, u32[]{:S(2)}) collective-permute-start(bf16[528,512]{1,0:T(8,128)(2,1)} %get-tuple-element.29.own_ref), channel_id=1, source_target_pairs={{0,1},{1,0},{2,3},{3,2},{4,5},{5,4},{6,7},{7,6},{8,9},{9,8},{10,11... | collective-permute-start | bytes 1622024 | tf_op jit(solution)/shard_map/ppermute | solution.py:683
  13.1 13.0 %copy-start = (bf16[528,512]{1,0:T(8,128)(2,1)S(1)}, bf16[528,512]{1,0:T(8,128)(2,1)}, u32[]{:S(2)}) copy-start(bf16[528,512]{1,0:T(8,128)(2,1)} %get-tuple-element.29.own_ref) | copy-start | bytes 1622020
  13.1 19.1 %copy-start.8 = (bf16[1,64,8,512]{3,2,1,0:T(8,128)(2,1)S(1)}, bf16[1,64,8,512]{3,2,1,0:T(8,128)(2,1)}, u32[]{:S(2)}) copy-start(bf16[1,64,8,512]{3,2,1,0:T(8,128)(2,1)} %param.11) | copy-start | bytes 1572868
  23.1 16.2 %copy-start.4 = (bf16[528,512]{1,0:T(8,128)(2,1)S(1)}, bf16[528,512]{1,0:T(8,128)(2,1)}, u32[]{:S(2)}) copy-start(bf16[528,512]{1,0:T(8,128)(2,1)} %get-tuple-element.32.own_back_ref) | copy-start | bytes 1622020
  23.1 17.6 %copy-start.2 = (f32[1,8,16,512]{3,2,1,0:T(8,128)S(1)}, f32[1,8,16,512]{3,2,1,0:T(8,128)}, u32[]{:S(2)}) copy-start(f32[1,8,16,512]{3,2,1,0:T(8,128)} %param.8) | copy-start | bytes 786436
  23.1 17.6 %copy-start.5 = (f32[8,512]{1,0:T(8,128)S(1)}, f32[8,512]{1,0:T(8,128)}, u32[]{:S(2)}) copy-start(f32[8,512]{1,0:T(8,128)} %hop_ref.7) | copy-start | bytes 49156
  23.2 17.6 %copy-start.6 = (s32[8,512]{1,0:T(8,128)S(1)}, s32[8,512]{1,0:T(8,128)}, u32[]{:S(2)}) copy-start(s32[8,512]{1,0:T(8,128)} %part_ref.5) | copy-start | bytes 49156
  23.2 16.1 %collective-permute-start.1 = (bf16[528,512]{1,0:T(8,128)(2,1)}, bf16[528,512]{1,0:T(8,128)(2,1)S(1)}, u32[]{:S(2)}, u32[]{:S(2)}) collective-permute-start(bf16[528,512]{1,0:T(8,128)(2,1)} %get-tuple-element.32.own_back_ref), channel_id=1, source_target_pairs={{0,1},{1,0},{2,3},{3,2},{4,5},{5,4},{6,7},{7,6},{8,9},{9,8},{10,11... | collective-permute-start | bytes 1622024 | tf_op jit(solution)/shard_map/ppermute | solution.py:685
  26.3 4.9 %collective-permute-start.2 = (bf16[16,512]{1,0:T(8,128)(2,1)S(1)}, bf16[16,512]{1,0:T(8,128)(2,1)S(1)}, u32[]{:S(2)}, u32[]{:S(2)}) collective-permute-start(bf16[16,512]{1,0:T(8,128)(2,1)S(1)} %start.1), channel_id=1, source_target_pairs={{0,2},{1,3},{8,10},{9,11},{16,18},{17,19},{24,26},{25,27},{32,34},... | collective-permute-start | bytes 49160 | tf_op jit(solution)/shard_map/ppermute | solution.py:694
  31.5 2.8 %collective-permute-start.3 = (bf16[16,512]{1,0:T(8,128)(2,1)S(1)}, bf16[16,512]{1,0:T(8,128)(2,1)S(1)}, u32[]{:S(2)}, u32[]{:S(2)}) collective-permute-start(bf16[16,512]{1,0:T(8,128)(2,1)S(1)} %get-tuple-element.34), channel_id=1, source_target_pairs={{2,4},{3,5},{10,12},{11,13},{18,20},{19,21},{26,28},{27,29},{34,36... | collective-permute-start | bytes 49160 | tf_op jit(solution)/shard_map/ppermute | solution.py:694
  32.4 15.2 %collective-permute-start.9 = (bf16[8,64,512]{2,1,0:T(8,128)(2,1)S(1)}, bf16[8,64,512]{2,1,0:T(8,128)(2,1)S(1)}, u32[]{:S(2)}, u32[]{:S(2)}) collective-permute-start(bf16[8,64,512]{2,1,0:T(8,128)(2,1)S(1)} %bitcast.19), channel_id=1, source_target_pairs={{8,16},{24,32},{40,48},{56,64},{72,80},{88,96},{104,112},{16,8},{3... | collective-permute-start | bytes 1572872 | tf_op jit(solution)/shard_map/ppermute | solution.py:691
  34.6 12.9 %collective-permute-start.8 = (bf16[8,64,512]{2,1,0:T(8,128)(2,1)S(1)}, bf16[8,64,512]{2,1,0:T(8,128)(2,1)S(1)}, u32[]{:S(2)}, u32[]{:S(2)}) collective-permute-start(bf16[8,64,512]{2,1,0:T(8,128)(2,1)S(1)} %bitcast.20), channel_id=1, source_target_pairs={{0,8},{8,0},{16,24},{24,16},{32,40},{40,32},{48,56},{56,48},{64,72... | collective-permute-start | bytes 1572872 | tf_op jit(solution)/shard_map/ppermute | solution.py:706
  34.6 4.7 %collective-permute-start.4 = (bf16[16,512]{1,0:T(8,128)(2,1)S(1)}, bf16[16,512]{1,0:T(8,128)(2,1)S(1)}, u32[]{:S(2)}, u32[]{:S(2)}) collective-permute-start(bf16[16,512]{1,0:T(8,128)(2,1)S(1)} %get-tuple-element.37), channel_id=1, source_target_pairs={{4,6},{5,7},{12,14},{13,15},{20,22},{21,23},{28,30},{29,31},{36,38... | collective-permute-start | bytes 49160 | tf_op jit(solution)/shard_map/ppermute | solution.py:694
  39.9 4.8 %collective-permute-start.5 = (bf16[16,512]{1,0:T(8,128)(2,1)S(1)}, bf16[16,512]{1,0:T(8,128)(2,1)S(1)}, u32[]{:S(2)}, u32[]{:S(2)}) collective-permute-start(bf16[16,512]{1,0:T(8,128)(2,1)S(1)} %get-tuple-element.41), channel_id=1, source_target_pairs={{6,4},{7,5},{14,12},{15,13},{22,20},{23,21},{30,28},{31,29},{38,36... | collective-permute-start | bytes 49160 | tf_op jit(solution)/shard_map/ppermute | solution.py:697
  40.7 6.8 %copy-start.3 = (f32[1,8,16,512]{3,2,1,0:T(8,128)S(1)}, f32[1,8,16,512]{3,2,1,0:T(8,128)}, u32[]{:S(2)}) copy-start(f32[1,8,16,512]{3,2,1,0:T(8,128)} %param.9) | copy-start | bytes 786436
  40.8 15.6 %copy-start.1 = (bf16[8,512,512]{2,1,0:T(8,128)(2,1)S(1)}, bf16[8,512,512]{2,1,0:T(8,128)(2,1)}, u32[]{:S(2)}) copy-start(bf16[8,512,512]{2,1,0:T(8,128)(2,1)} %get-tuple-element.49.q_ref) | copy-start | bytes 12582916
  45.1 0.7 collective-permute-start.6
  46.2 10.1 %collective-permute-start.7 = (bf16[16,512]{1,0:T(8,128)(2,1)S(1)}, bf16[16,512]{1,0:T(8,128)(2,1)S(1)}, u32[]{:S(2)}, u32[]{:S(2)}) collective-permute-start(bf16[16,512]{1,0:T(8,128)(2,1)S(1)} %get-tuple-element.46), channel_id=1, source_target_pairs={{2,0},{3,1},{10,8},{11,9},{18,16},{19,17},{26,24},{27,25},{34,32},... | collective-permute-start | bytes 49160 | tf_op jit(solution)/shard_map/ppermute | solution.py:697
  48.3 26.2 %copy-start.7 = (f32[1,16,16]{2,1,0:T(8,128)S(1)}, f32[1,16,16]{2,1,0:T(8,128)}, u32[]{:S(2)}) copy-start(f32[1,16,16]{2,1,0:T(8,128)} %param.10) | copy-start | bytes 3076
  58.4 5.8 %collective-permute-start.10 = (f32[136,128]{1,0:T(8,128)S(1)}, f32[136,128]{1,0:T(8,128)S(1)}, u32[]{:S(2)}, u32[]{:S(2)}) collective-permute-start(f32[136,128]{1,0:T(8,128)S(1)} %get-tuple-element.50), channel_id=1, source_target_pairs={{0,1},{1,0},{2,3},{3,2},{4,5},{5,4},{6,7},{7,6},{8,9},{9,8},{10,11... | collective-permute-start | bytes 208904 | tf_op jit(solution)/shard_map/ppermute | solution.py:726
  64.2 4.4 %collective-permute-start.11 = (f32[136,128]{1,0:T(8,128)S(1)}, f32[136,128]{1,0:T(8,128)S(1)}, u32[]{:S(2)}, u32[]{:S(2)}) collective-permute-start(f32[136,128]{1,0:T(8,128)S(1)} %add.9), channel_id=1, source_target_pairs={{0,2},{1,3},{2,0},{3,1},{4,6},{5,7},{6,4},{7,5},{8,10},{9,11},{10,... | collective-permute-start | bytes 208904 | tf_op jit(solution)/shard_map/ppermute | solution.py:726
  68.6 5.9 %collective-permute-start.12 = (f32[136,128]{1,0:T(8,128)S(1)}, f32[136,128]{1,0:T(8,128)S(1)}, u32[]{:S(2)}, u32[]{:S(2)}) collective-permute-start(f32[136,128]{1,0:T(8,128)S(1)} %add.10), channel_id=1, source_target_pairs={{0,4},{1,5},{2,6},{3,7},{4,0},{5,1},{6,2},{7,3},{8,12},{9,13},{10,... | collective-permute-start | bytes 208904 | tf_op jit(solution)/shard_map/ppermute | solution.py:726

commit v7 on v6

--- a/solution.py
+++ b/solution.py
@@ -576,7 +576,7 @@
 
 def finish_kernel(
     scale, products_ref, coupling_ref, x_ref, cur_ref, prev_ref, below_ref, above_ref,
-    next_ref, upper_ref, ritz_ref,
+    next_ref, upper_ref, ritz_ref, following, sem,
 ):
     slabs, rows, width = x_ref.shape
     near = products_ref.shape[1]
@@ -638,11 +638,14 @@
         )
         rest = jnp.concatenate([x_low, cur_low, prev_low], axis=0)
         main = mm(both, stack)
-        next_ref[k] = main[:rows] + main[rows:] + mm(weight_high[:, : 3 * rows], rest)
+        following[k] = main[:rows] + main[rows:] + mm(weight_high[:, : 3 * rows], rest)
+        pltpu.make_async_copy(following.at[k], next_ref.at[k], sem.at[k]).start()
         next(eigen, None)
     for _ in eigen:
         pass
     ritz_ref[...] = ritz[0]
+    for k in range(slabs):
+        pltpu.make_async_copy(following.at[k], next_ref.at[k], sem.at[k]).wait()
 
 
 def finish(scale, products, coupling, x, current, previous, below, above):
@@ -654,6 +657,16 @@
             jax.ShapeDtypeStruct((rows, rows), F32),
             jax.ShapeDtypeStruct((1, rows), F32),
         ),
+        in_specs=[pl.BlockSpec(memory_space=pltpu.VMEM)] * 7,
+        out_specs=(
+            pl.BlockSpec(memory_space=pl.ANY),
+            pl.BlockSpec(memory_space=pltpu.VMEM),
+            pl.BlockSpec(memory_space=pltpu.VMEM),
+        ),
+        scratch_shapes=[
+            pltpu.VMEM((slabs, rows, width), F32),
+            pltpu.SemaphoreType.DMA((slabs,)),
+        ],
         compiler_params=pltpu.CompilerParams(vmem_limit_bytes=SMALL_LIMIT),
         name="finish",
     )(products, coupling, x, current, previous, below, above)

time: 78.7 us -> 79.4 us (level)
  no operation moved by 1% of the time
where the time goes in v7:
time: 79.4 us; the launch traced here: 79.1 us
  Pallas kernels  32 us (40%)
  waiting for transfers between devices  29.5 us (37%)
  starting transfers between devices  15.7 us (20%)
  between operations  1.7 us (2%)
    ppermute x3, waiting for transfers between devices, per_device(): lax.ppermute(products, 'slab', [(i, i ^ step) for i in range(devices)])  13.7 us
    pallas_call x1, Pallas kernels, backward_range(): pl.pallas_call(backward_kernel, out_shape=(jax.ShapeDtypeStruct((width +...  10 us
    pallas_call x1, Pallas kernels, forward_range(): pl.pallas_call(forward_kernel, out_shape=(jax.ShapeDtypeStruct((width + r...  8.71 us
    ppermute x3, waiting for transfers between devices, back(): return lax.ppermute(value, 'slab', [(r, r - 2), (r + 1, r - 1)])  8.06 us
    ppermute x3, starting transfers between devices, up(): return lax.ppermute(value, 'slab', [(r, r + 2), (r + 1, r + 3)])  4.81 us
    pallas_call x1, Pallas kernels, finish(): pl.pallas_call(functools.partial(finish_kernel, scale), out_shape=(jax.Sh...  4.42 us
    ppermute x1, waiting for transfers between devices, per_device(): sh_other = lax.ppermute(sh, 'slab', swap)  3.99 us
    pallas_call x1, Pallas kernels, lower_sweep(): pl.pallas_call(lower_kernel, out_shape=jax.ShapeDtypeStruct((slabs, rows,...  3.9 us
  transfers between devices with their start and end apart: 13, of which 7 were waited for; matrix products, arithmetic and copies ran while one was open for 0% of the time, Pallas kernels for 21%

profile of v7, /device:TPU:96, one launch (start us, length us, event | category | flops | bytes accessed | tf_op | source)
XLA Modules:
  0.0 79.1 jit_solution(13395128836587207225)
XLA Ops:
  1.3 8.7 %forward_range.1 = (bf16[528,512]{1,0:T(8,128)(2,1)}, f32[8,16,512]{2,1,0:T(8,128)}, bf16[8,512,512]{2,1,0:T(8,128)(2,1)}) custom-call(s32[1]{0:T(128)S(6)} %copy.14.shift_ref, f32[8,512]{1,0:T(8,128)} %hop_ref.7, s32[8,512]{1,0:T(8,128)} %part_ref.5, f32[8,16,512]{2,1,0:T(8,128)} %bitcast.10, bf16[2,8,512,512]{3,2,1,0:T(8,128)(2,1)} %piv_ref.5), custom_call_target="tpu_custom_call" | custom-call | flops 4294967296 | bytes 12582912 | tf_op jit(solution)/shard_map/forward_range/pallas_call | solution.py:105
  10.0 3.1 %collective-permute-start = (bf16[528,512]{1,0:T(8,128)(2,1)}, bf16[528,512]{1,0:T(8,128)(2,1)S(1)}, u32[]{:S(2)}, u32[]{:S(2)}) collective-permute-start(bf16[528,512]{1,0:T(8,128)(2,1)} %get-tuple-element.29.own_ref), channel_id=1, source_target_pairs={{0,1},{1,0},{2,3},{3,2},{4,5},{5,4},{6,7},{7,6},{8,9},{9,8},{10,11... | collective-permute-start | bytes 1622024 | tf_op jit(solution)/shard_map/ppermute | solution.py:696
  13.1 10.0 %backward_range.1 = (bf16[528,512]{1,0:T(8,128)(2,1)}, bf16[8,512,512]{2,1,0:T(8,128)(2,1)}) custom-call(s32[1]{0:T(128)S(6)} %copy.14.shift_ref, f32[8,512]{1,0:T(8,128)} %hop_ref.7, s32[8,512]{1,0:T(8,128)} %part_ref.5, f32[8,16,512]{2,1,0:T(8,128)} %get-tuple-element.30.own_ref, bf16[8,512,512]{2,1,0:T(8,128)(2,1)} %get-tuple-element.31.op_ref, ...), custom_call_target="tpu_custom_call" | custom-call | flops 4294967296 | bytes 12582912 | tf_op jit(solution)/shard_map/backward_range/pallas_call | solution.py:197
  23.2 0.6 collective-permute-start.1
  23.8 2.3 %collective-permute-done.other_ref = bf16[528,512]{1,0:T(8,128)(2,1)S(1)} collective-permute-done((bf16[528,512]{1,0:T(8,128)(2,1)}, bf16[528,512]{1,0:T(8,128)(2,1)S(1)}, u32[]{:S(2)}, u32[]{:S(2)}) %collective-permute-start) | collective-permute-done | bytes 540704 | tf_op jit(solution)/shard_map/ppermute | solution.py:696
  26.3 3.5 %collective-permute-start.2 = (bf16[16,512]{1,0:T(8,128)(2,1)S(1)}, bf16[16,512]{1,0:T(8,128)(2,1)S(1)}, u32[]{:S(2)}, u32[]{:S(2)}) collective-permute-start(bf16[16,512]{1,0:T(8,128)(2,1)S(1)} %start.1), channel_id=1, source_target_pairs={{0,2},{1,3},{8,10},{9,11},{16,18},{17,19},{24,26},{25,27},{32,34},... | collective-permute-start | bytes 49160 | tf_op jit(solution)/shard_map/ppermute | solution.py:707
  29.8 1.4 %collective-permute-done.2.new_ref = bf16[16,512]{1,0:T(8,128)(2,1)S(1)} collective-permute-done((bf16[16,512]{1,0:T(8,128)(2,1)S(1)}, bf16[16,512]{1,0:T(8,128)(2,1)S(1)}, u32[]{:S(2)}, u32[]{:S(2)}) %collective-permute-start.2) | collective-permute-done | bytes 16416 | tf_op jit(solution)/shard_map/ppermute | solution.py:707
  31.5 0.7 collective-permute-start.3
  32.4 1.9 %collective-permute-start.9 = (bf16[8,64,512]{2,1,0:T(8,128)(2,1)S(1)}, bf16[8,64,512]{2,1,0:T(8,128)(2,1)S(1)}, u32[]{:S(2)}, u32[]{:S(2)}) collective-permute-start(bf16[8,64,512]{2,1,0:T(8,128)(2,1)S(1)} %bitcast.19), channel_id=1, source_target_pairs={{8,16},{24,32},{40,48},{56,64},{72,80},{88,96},{104,112},{16,8},{3... | collective-permute-start | bytes 1572872 | tf_op jit(solution)/shard_map/ppermute | solution.py:704
  34.6 0.7 collective-permute-start.4
  35.3 4.0 %collective-permute-done.1.other_back_ref = bf16[528,512]{1,0:T(8,128)(2,1)S(1)} collective-permute-done((bf16[528,512]{1,0:T(8,128)(2,1)}, bf16[528,512]{1,0:T(8,128)(2,1)S(1)}, u32[]{:S(2)}, u32[]{:S(2)}) %collective-permute-start.1) | collective-permute-done | bytes 540704 | tf_op jit(solution)/shard_map/ppermute | solution.py:698
  39.3 0.5 turn.1
  39.9 0.9 %collective-permute-start.5 = (bf16[16,512]{1,0:T(8,128)(2,1)S(1)}, bf16[16,512]{1,0:T(8,128)(2,1)S(1)}, u32[]{:S(2)}, u32[]{:S(2)}) collective-permute-start(bf16[16,512]{1,0:T(8,128)(2,1)S(1)} %get-tuple-element.41), channel_id=1, source_target_pairs={{6,4},{7,5},{14,12},{15,13},{22,20},{23,21},{30,28},{31,29},{38,36... | collective-permute-start | bytes 49160 | tf_op jit(solution)/shard_map/ppermute | solution.py:710
  40.8 3.9 %lower_sweep.1.low_ref = f32[8,16,512]{2,1,0:T(8,128)S(1)} custom-call(s32[1]{0:T(128)S(6)} %copy.14.shift_ref, bf16[16,512]{1,0:T(8,128)(2,1)S(1)} %get-tuple-element.40.inflow_ref, f32[8,16,512]{2,1,0:T(8,128)S(1)} %bitcast.11, f32[8,512]{1,0:T(8,128)S(1)} %copy-done.5, s32[8,512]{1,0:T(8,128)S(1)} %copy-done.6, bf16[2,8,512,512]{3,2,1,0:T(8,128)(2,1)} %piv_ref.5), custom_call_target="tpu_custom_call" | custom-call | flops 67108864 | bytes 4194304 | tf_op jit(solution)/shard_map/lower_sweep/pallas_call | solution.py:330
  45.1 0.7 collective-permute-start.6
  46.2 1.3 %collective-permute-start.7 = (bf16[16,512]{1,0:T(8,128)(2,1)S(1)}, bf16[16,512]{1,0:T(8,128)(2,1)S(1)}, u32[]{:S(2)}, u32[]{:S(2)}) collective-permute-start(bf16[16,512]{1,0:T(8,128)(2,1)S(1)} %get-tuple-element.46), channel_id=1, source_target_pairs={{2,0},{3,1},{10,8},{11,9},{18,16},{19,17},{26,24},{27,25},{34,32},... | collective-permute-start | bytes 49160 | tf_op jit(solution)/shard_map/ppermute | solution.py:710
  47.6 0.7 known_products.1.known_ref
  48.3 8.1 %collective-permute-done.7.new_ref = bf16[16,512]{1,0:T(8,128)(2,1)S(1)} collective-permute-done((bf16[16,512]{1,0:T(8,128)(2,1)S(1)}, bf16[16,512]{1,0:T(8,128)(2,1)S(1)}, u32[]{:S(2)}, u32[]{:S(2)}) %collective-permute-start.7) | collective-permute-done | bytes 16416 | tf_op jit(solution)/shard_map/ppermute | solution.py:710
  56.4 2.0 %upper_sweep.1 = (f32[8,16,512]{2,1,0:T(8,128)S(1)}, f32[136,128]{1,0:T(8,128)S(1)}) custom-call(bf16[528,512]{1,0:T(8,128)(2,1)S(1)} %copy-done, bf16[528,512]{1,0:T(8,128)(2,1)S(1)} %collective-permute-done.other_ref, f32[16,512]{1,0:T(8,128)S(1)} %get-tuple-element.38.second_back_ref, bf16[16,512]{1,0:T(8,128)(2,1)S(1)} %get-tuple-element.45.to_ref, ...), custom_call_target="tpu_custom_call" | custom-call | flops 67108864 | bytes 4194304 | tf_op jit(solution)/shard_map/upper_sweep/pallas_call | solution.py:446
  58.4 2.2 %collective-permute-start.10 = (f32[136,128]{1,0:T(8,128)S(1)}, f32[136,128]{1,0:T(8,128)S(1)}, u32[]{:S(2)}, u32[]{:S(2)}) collective-permute-start(f32[136,128]{1,0:T(8,128)S(1)} %get-tuple-element.50), channel_id=1, source_target_pairs={{0,1},{1,0},{2,3},{3,2},{4,5},{5,4},{6,7},{7,6},{8,9},{9,8},{10,11... | collective-permute-start | bytes 208904 | tf_op jit(solution)/shard_map/ppermute | solution.py:739
  60.6 3.6 %collective-permute-done.10 = f32[136,128]{1,0:T(8,128)S(1)} collective-permute-done((f32[136,128]{1,0:T(8,128)S(1)}, f32[136,128]{1,0:T(8,128)S(1)}, u32[]{:S(2)}, u32[]{:S(2)}) %collective-permute-start.10) | collective-permute-done | bytes 69664 | tf_op jit(solution)/shard_map/ppermute | solution.py:739
  64.3 4.3 %collective-permute-done.11 = f32[136,128]{1,0:T(8,128)S(1)} collective-permute-done((f32[136,128]{1,0:T(8,128)S(1)}, f32[136,128]{1,0:T(8,128)S(1)}, u32[]{:S(2)}, u32[]{:S(2)}) %collective-permute-start.11) | collective-permute-done | bytes 69664 | tf_op jit(solution)/shard_map/ppermute | solution.py:739
  68.7 5.8 %collective-permute-done.12 = f32[136,128]{1,0:T(8,128)S(1)} collective-permute-done((f32[136,128]{1,0:T(8,128)S(1)}, f32[136,128]{1,0:T(8,128)S(1)}, u32[]{:S(2)}, u32[]{:S(2)}) %collective-permute-start.12) | collective-permute-done | bytes 69664 | tf_op jit(solution)/shard_map/ppermute | solution.py:739
  74.5 4.4 %finish.1 = (f32[8,16,512]{2,1,0:T(8,128)}, f32[16,16]{1,0:T(8,128)}, f32[1,16]{1,0:T(1,128)}) custom-call(f32[136,128]{1,0:T(8,128)S(1)} %add.11.products_ref, f32[16,16]{1,0:T(8,128)S(1)} %bitcast.18, f32[8,16,512]{2,1,0:T(8,128)S(1)} %get-tuple-element.51.x_ref, f32[8,16,512]{2,1,0:T(8,128)S(1)} %bitcast.14, f32[8,16,512]{2,1,0:T(8,128)S(1)} %bitcast.17, ...), custom_call_target="tpu_custom_call" | custom-call | tf_op jit(solution)/shard_map/finish/pallas_call | solution.py:653
  (37 shorter events, 2.1 us)
Async XLA Ops:
  10.0 16.1 %collective-permute-start = (bf16[528,512]{1,0:T(8,128)(2,1)}, bf16[528,512]{1,0:T(8,128)(2,1)S(1)}, u32[]{:S(2)}, u32[]{:S(2)}) collective-permute-start(bf16[528,512]{1,0:T(8,128)(2,1)} %get-tuple-element.29.own_ref), channel_id=1, source_target_pairs={{0,1},{1,0},{2,3},{3,2},{4,5},{5,4},{6,7},{7,6},{8,9},{9,8},{10,11... | collective-permute-start | bytes 1622024 | tf_op jit(solution)/shard_map/ppermute | solution.py:696
  13.1 13.0 %copy-start = (bf16[528,512]{1,0:T(8,128)(2,1)S(1)}, bf16[528,512]{1,0:T(8,128)(2,1)}, u32[]{:S(2)}) copy-start(bf16[528,512]{1,0:T(8,128)(2,1)} %get-tuple-element.29.own_ref) | copy-start | bytes 1622020
  13.1 19.1 %copy-start.8 = (bf16[1,64,8,512]{3,2,1,0:T(8,128)(2,1)S(1)}, bf16[1,64,8,512]{3,2,1,0:T(8,128)(2,1)}, u32[]{:S(2)}) copy-start(bf16[1,64,8,512]{3,2,1,0:T(8,128)(2,1)} %param.11) | copy-start | bytes 1572868
  23.1 16.2 %copy-start.4 = (bf16[528,512]{1,0:T(8,128)(2,1)S(1)}, bf16[528,512]{1,0:T(8,128)(2,1)}, u32[]{:S(2)}) copy-start(bf16[528,512]{1,0:T(8,128)(2,1)} %get-tuple-element.32.own_back_ref) | copy-start | bytes 1622020
  23.1 17.6 %copy-start.2 = (f32[1,8,16,512]{3,2,1,0:T(8,128)S(1)}, f32[1,8,16,512]{3,2,1,0:T(8,128)}, u32[]{:S(2)}) copy-start(f32[1,8,16,512]{3,2,1,0:T(8,128)} %param.8) | copy-start | bytes 786436
  23.1 17.6 %copy-start.5 = (f32[8,512]{1,0:T(8,128)S(1)}, f32[8,512]{1,0:T(8,128)}, u32[]{:S(2)}) copy-start(f32[8,512]{1,0:T(8,128)} %hop_ref.7) | copy-start | bytes 49156
  23.2 17.6 %copy-start.6 = (s32[8,512]{1,0:T(8,128)S(1)}, s32[8,512]{1,0:T(8,128)}, u32[]{:S(2)}) copy-start(s32[8,512]{1,0:T(8,128)} %part_ref.5) | copy-start | bytes 49156
  23.2 16.1 %collective-permute-start.1 = (bf16[528,512]{1,0:T(8,128)(2,1)}, bf16[528,512]{1,0:T(8,128)(2,1)S(1)}, u32[]{:S(2)}, u32[]{:S(2)}) collective-permute-start(bf16[528,512]{1,0:T(8,128)(2,1)} %get-tuple-element.32.own_back_ref), channel_id=1, source_target_pairs={{0,1},{1,0},{2,3},{3,2},{4,5},{5,4},{6,7},{7,6},{8,9},{9,8},{10,11... | collective-permute-start | bytes 1622024 | tf_op jit(solution)/shard_map/ppermute | solution.py:698
  26.3 4.9 %collective-permute-start.2 = (bf16[16,512]{1,0:T(8,128)(2,1)S(1)}, bf16[16,512]{1,0:T(8,128)(2,1)S(1)}, u32[]{:S(2)}, u32[]{:S(2)}) collective-permute-start(bf16[16,512]{1,0:T(8,128)(2,1)S(1)} %start.1), channel_id=1, source_target_pairs={{0,2},{1,3},{8,10},{9,11},{16,18},{17,19},{24,26},{25,27},{32,34},... | collective-permute-start | bytes 49160 | tf_op jit(solution)/shard_map/ppermute | solution.py:707
  31.5 2.8 %collective-permute-start.3 = (bf16[16,512]{1,0:T(8,128)(2,1)S(1)}, bf16[16,512]{1,0:T(8,128)(2,1)S(1)}, u32[]{:S(2)}, u32[]{:S(2)}) collective-permute-start(bf16[16,512]{1,0:T(8,128)(2,1)S(1)} %get-tuple-element.34), channel_id=1, source_target_pairs={{2,4},{3,5},{10,12},{11,13},{18,20},{19,21},{26,28},{27,29},{34,36... | collective-permute-start | bytes 49160 | tf_op jit(solution)/shard_map/ppermute | solution.py:707
  32.4 15.2 %collective-permute-start.9 = (bf16[8,64,512]{2,1,0:T(8,128)(2,1)S(1)}, bf16[8,64,512]{2,1,0:T(8,128)(2,1)S(1)}, u32[]{:S(2)}, u32[]{:S(2)}) collective-permute-start(bf16[8,64,512]{2,1,0:T(8,128)(2,1)S(1)} %bitcast.19), channel_id=1, source_target_pairs={{8,16},{24,32},{40,48},{56,64},{72,80},{88,96},{104,112},{16,8},{3... | collective-permute-start | bytes 1572872 | tf_op jit(solution)/shard_map/ppermute | solution.py:704
  34.6 12.9 %collective-permute-start.8 = (bf16[8,64,512]{2,1,0:T(8,128)(2,1)S(1)}, bf16[8,64,512]{2,1,0:T(8,128)(2,1)S(1)}, u32[]{:S(2)}, u32[]{:S(2)}) collective-permute-start(bf16[8,64,512]{2,1,0:T(8,128)(2,1)S(1)} %bitcast.20), channel_id=1, source_target_pairs={{0,8},{8,0},{16,24},{24,16},{32,40},{40,32},{48,56},{56,48},{64,72... | collective-permute-start | bytes 1572872 | tf_op jit(solution)/shard_map/ppermute | solution.py:719
  34.6 4.7 %collective-permute-start.4 = (bf16[16,512]{1,0:T(8,128)(2,1)S(1)}, bf16[16,512]{1,0:T(8,128)(2,1)S(1)}, u32[]{:S(2)}, u32[]{:S(2)}) collective-permute-start(bf16[16,512]{1,0:T(8,128)(2,1)S(1)} %get-tuple-element.37), channel_id=1, source_target_pairs={{4,6},{5,7},{12,14},{13,15},{20,22},{21,23},{28,30},{29,31},{36,38... | collective-permute-start | bytes 49160 | tf_op jit(solution)/shard_map/ppermute | solution.py:707
  39.9 4.8 %collective-permute-start.5 = (bf16[16,512]{1,0:T(8,128)(2,1)S(1)}, bf16[16,512]{1,0:T(8,128)(2,1)S(1)}, u32[]{:S(2)}, u32[]{:S(2)}) collective-permute-start(bf16[16,512]{1,0:T(8,128)(2,1)S(1)} %get-tuple-element.41), channel_id=1, source_target_pairs={{6,4},{7,5},{14,12},{15,13},{22,20},{23,21},{30,28},{31,29},{38,36... | collective-permute-start | bytes 49160 | tf_op jit(solution)/shard_map/ppermute | solution.py:710
  40.7 6.8 %copy-start.3 = (f32[1,8,16,512]{3,2,1,0:T(8,128)S(1)}, f32[1,8,16,512]{3,2,1,0:T(8,128)}, u32[]{:S(2)}) copy-start(f32[1,8,16,512]{3,2,1,0:T(8,128)} %param.9) | copy-start | bytes 786436
  40.8 15.6 %copy-start.1 = (bf16[8,512,512]{2,1,0:T(8,128)(2,1)S(1)}, bf16[8,512,512]{2,1,0:T(8,128)(2,1)}, u32[]{:S(2)}) copy-start(bf16[8,512,512]{2,1,0:T(8,128)(2,1)} %get-tuple-element.49.q_ref) | copy-start | bytes 12582916
  45.1 0.7 collective-permute-start.6
  46.2 10.1 %collective-permute-start.7 = (bf16[16,512]{1,0:T(8,128)(2,1)S(1)}, bf16[16,512]{1,0:T(8,128)(2,1)S(1)}, u32[]{:S(2)}, u32[]{:S(2)}) collective-permute-start(bf16[16,512]{1,0:T(8,128)(2,1)S(1)} %get-tuple-element.46), channel_id=1, source_target_pairs={{2,0},{3,1},{10,8},{11,9},{18,16},{19,17},{26,24},{27,25},{34,32},... | collective-permute-start | bytes 49160 | tf_op jit(solution)/shard_map/ppermute | solution.py:710
  48.3 26.2 %copy-start.7 = (f32[1,16,16]{2,1,0:T(8,128)S(1)}, f32[1,16,16]{2,1,0:T(8,128)}, u32[]{:S(2)}) copy-start(f32[1,16,16]{2,1,0:T(8,128)} %param.10) | copy-start | bytes 3076
  58.4 5.8 %collective-permute-start.10 = (f32[136,128]{1,0:T(8,128)S(1)}, f32[136,128]{1,0:T(8,128)S(1)}, u32[]{:S(2)}, u32[]{:S(2)}) collective-permute-start(f32[136,128]{1,0:T(8,128)S(1)} %get-tuple-element.50), channel_id=1, source_target_pairs={{0,1},{1,0},{2,3},{3,2},{4,5},{5,4},{6,7},{7,6},{8,9},{9,8},{10,11... | collective-permute-start | bytes 208904 | tf_op jit(solution)/shard_map/ppermute | solution.py:739
  64.2 4.4 %collective-permute-start.11 = (f32[136,128]{1,0:T(8,128)S(1)}, f32[136,128]{1,0:T(8,128)S(1)}, u32[]{:S(2)}, u32[]{:S(2)}) collective-permute-start(f32[136,128]{1,0:T(8,128)S(1)} %add.9), channel_id=1, source_target_pairs={{0,2},{1,3},{2,0},{3,1},{4,6},{5,7},{6,4},{7,5},{8,10},{9,11},{10,... | collective-permute-start | bytes 208904 | tf_op jit(solution)/shard_map/ppermute | solution.py:739
  68.6 5.9 %collective-permute-start.12 = (f32[136,128]{1,0:T(8,128)S(1)}, f32[136,128]{1,0:T(8,128)S(1)}, u32[]{:S(2)}, u32[]{:S(2)}) collective-permute-start(f32[136,128]{1,0:T(8,128)S(1)} %add.10), channel_id=1, source_target_pairs={{0,4},{1,5},{2,6},{3,7},{4,0},{5,1},{6,2},{7,3},{8,12},{9,13},{10,... | collective-permute-start | bytes 208904 | tf_op jit(solution)/shard_map/ppermute | solution.py:739
